TPU v7x, 32 devices: a whole 2x2x4 slice. The times are simulated.
32 devices in a mesh: dp: 32 (over z, y, x, core).
Axes of the slice: x: 2, y: 2, z: 4, core: 2. Of those that a mesh axis runs over, the one named last changes fastest.
Arguments:
- block_in: bfloat16 [12608, 768], P('dp'), may hold values from -6 to 6
- slot_mask: int32 [12608], P('dp'), may hold values from 0 to 1, as said below
- gain_first: bfloat16 [768], P('dp'), may hold values from 0.5 to 1.5
- shift_first: bfloat16 [768], P('dp'), may hold values from -3 to 3
- packed_weight: bfloat16 [768, 2304], P('dp'), may hold values from -0.21875 to 0.21875
- query_bias: bfloat16 [768], P('dp'), may hold values from -3 to 3
- value_bias: bfloat16 [768], P('dp'), may hold values from -3 to 3
- out_weight: bfloat16 [768, 768], P('dp'), may hold values from -1.75 to 1.75
- out_bias: bfloat16 [768], P('dp'), may hold values from -3 to 3
- gain_second: bfloat16 [768], P('dp'), may hold values from 0.5 to 1.5
- shift_second: bfloat16 [768], P('dp'), may hold values from -3 to 3
- up_weight: bfloat16 [768, 3072], P('dp'), may hold values from -0.21875 to 0.21875
- up_bias: bfloat16 [3072], P('dp'), may hold values from -3 to 3
- down_weight: bfloat16 [3072, 768], P('dp'), may hold values from -0.109375 to 0.109375
- down_bias: bfloat16 [768], P('dp'), may hold values from -3 to 3
- cotangent: bfloat16 [12608, 768], P('dp'), may hold values from -6 to 6
Outputs:
- block_out: bfloat16 [12608, 768], P('dp')
- input_grad: float32 [12608, 768], P('dp')
- grad_gain_first: float32 [768], P('dp')
- grad_shift_first: float32 [768], P('dp')
- grad_packed_weight: float32 [768, 2304], P('dp')
- grad_query_bias: float32 [768], P('dp')
- grad_value_bias: float32 [768], P('dp')
- grad_out_weight: float32 [768, 768], P('dp')
- grad_out_bias: float32 [768], P('dp')
- grad_gain_second: float32 [768], P('dp')
- grad_shift_second: float32 [768], P('dp')
- grad_up_weight: float32 [768, 3072], P('dp')
- grad_up_bias: float32 [3072], P('dp')
- grad_down_weight: float32 [3072, 768], P('dp')
- grad_down_bias: float32 [768], P('dp')
Inputs may be any that keep to these rules, and one draw needn't show every extreme that they name: `slot_mask`: each image slot of 197 tokens is all ones or all zeros; on each device the live image slots come first; each device has at least 1 of its 2 image slots live, and some device has both live.
All inputs are finite; a program needn't handle non-finite values.
Results may differ from a plain program's by a relative error of at most 0.011.
Values may be sent and summed in bfloat16 or wider, within the bound.
No kernel may reach another device: no remote copies, remote signals or barrier semaphores. Data moves between devices by JAX's collectives and lax.ppermute only.
A program may use at most 192 MiB of HBM per device.

v0:
```python
import functools

import jax
import jax.numpy as jnp
from jax import lax
from jax.experimental import pallas as pl
from jax.experimental.pallas import tpu as pltpu
from jax.sharding import PartitionSpec as P

D = 768
HEADS = 12
HEAD_DIM = 64
FF = 3072
LEN = 197
SLOT = 208
SPEED = 1.15e9
LENGTHS = (32, 0.25, 8, 24, 0.5, 0.25, 3, 0.25, 0.25, 8, 2, 4, 12, 8, 2, 0.25, 0.5, 24, 16, 1, 6, 1, 16, 24, 16, 0.25, 0.5, 16, 6, 2, 32, 0.5, 3, 8, 2)
SCALE = HEAD_DIM ** (-0.5)
F32 = jnp.float32
BF16 = jnp.bfloat16
VMEM = pl.BlockSpec(memory_space=pltpu.VMEM)
SMEM = pl.BlockSpec(memory_space=pltpu.SMEM)
ANY = pl.BlockSpec(memory_space=pl.ANY)


def params(megabytes):
    return pltpu.CompilerParams(
        vmem_limit_bytes=megabytes << 20, dimension_semantics=("arbitrary",)
    )


def cost(length):
    return pl.CostEstimate(flops=int(length * SPEED), transcendentals=0, bytes_accessed=D)


def mul(a, b):
    return jnp.dot(a, b, preferred_element_type=F32)


def mul_t(a, b):
    return lax.dot_general(a, b, (((1,), (1,)), ((), ())), preferred_element_type=F32)


def t_mul(a, b):
    return lax.dot_general(a, b, (((0,), (0,)), ((), ())), preferred_element_type=F32)


class Links:
    def __init__(self, count):
        chips = count // 2
        z = min(4, chips)
        plane = chips // z
        x = 1
        while x * x < plane:
            x *= 2
        self.count, self.z, self.plane = count, z, plane
        bit = 2
        x_bits, y_bits, z_bits = [], [], []
        for bits, extent in ((x_bits, x), (y_bits, plane // x), (z_bits, z)):
            size = 1
            while size < extent:
                bits.append(bit)
                bit *= 2
                size *= 2
        self.steps = [(b, b) for b in reversed(z_bits)]
        self.steps += list(zip(x_bits + y_bits, y_bits + x_bits))
        index = lax.axis_index("dp")
        core = index % 2
        sides = [((index & jnp.where(core == 0, *step)) != 0).astype(jnp.int32) for step in self.steps]
        self.place = jnp.stack([core.astype(jnp.int32)] + sides)
        self.last = None
        self.lengths = iter(LENGTHS + (1,) * 64)

    def length(self):
        return next(self.lengths)

    def run(self, kernel, *args, **options):
        out = kernel(self.last, *args, **options)
        self.last = out[0] if isinstance(out, (tuple, list)) else out
        return out

    def slot(self, device):
        place = 0
        for weight, step in enumerate(self.steps):
            if device & step[device % 2]:
                place |= 1 << weight
        return place // self.z, place % self.z

    def swap(self, value, even, odd):
        pairs = [(i, i ^ (odd if i % 2 else even)) for i in range(self.count)]
        return lax.ppermute(value, "dp", pairs)

    def pair(self, at, *parts):
        count, rows = parts[0][0].shape[:2]
        widths = [part[0].shape[2] for part in parts]
        flat = [part[0] for part in parts] + [part[1] for part in parts]

        def body(place, *refs):
            out = refs[-1]
            high = place[1 + at]

            def copy(i, carry):
                start = 0
                for k, width in enumerate(widths):
                    cols = pl.ds(start, width)
                    out[high, i, :, cols] = refs[k][i]
                    out[1 - high, i, :, cols] = refs[len(widths) + k][i]
                    start += width
                return carry

            lax.fori_loop(0, count, copy, 0)

        def kernel(last):
            joined = pl.pallas_call(
                body,
                out_shape=jax.ShapeDtypeStruct((2, count, rows, sum(widths)), BF16),
                in_specs=[SMEM] + [VMEM] * len(flat) + ([] if last is None else [ANY]),
                out_specs=VMEM,
                compiler_params=pltpu.CompilerParams(vmem_limit_bytes=24 << 20),
                cost_estimate=cost(self.length()),
                name="pair",
            )(self.place, *flat, *([] if last is None else [last]))
            return joined

        return self.run(kernel).reshape(2 * count, rows, sum(widths))

    def advance(self, held, first, last):
        for at in range(first, last):
            held = self.pair(at, (held, self.swap(held, *self.steps[at])))
        return held

    def across(self, held):
        held = held.reshape((self.plane, self.z) + held.shape[1:])
        return held, self.swap(held, 1, 1)

    def exchange(self, kept, sent):
        other = self.swap(sent, 1, 1)
        return kept.reshape((-1,) + kept.shape[2:]), other.reshape((-1,) + kept.shape[2:])

    def halve(self, at, kept, other):
        half = kept.shape[0] // 2
        chunk = max(1, half // 4)
        grid = half // chunk
        block = (chunk,) + kept.shape[1:]
        upper = pl.BlockSpec(block, lambda i, place: (place[1 + at] * grid + i, 0, 0))
        lower = pl.BlockSpec(block, lambda i, place: ((1 - place[1 + at]) * grid + i, 0, 0))
        straight = pl.BlockSpec(block, lambda i, place: (i, 0, 0))

        def body(place, kept_up, kept_low, other_up, other_low, last, stay, leave):
            stay[...] = kept_up[...].astype(F32) + other_up[...].astype(F32)
            leave[...] = (kept_low[...].astype(F32) + other_low[...].astype(F32)).astype(BF16)

        def kernel(last):
            return pl.pallas_call(
                body,
                grid_spec=pltpu.PrefetchScalarGridSpec(
                    num_scalar_prefetch=1,
                    grid=(grid,),
                    in_specs=[upper, lower, upper, lower, ANY],
                    out_specs=(straight, straight),
                ),
                out_shape=(
                    jax.ShapeDtypeStruct((half,) + kept.shape[1:], F32),
                    jax.ShapeDtypeStruct((half,) + kept.shape[1:], BF16),
                ),
                compiler_params=params(24),
                cost_estimate=cost(self.length()),
                name="halve",
            )(self.place, kept, kept, other, other, last)

        return self.run(kernel)

    def reduce(self, parts, first, last):
        for at in list(range(len(self.steps)))[::-1][first:last]:
            kept, low = self.halve(at, *parts)
            parts = kept, self.swap(low, *self.steps[at])
        return parts


def settle(parts):
    return parts[0][0].astype(F32) + parts[1][0].astype(F32)


def collect(into, rows, slots, core, held, other):
    for place, (parity, piece) in enumerate(slots):
        mine = held(piece)
        theirs = other(piece)
        first, second = (mine, theirs) if parity == 0 else (theirs, mine)
        into[place * rows : (place + 1) * rows, :] = jnp.where(core == 0, first, second)


def deal(values, rows, slots, core, kept, sent):
    halves = ({}, {})
    for place, (parity, piece) in enumerate(slots):
        halves[parity][piece] = values[place * rows : (place + 1) * rows, :]
    for piece, even in halves[0].items():
        odd = halves[1][piece]
        kept(piece, jnp.where(core == 0, even, odd))
        sent(piece, jnp.where(core == 0, odd, even))


def standard(values):
    centred = values - jnp.mean(values, axis=-1, keepdims=True)
    rate = lax.rsqrt(jnp.mean(centred * centred, axis=-1, keepdims=True) + 1e-06)
    return centred * rate, rate


def standard_back(grad, gain, standardised, rate):
    pushed = grad * gain
    along = jnp.mean(pushed * standardised, axis=-1, keepdims=True)
    inner = pushed - jnp.mean(pushed, axis=-1, keepdims=True) - standardised * along
    sums = (jnp.sum(grad * standardised, axis=0, keepdims=True), jnp.sum(grad, axis=0, keepdims=True))
    return (rate * inner,) + sums


def first_half(width):
    return lax.broadcasted_iota(jnp.int32, (SLOT, 2 * HEAD_DIM), 1) < HEAD_DIM


def line_up_kernel(*refs):
    *lines, bias, columns = refs
    rows = columns.shape[1]
    lines = [line[...].astype(F32).reshape(1, rows) for line in lines]
    bias = bias[...].astype(F32).reshape(1, -1)
    lines += [bias[:, at : at + rows] for at in range(0, bias.shape[1], rows)]
    lines.append(jnp.zeros((128 - len(lines), rows), F32))
    columns[0] = jnp.concatenate(lines, axis=0).T.astype(BF16)


def spread_kernel(images, live, block_in, cotangent, earlier, x_ref, dm_ref):
    for ref, into in ((block_in, x_ref), (cotangent, dm_ref)):
        values = ref[...].astype(F32)
        for image in range(images):
            part = values[image * LEN : (image + 1) * LEN]
            if into is dm_ref:
                part = jnp.where(live[image * LEN] != 0, part, 0.0)
            part = jnp.concatenate([part, jnp.zeros((SLOT - LEN, D), F32)], axis=0)
            into[image * SLOT : (image + 1) * SLOT, :] = part.astype(BF16)


def trim(values):
    parts = [values[at : at + LEN] for at in range(0, values.shape[0], SLOT)]
    return jnp.concatenate(parts, axis=0)


def join_kernel(*refs):
    *parts, earlier, out = refs
    start = 0
    for part in parts:
        out[0, :, start : start + part.shape[1]] = part[...]
        start += part.shape[1]


def attend_kernel(slots, rows, place, x_ref, held, other, earlier, normed, qkv, attended, lse, vec, weight, columns):
    core = place[0]
    collect(
        weight,
        rows,
        slots,
        core,
        lambda p: held[p[0], p[1], :, : 3 * D],
        lambda p: other[p[0], p[1], :, : 3 * D],
    )
    collect(
        columns,
        rows,
        slots,
        core,
        lambda p: held[p[0], p[1], :, 3 * D :],
        lambda p: other[p[0], p[1], :, 3 * D :],
    )
    vec[...] = columns[...].astype(F32).T[: vec.shape[0], :]
    shaped, _ = standard(x_ref[...].astype(F32))
    low = (shaped * vec[0:1, :] + vec[1:2, :]).astype(BF16)
    normed[...] = low
    for part, row in ((0, 2), (1, None), (2, 3)):
        cols = pl.ds(part * D, D)
        packed = mul(low, weight[:, cols])
        if row is not None:
            packed = packed + vec[row : row + 1, :]
        qkv[:, cols] = packed.astype(BF16)
    left = first_half(0)
    real = lax.broadcasted_iota(jnp.int32, (SLOT, SLOT), 1) < LEN
    lane = lax.broadcasted_iota(jnp.int32, (SLOT, 128), 1)
    images = x_ref.shape[0] // SLOT
    lse[...] = jnp.zeros_like(lse)

    def pair_step(at, carry):
        image, pair = at // (HEADS // 2), at % (HEADS // 2)
        tokens = pl.ds(pl.multiple_of(image * SLOT, 16), SLOT)
        cols = lambda part: pl.ds(pl.multiple_of(part * D + pair * 128, 128), 128)
        query, key, value = qkv[tokens, cols(0)], qkv[tokens, cols(1)], qkv[tokens, cols(2)]
        mixed, logs = [], lse[tokens, :]
        for side in range(2):
            chosen = left if side == 0 else ~left
            scores = mul_t(jnp.where(chosen, query, jnp.zeros_like(query)), key) * SCALE
            scores = jnp.where(real, scores, -1e30)
            top = jnp.max(scores, axis=-1, keepdims=True)
            raised = jnp.exp(scores - top)
            total = jnp.sum(raised, axis=-1, keepdims=True)
            logs = jnp.where(lane == pair * 2 + side, top + jnp.log(total), logs)
            mixed.append(mul((raised * (1.0 / total)).astype(BF16), value))
        lse[tokens, :] = logs
        attended[tokens, cols(0)] = jnp.where(left, mixed[0], mixed[1]).astype(BF16)
        return carry

    lax.fori_loop(0, images * (HEADS // 2), pair_step, 0)


def up_kernel(slots, plane_slots, rows, ff_rows, place, x_ref, attended, dm, held, other, vec, ubias, earlier, middle, normed, active, slope, kept, sent, weight):
    core = place[0]
    step = pl.program_id(0)
    collect(weight, rows, slots, core, lambda p: held[p[0], p[1]], lambda p: other[p[0], p[1]])

    @pl.when(step == 0)
    def _():
        total = x_ref[...].astype(F32) + mul(attended[...], weight[...]) + vec[4:5, :]
        middle[...] = total
        shaped, _ = standard(total)
        normed[...] = (shaped * vec[5:6, :] + vec[6:7, :]).astype(BF16)

    @pl.when(step > 0)
    def _():
        pre = mul(normed[...], weight[...]) + ubias[0:1, :]
        share = 0.5 + 0.5 * lax.erf(pre * (0.5**0.5))
        low = (pre * share).astype(BF16)
        active[...] = low
        slope[...] = share + pre * (jnp.exp(pre * pre * -0.5) * 0.3989422804014327)
        grad = t_mul(low, dm[...]).astype(BF16)

        def put(ref):
            def store(piece, value):
                ref[piece[0], 0] = value

            return store

        deal(grad, ff_rows, plane_slots, core, put(kept), put(sent))


def down_kernel(slots, plane_slots, rows, ff_rows, place, live, dm, middle, normed, attended, active, slope, held, other, dheld, dother, vec, earlier, dmid, datt, kept, sent, sums, usums, result, weight, dweight, mixed, back):
    core = place[0]
    step = pl.program_id(0)
    collect(weight, rows, slots, core, lambda p: held[p[0], p[1]], lambda p: other[p[0], p[1]])

    def put(ref):
        def store(piece, value):
            ref[piece[0], piece[1]] = value

        return store

    @pl.when(step < 4)
    def _():
        collect(dweight, ff_rows, plane_slots, core, lambda p: dheld[p[0], 0], lambda p: dother[p[0], 0])
        grad = mul_t(dm[...], dweight[...]) * slope[...]
        low = grad.astype(BF16)
        usums[...] = jnp.broadcast_to(jnp.sum(low.astype(F32), axis=0, keepdims=True), usums.shape)
        deal(t_mul(normed[...], low).astype(BF16), rows, slots, core, put(kept), put(sent))
        more = mul(active[...], dweight[...])
        turned = mul_t(low, weight[...])

        @pl.when(step == 0)
        def _():
            mixed[...] = more
            back[...] = turned

        @pl.when(step > 0)
        def _():
            mixed[...] += more
            back[...] += turned

    @pl.when(step == 4)
    def _():
        source = dm[...].astype(F32)
        full = middle[...] + mixed[...] + vec[7:8, :]
        keep = jnp.concatenate(
            [jnp.where(live[image * LEN] != 0, full[image * SLOT : image * SLOT + LEN], 0.0) for image in range(full.shape[0] // SLOT)],
            axis=0,
        )
        result[...] = keep.astype(BF16)
        shaped, rate = standard(middle[...])
        inner, ggain, gshift = standard_back(back[...], vec[5:6, :], shaped, rate)
        total = source + inner
        dmid[...] = total
        low = total.astype(BF16)
        datt[...] = mul_t(low, weight[...]).astype(BF16)
        deal(t_mul(attended[...], low).astype(BF16), rows, slots, core, put(kept), put(sent))
        gout = jnp.sum(low.astype(F32), axis=0, keepdims=True)
        gdown = jnp.sum(source, axis=0, keepdims=True)
        sums[...] = jnp.concatenate([gout, ggain, gshift, gdown] * 2, axis=0)


def heads_kernel(qkv, datt, lse, earlier, dqkv):
    left = first_half(0)
    real = lax.broadcasted_iota(jnp.int32, (SLOT, SLOT), 1) < LEN
    lane = lax.broadcasted_iota(jnp.int32, (SLOT, 128), 1)
    logs = lse[...]

    def pair_step(pair, carry):
        cols = lambda part: pl.ds(pl.multiple_of(part * D + pair * 128, 128), 128)
        query, key, value = qkv[:, cols(0)], qkv[:, cols(1)], qkv[:, cols(2)]
        grad = datt[:, cols(0)]
        dq, dk, dv = [], [], []
        for side in range(2):
            chosen = left if side == 0 else ~left
            scores = mul_t(jnp.where(chosen, query, jnp.zeros_like(query)), key) * SCALE
            log = jnp.sum(jnp.where(lane == pair * 2 + side, logs, 0.0), axis=-1, keepdims=True)
            attn = jnp.where(real, jnp.exp(scores - log), 0.0)
            dattn = mul_t(jnp.where(chosen, grad, jnp.zeros_like(grad)), value)
            dscores = (attn * (dattn - jnp.sum(attn * dattn, axis=-1, keepdims=True))).astype(BF16)
            dv.append(t_mul(attn.astype(BF16), grad))
            dq.append(mul(dscores, key) * SCALE)
            dk.append(t_mul(dscores, query) * SCALE)
        for part, halves in ((0, dq), (1, dk), (2, dv)):
            dqkv[:, cols(part)] = jnp.where(left, halves[0], halves[1]).astype(BF16)
        return carry

    lax.fori_loop(0, HEADS // 2, pair_step, 0)


def input_kernel(slots, rows, images, place, x_ref, dmid, normed, *refs):
    dqkv, (held, other, vec, sums, usums, earlier, kept, sent, igrad, weight) = refs[:images], refs[images:]
    core = place[0]
    collect(
        weight,
        rows,
        slots,
        core,
        lambda p: held[p[0], p[1], :, : 3 * D],
        lambda p: other[p[0], p[1], :, : 3 * D],
    )

    def put(ref, cols):
        def store(piece, value):
            ref[piece[0], piece[1], :, cols] = value

        return store

    back = None
    rowsums = []
    for part in range(3):
        cols = pl.ds(part * D, D)
        low = jnp.concatenate([ref[:, cols] for ref in dqkv], axis=0)
        rowsums.append(jnp.sum(low.astype(F32), axis=0, keepdims=True))
        grad = t_mul(normed[...], low).astype(BF16)
        deal(grad, rows, slots, core, put(kept, cols), put(sent, cols))
        more = mul_t(low, weight[:, cols])
        back = more if back is None else back + more
    shaped, rate = standard(x_ref[...].astype(F32))
    inner, ggain, gshift = standard_back(back, vec[0:1, :], shaped, rate)
    igrad[...] = trim(dmid[...] + inner)
    lines = [ggain, gshift, rowsums[0], rowsums[2], sums[0:4, :], usums[0:4, :]]
    lines.append(jnp.zeros((128 - 12, D), F32))
    columns = jnp.concatenate(lines, axis=0).T.astype(BF16)
    cols = pl.ds(3 * D, 128)
    deal(columns, rows, slots, core, put(kept, cols), put(sent, cols))


def shards(
    block_in,
    slot_mask,
    gain_first,
    shift_first,
    packed_weight,
    query_bias,
    value_bias,
    out_weight,
    out_bias,
    gain_second,
    shift_second,
    up_weight,
    up_bias,
    down_weight,
    down_bias,
    cotangent,
):
    links = Links(lax.axis_size("dp"))
    rows = packed_weight.shape[0]
    ff_rows = down_weight.shape[0]
    wide = ff_rows // rows
    count, plane, depth = links.count, links.plane, links.z
    slots = tuple((i % 2, links.slot(i)) for i in range(count))
    per_plane = count // depth
    plane_slots = slots[:per_plane]
    place = links.place
    tokens = block_in.shape[0]
    images = tokens // LEN
    size = images * SLOT
    shape = jax.ShapeDtypeStruct
    steps_z = depth.bit_length() - 1
    final = len(links.steps)

    gather_a = packed_weight[None]
    came_a = links.swap(gather_a, *links.steps[0])
    vectors = (gain_first, shift_first, query_bias, value_bias, out_bias, gain_second, shift_second, down_bias, up_bias)
    line_up = pl.pallas_call(
        line_up_kernel,
        out_shape=shape((1, rows, 128), BF16),
        in_specs=[VMEM] * 9,
        out_specs=VMEM,
        cost_estimate=cost(links.length()),
        name="line_up",
    )
    columns = links.run(lambda last: line_up(*vectors))
    came_v = links.swap(columns, *links.steps[0])
    x, dm = links.run(
        lambda last: pl.pallas_call(
            functools.partial(spread_kernel, images),
            out_shape=(shape((size, D), BF16), shape((size, D), BF16)),
            in_specs=[SMEM, VMEM, VMEM, ANY],
            out_specs=(VMEM, VMEM),
            compiler_params=pltpu.CompilerParams(vmem_limit_bytes=16 << 20),
            cost_estimate=cost(links.length()),
            name="spread",
        )(slot_mask, block_in, cotangent, last)
    )

    def joined(*parts):
        width = sum(part.shape[1] for part in parts)
        return links.run(
            lambda last: pl.pallas_call(
                join_kernel,
                out_shape=shape((1, parts[0].shape[0], width), BF16),
                in_specs=[VMEM] * len(parts) + [ANY],
                out_specs=VMEM,
                cost_estimate=cost(links.length()),
                name="join",
            )(*parts, last)
        )

    gather_a = links.pair(0, (gather_a, came_a))
    gather_b = joined(out_weight, up_weight)
    columns = links.pair(0, (columns, came_v))
    if steps_z > 2:
        gather_a = links.advance(gather_a, 1, steps_z - 1)
        columns = links.advance(columns, 1, steps_z - 1)
    at = steps_z - 1
    came_a, came_v = links.swap(gather_a, *links.steps[at]), links.swap(columns, *links.steps[at])
    came_b = links.swap(gather_b, *links.steps[0])
    gather_a = links.pair(at, (gather_a, came_a), (columns, came_v))
    gather_b = links.pair(0, (gather_b, came_b))
    gather_c = joined(down_weight)
    gather_a = links.advance(gather_a, steps_z, final - 1)
    gather_b = links.advance(gather_b, 1, steps_z)
    gather_c = links.advance(gather_c, 0, 1)
    held_a, other_a = links.across(links.advance(gather_a, final - 1, final))
    gather_b = links.advance(gather_b, steps_z, final - 1)
    gather_c = links.advance(gather_c, 1, steps_z)

    wide_a = 3 * D + 128
    normed, qkv, attended, lse, vec = links.run(
        lambda last: pl.pallas_call(
            functools.partial(attend_kernel, slots, rows),
            out_shape=(
                shape((size, D), BF16),
                shape((size, 3 * D), BF16),
                shape((size, D), BF16),
                shape((size, 128), F32),
                shape((16, D), F32),
            ),
            in_specs=[SMEM] + [VMEM] * 3 + [ANY],
            out_specs=(VMEM,) * 5,
            scratch_shapes=[pltpu.VMEM((D, 3 * D), BF16), pltpu.VMEM((D, 128), BF16)],
            compiler_params=pltpu.CompilerParams(vmem_limit_bytes=32 << 20),
            cost_estimate=cost(links.length()),
            name="attend",
        )(place, x, held_a, other_a, last)
    )
    ubias = vec[8 : 8 + wide].reshape(wide, count, rows).transpose(1, 0, 2).reshape(1, FF)
    gather_c = links.advance(gather_c, steps_z, final - 1)
    held_b, other_b = links.across(links.advance(gather_b, final - 1, final))

    fixed = lambda height, width: pl.BlockSpec((height, width), lambda t: (0, 0))
    z_place = lambda t: jnp.where(depth == 4, (t % 2) * 2 + t // 2, t)
    tile = FF // depth
    steps = depth + 1

    before = lambda t: jnp.maximum(t - 1, 0)
    block_b = pl.BlockSpec((plane, depth, rows, D), lambda t: (0, 0, 0, t))
    tiled = lambda height, at: pl.BlockSpec((height, tile), lambda t: (0, at(t)))
    dealt = pl.BlockSpec((plane, 1, ff_rows, D), lambda t: (0, z_place(before(t)), 0, 0))
    middle, normed_two, active, slope, kept_c, sent_c = links.run(
        lambda last: pl.pallas_call(
            functools.partial(up_kernel, slots, plane_slots, rows, ff_rows),
            grid=(steps,),
            out_shape=(
                shape((size, D), F32),
                shape((size, D), BF16),
                shape((size, FF), BF16),
                shape((size, FF), F32),
                shape((plane, depth, ff_rows, D), BF16),
                shape((plane, depth, ff_rows, D), BF16),
            ),
            in_specs=[SMEM] + [fixed(size, D)] * 3 + [block_b, block_b, fixed(16, D), tiled(1, before), ANY],
            out_specs=(fixed(size, D), fixed(size, D), tiled(size, before), tiled(size, before), dealt, dealt),
            scratch_shapes=[pltpu.VMEM((D, D), BF16)],
            compiler_params=params(32),
            cost_estimate=cost(links.length()),
            name="up",
        )(place, x, attended, dm, held_b, other_b, vec, ubias, last)
    )
    held_c, other_c = links.across(links.advance(gather_c, final - 1, final))
    parts_c = links.exchange(kept_c, sent_c)
    parts_c = links.reduce(parts_c, 0, 1)

    upto = lambda t: jnp.minimum(t, depth - 1)
    block_b = pl.BlockSpec((plane, depth, rows, D), lambda t: (0, 0, 0, (t + 1) % steps))
    block_c = pl.BlockSpec((plane, 1, ff_rows, D), lambda t: (0, z_place(upto(t)), 0, 0))
    dmid, datt, kept_b, sent_b, sums, usums, block_out = links.run(
        lambda last: pl.pallas_call(
            functools.partial(down_kernel, slots, plane_slots, rows, ff_rows),
            grid=(steps,),
            out_shape=(
                shape((size, D), F32),
                shape((size, D), BF16),
                shape((plane, depth, rows, D + FF), BF16),
                shape((plane, depth, rows, D + FF), BF16),
                shape((8, D), F32),
                shape((8, FF), F32),
                shape((tokens, D), BF16),
            ),
            in_specs=[SMEM, SMEM]
            + [fixed(size, D)] * 4
            + [tiled(size, upto), tiled(size, upto), block_b, block_b, block_c, block_c, fixed(16, D), ANY],
            out_specs=(
                fixed(size, D),
                fixed(size, D),
                block_b,
                block_b,
                fixed(8, D),
                tiled(8, upto),
                fixed(tokens, D),
            ),
            scratch_shapes=[
                pltpu.VMEM((D, D), BF16),
                pltpu.VMEM((D, D), BF16),
                pltpu.VMEM((size, D), F32),
                pltpu.VMEM((size, D), F32),
            ],
            compiler_params=params(40),
            cost_estimate=cost(links.length()),
            name="down",
        )(
            place,
            slot_mask,
            dm,
            middle,
            normed_two,
            attended,
            active,
            slope,
            held_b,
            other_b,
            held_c,
            other_c,
            vec,
            last,
        )
    )
    parts_b = links.exchange(kept_b, sent_b)
    parts_c = links.reduce(parts_c, 1, final - 2)
    usums = usums[0].reshape(count, wide, rows).transpose(1, 0, 2).reshape(wide, D)
    usums = jnp.pad(usums, ((0, 8 - wide), (0, 0)))

    def heads(image):
        row = lambda width: pl.BlockSpec((SLOT, width), lambda i: (image, 0))
        return links.run(
            lambda last: pl.pallas_call(
                heads_kernel,
                grid=(1,),
                out_shape=shape((SLOT, 3 * D), BF16),
                in_specs=[row(3 * D), row(D), row(128), ANY],
                out_specs=pl.BlockSpec((SLOT, 3 * D), lambda i: (0, 0)),
                compiler_params=params(16),
                cost_estimate=cost(links.length()),
                name="heads",
            )(qkv, datt, lse, last)
        )

    dqkv = [heads(0)]
    parts_b = links.reduce(parts_b, 0, 1)
    dqkv += [heads(image) for image in range(1, images)]
    parts_c = links.reduce(parts_c, final - 2, final - 1)
    kept_a, sent_a, igrad = links.run(
        lambda last: pl.pallas_call(
            functools.partial(input_kernel, slots, rows, images),
            out_shape=(
                shape((plane, depth, rows, wide_a), BF16),
                shape((plane, depth, rows, wide_a), BF16),
                shape((tokens, D), F32),
            ),
            in_specs=[SMEM] + [VMEM] * (8 + images) + [ANY],
            out_specs=(VMEM,) * 3,
            scratch_shapes=[pltpu.VMEM((D, 3 * D), BF16)],
            compiler_params=pltpu.CompilerParams(vmem_limit_bytes=36 << 20),
            cost_estimate=cost(links.length()),
            name="inward",
        )(place, x, dmid, normed, *dqkv, held_a, other_a, vec, sums, usums, last)
    )
    parts_a = links.exchange(kept_a, sent_a)
    parts_b = links.reduce(parts_b, 1, final - 2)
    parts_c = links.reduce(parts_c, final - 1, final)
    parts_a = links.reduce(parts_a, 0, 1)
    parts_b = links.reduce(parts_b, final - 2, final - 1)
    parts_a = links.reduce(parts_a, 1, final - 2)
    parts_b = links.reduce(parts_b, final - 1, final)
    parts_a = links.reduce(parts_a, final - 2, final)
    grads_a, grads_b, grad_down_weight = settle(parts_a), settle(parts_b), settle(parts_c)
    small = grads_a[:, 3 * D : 3 * D + 8 + wide].T
    return (
        block_out,
        igrad,
        small[0],
        small[1],
        grads_a[:, : 3 * D],
        small[2],
        small[3],
        grads_b[:, :D],
        small[4],
        small[5],
        small[6],
        grads_b[:, D:],
        small[8:].reshape(-1),
        grad_down_weight,
        small[7],
    )


def solution(mesh):
    row, flat = P("dp", None), P("dp")
    in_specs = (row, flat, flat, flat, row, flat, flat, row, flat, flat, flat, row, flat, row, flat, row)
    out_specs = (row, row, flat, flat, row, flat, flat, row, flat, flat, flat, row, flat, row, flat)
    return jax.shard_map(shards, mesh=mesh, in_specs=in_specs, out_specs=out_specs, check_vma=False)
```

profile of v0, /device:TPU:0, one launch (start us, length us, event | category | flops | bytes accessed | tf_op | source)
XLA Modules:
  0.0 231.0 jit_solution(8128672215924251020)
XLA Ops:
  0.7 4.1 %collective-permute-start = (bf16[1,24,2304]{2,1,0:T(8,128)(2,1)}, bf16[1,24,2304]{2,1,0:T(8,128)(2,1)S(1)}, u32[]{:S(2)}, u32[]{:S(2)}) collective-permute-start(bf16[1,24,2304]{2,1,0:T(8,128)(2,1)} %bitcast.64), channel_id=1, source_target_pairs={{0,16},{1,17},{2,18},{3,19},{4,20},{5,21},{6,22},{7,23},{8,24},{9,... | collective-permute-start | bytes 331784 | tf_op jit(solution)/shard_map/ppermute | solution.py:91
  4.8 1.5 line_up.1.earlier.refs_0_
  7.9 2.5 %collective-permute-done.refs_1_ = bf16[1,24,2304]{2,1,0:T(8,128)(2,1)S(1)} collective-permute-done((bf16[1,24,2304]{2,1,0:T(8,128)(2,1)}, bf16[1,24,2304]{2,1,0:T(8,128)(2,1)S(1)}, u32[]{:S(2)}, u32[]{:S(2)}) %collective-permute-start) | collective-permute-done | bytes 110624 | tf_op jit(solution)/shard_map/ppermute | solution.py:91
  11.9 1.6 join.2.refs_2_.refs_0_
  13.6 3.3 %collective-permute-start.5 = (bf16[1,24,3840]{2,1,0:T(8,128)(2,1)}, bf16[1,24,3840]{2,1,0:T(8,128)(2,1)S(1)}, u32[]{:S(2)}, u32[]{:S(2)}) collective-permute-start(bf16[1,24,3840]{2,1,0:T(8,128)(2,1)} %join.2.refs_2_.refs_0_), channel_id=1, source_target_pairs={{0,16},{1,17},{2,18},{3,19},{4,20},{5,21},{6,22},{7,23},{8,24},{9,... | collective-permute-start | bytes 552968 | tf_op jit(solution)/shard_map/ppermute | solution.py:91
  16.9 8.9 %collective-permute-done.1.refs_1_ = bf16[1,24,128]{2,1,0:T(8,128)(2,1)S(1)} collective-permute-done((bf16[1,24,128]{2,1,0:T(8,128)(2,1)S(1)}, bf16[1,24,128]{2,1,0:T(8,128)(2,1)S(1)}, u32[]{:S(2)}, u32[]{:S(2)}) %collective-permute-start.1) | collective-permute-done | bytes 6176 | tf_op jit(solution)/shard_map/ppermute | solution.py:91
  27.5 3.6 %collective-permute-done.3.refs_3_ = bf16[2,24,128]{2,1,0:T(8,128)(2,1)S(1)} collective-permute-done((bf16[2,24,128]{2,1,0:T(8,128)(2,1)S(1)}, bf16[2,24,128]{2,1,0:T(8,128)(2,1)S(1)}, u32[]{:S(2)}, u32[]{:S(2)}) %collective-permute-start.3) | collective-permute-done | bytes 12320 | tf_op jit(solution)/shard_map/ppermute | solution.py:91
  31.7 1.5 collective-permute-start.4
  33.2 1.3 pair.16.refs_1_
  34.7 1.6 join.3.refs_2_.refs_0_
  36.3 3.3 %collective-permute-start.7 = (bf16[1,96,768]{2,1,0:T(8,128)(2,1)}, bf16[1,96,768]{2,1,0:T(8,128)(2,1)S(1)}, u32[]{:S(2)}, u32[]{:S(2)}) collective-permute-start(bf16[1,96,768]{2,1,0:T(8,128)(2,1)} %join.3.refs_2_.refs_0_), channel_id=1, source_target_pairs={{0,16},{1,17},{2,18},{3,19},{4,20},{5,21},{6,22},{7,23},{8,24},{9,... | collective-permute-start | bytes 442376 | tf_op jit(solution)/shard_map/ppermute | solution.py:91
  41.8 1.5 collective-permute-start.6
  43.4 2.7 %collective-permute-done.8.refs_1_ = bf16[2,24,3840]{2,1,0:T(8,128)(2,1)S(1)} collective-permute-done((bf16[2,24,3840]{2,1,0:T(8,128)(2,1)}, bf16[2,24,3840]{2,1,0:T(8,128)(2,1)S(1)}, u32[]{:S(2)}, u32[]{:S(2)}) %collective-permute-start.8) | collective-permute-done | bytes 368672 | tf_op jit(solution)/shard_map/ppermute | solution.py:91
  46.1 1.1 pair.18.refs_2_
  47.2 1.6 collective-permute-start.11
  49.4 13.6 %collective-permute-done.6.refs_1_ = bf16[8,24,2432]{2,1,0:T(8,128)(2,1)S(1)} collective-permute-done((bf16[8,24,2432]{2,1,0:T(8,128)(2,1)S(1)}, bf16[8,24,2432]{2,1,0:T(8,128)(2,1)S(1)}, u32[]{:S(2)}, u32[]{:S(2)}) %collective-permute-start.6) | collective-permute-done | bytes 933920 | tf_op jit(solution)/shard_map/ppermute | solution.py:91
  65.6 3.0 %collective-permute-start.13 = (bf16[4,96,768]{2,1,0:T(8,128)(2,1)S(1)}, bf16[4,96,768]{2,1,0:T(8,128)(2,1)S(1)}, u32[]{:S(2)}, u32[]{:S(2)}) collective-permute-start(bf16[4,96,768]{2,1,0:T(8,128)(2,1)S(1)} %bitcast.50), channel_id=1, source_target_pairs={{0,2},{1,5},{2,0},{3,7},{4,6},{5,1},{6,4},{7,3},{8,10},{9,13},{10,... | collective-permute-start | bytes 1769480 | tf_op jit(solution)/shard_map/ppermute | solution.py:91
  68.6 13.5 %attend.1 = (bf16[416,768]{1,0:T(8,128)(2,1)S(1)}, bf16[416,2304]{1,0:T(8,128)(2,1)S(1)}, bf16[416,768]{1,0:T(8,128)(2,1)S(1)}, f32[416,128]{1,0:T(8,128)S(1)}, f32[16,768]{1,0:T(8,128)S(1)}) custom-call(s32[5]{0:T(128)S(1)} %stack.39.place, bf16[416,768]{1,0:T(8,128)(2,1)S(1)} %get-tuple-element.63.refs_2_.x_ref, bf16[4,4,24,2432]{3,2,1,0:T(8,128)(2,1)S(1)} %bitcast.44, ...), custom_call_target="tpu_custom_call" | custom-call | flops 2300000000 | bytes 768 | tf_op jit(solution)/shard_map/attend/pallas_call | solution.py:551
  83.5 6.8 %collective-permute-done.12.refs_1_ = bf16[8,24,3840]{2,1,0:T(8,128)(2,1)S(1)} collective-permute-done((bf16[8,24,3840]{2,1,0:T(8,128)(2,1)S(1)}, bf16[8,24,3840]{2,1,0:T(8,128)(2,1)S(1)}, u32[]{:S(2)}, u32[]{:S(2)}) %collective-permute-start.12) | collective-permute-done | bytes 1474592 | tf_op jit(solution)/shard_map/ppermute | solution.py:91
  90.3 2.4 %pair.24.earlier = bf16[2,8,24,3840]{3,2,1,0:T(8,128)(2,1)} custom-call(s32[5]{0:T(128)S(1)} %stack.39.place, bf16[8,24,3840]{2,1,0:T(8,128)(2,1)S(1)} %bitcast.47, bf16[8,24,3840]{2,1,0:T(8,128)(2,1)S(1)} %collective-permute-done.12.refs_1_, bf16[2,4,96,768]{3,2,1,0:T(8,128)(2,1)S(1)} %pair.23.refs_2_), custom_call_target="tpu_custom_call" | custom-call | flops 575000000 | bytes 768 | tf_op jit(solution)/shard_map/pair/pallas_call | solution.py:114
  94.1 4.4 %collective-permute-done.14.other = bf16[4,4,24,3840]{3,2,1,0:T(8,128)(2,1)} collective-permute-done((bf16[4,4,24,3840]{3,2,1,0:T(8,128)(2,1)}, bf16[4,4,24,3840]{3,2,1,0:T(8,128)(2,1)}, u32[]{:S(2)}, u32[]{:S(2)}) %collective-permute-start.14) | collective-permute-done | bytes 2949152 | tf_op jit(solution)/shard_map/ppermute | solution.py:91
  98.5 1.1 copy-done.23
  99.6 1.1 copy-done.33
  100.7 10.8 %up.1 = (f32[416,768]{1,0:T(8,128)S(1)}, bf16[416,768]{1,0:T(8,128)(2,1)S(1)}, bf16[416,3072]{1,0:T(8,128)(2,1)S(1)}, f32[416,3072]{1,0:T(8,128)S(1)}, bf16[4,4,...) custom-call(s32[5]{0:T(128)S(1)} %stack.39.place, bf16[416,768]{1,0:T(8,128)(2,1)S(1)} %get-tuple-element.63.refs_2_.x_ref, ...), custom_call_target="tpu_custom_call" | custom-call | flops 27599998976 | bytes 768 | tf_op jit(solution)/shard_map/up/pallas_call | solution.py:582
  111.5 2.3 copy-done.30
  115.4 2.9 %collective-permute-done.17 = bf16[4,4,96,768]{3,2,1,0:T(8,128)(2,1)S(1)} collective-permute-done((bf16[4,4,96,768]{3,2,1,0:T(8,128)(2,1)S(1)}, bf16[4,4,96,768]{3,2,1,0:T(8,128)(2,1)S(1)}, u32[]{:S(2)}, u32[]{:S(2)}) %collective-permute-start.17) | collective-permute-done | bytes 2359328 | tf_op jit(solution)/shard_map/ppermute | solution.py:91
  118.3 2.4 %halve.12 = (f32[8,96,768]{2,1,0:T(8,128)S(1)}, bf16[8,96,768]{2,1,0:T(8,128)(2,1)}) custom-call(s32[5]{0:T(128)S(1)} %stack.39.place, bf16[16,96,768]{2,1,0:T(8,128)(2,1)S(1)} %bitcast.35, bf16[16,96,768]{2,1,0:T(8,128)(2,1)S(1)} %bitcast.36, bf16[16,96,768]{2,1,0:T(8,128)(2,1)S(1)} %bitcast.37, bf16[16,96,768]{2,1,0:T(8,128)(2,1)S(1)} %bitcast.38, ...), custom_call_target="tpu_custom_call" | custom-call | flops 1150000000 | bytes 768 | tf_op jit(solution)/shard_map/halve/pallas_call | solution.py:154
  121.7 17.2 %down.1 = (f32[416,768]{1,0:T(8,128)S(1)}, bf16[416,768]{1,0:T(8,128)(2,1)S(1)}, bf16[4,4,24,3840]{3,2,1,0:T(8,128)(2,1)}, bf16[4,4,24,3840]{3,2,1,0:T(8,128)(2,...) custom-call(s32[5]{0:T(128)S(1)} %stack.39.place, s32[394]{0:T(512)S(1)} %copy-done.21, ...), custom_call_target="tpu_custom_call" | custom-call | flops 6899999744 | bytes 768 | tf_op jit(solution)/shard_map/down/pallas_call | solution.py:609
  138.9 1.0 copy-done
  142.8 1.5 copy.35
  145.3 1.3 copy-done.1
  147.4 1.9 collective-permute-start.20
  149.3 5.8 %heads.2.last.refs_0_ = bf16[208,2304]{1,0:T(8,128)(2,1)S(1)} custom-call(bf16[416,2304]{1,0:T(8,128)(2,1)S(1)} %copy-done.38, bf16[416,768]{1,0:T(8,128)(2,1)S(1)} %copy-done.36, f32[416,128]{1,0:T(8,128)S(1)} %copy-done.40, f32[4,96,768]{2,1,0:T(8,128)S(1)} %get-tuple-element.80.earlier.kept_up.kept_low), custom_call_target="tpu_custom_call" | custom-call | flops 18400000000 | bytes 768 | tf_op jit(solution)/shard_map/heads/pallas_call | solution.py:667
  155.1 3.4 %halve.14 = (f32[8,24,3840]{2,1,0:T(8,128)S(1)}, bf16[8,24,3840]{2,1,0:T(8,128)(2,1)S(1)}) custom-call(s32[5]{0:T(128)S(1)} %stack.39.place, bf16[16,24,3840]{2,1,0:T(8,128)(2,1)S(1)} %bitcast.68, bf16[16,24,3840]{2,1,0:T(8,128)(2,1)S(1)} %bitcast.69, bf16[16,24,3840]{2,1,0:T(8,128)(2,1)} %bitcast.23.other_up.other_low, ...), custom_call_target="tpu_custom_call" | custom-call | flops 27599998976 | bytes 768 | tf_op jit(solution)/shard_map/halve/pallas_call | solution.py:154
  158.5 1.1 collective-permute-start.23
  159.6 5.8 %heads.3.last.refs_1_ = bf16[208,2304]{1,0:T(8,128)(2,1)S(1)} custom-call(bf16[416,2304]{1,0:T(8,128)(2,1)S(1)} %copy-done.38, bf16[416,768]{1,0:T(8,128)(2,1)S(1)} %copy-done.36, f32[416,128]{1,0:T(8,128)S(1)} %copy-done.40, f32[8,24,3840]{2,1,0:T(8,128)S(1)} %get-tuple-element.83.earlier.kept_up.kept_low), custom_call_target="tpu_custom_call" | custom-call | flops 18400000000 | bytes 768 | tf_op jit(solution)/shard_map/heads/pallas_call | solution.py:667
  167.6 6.0 %inward.1 = (bf16[4,4,24,2432]{3,2,1,0:T(8,128)(2,1)S(1)}, bf16[4,4,24,2432]{3,2,1,0:T(8,128)(2,1)S(1)}, f32[394,768]{1,0:T(8,128)}) custom-call(s32[5]{0:T(128)S(1)} %stack.39.place, bf16[416,768]{1,0:T(8,128)(2,1)S(1)} %copy-done.10, f32[416,768]{1,0:T(8,128)S(1)} %copy-done.2, bf16[416,768]{1,0:T(8,128)(2,1)S(1)} %copy-done.4, ...), custom_call_target="tpu_custom_call" | custom-call | flops 575000000 | bytes 768 | tf_op jit(solution)/shard_map/inward/pallas_call | solution.py:684
  173.6 4.3 %collective-permute-done.23.other_up.other_low = bf16[8,24,3840]{2,1,0:T(8,128)(2,1)S(1)} collective-permute-done((bf16[8,24,3840]{2,1,0:T(8,128)(2,1)S(1)}, bf16[8,24,3840]{2,1,0:T(8,128)(2,1)S(1)}, u32[]{:S(2)}, u32[]{:S(2)}) %collective-permute-start.23) | collective-permute-done | bytes 1474592 | tf_op jit(solution)/shard_map/ppermute | solution.py:91
  180.4 1.0 halve.18
  181.4 1.1 collective-permute-start.24
  182.5 15.4 %collective-permute-done.25.other_up.other_low = bf16[4,24,3840]{2,1,0:T(8,128)(2,1)S(1)} collective-permute-done((bf16[4,24,3840]{2,1,0:T(8,128)(2,1)S(1)}, bf16[4,24,3840]{2,1,0:T(8,128)(2,1)S(1)}, u32[]{:S(2)}, u32[]{:S(2)}) %collective-permute-start.25) | collective-permute-done | bytes 737312 | tf_op jit(solution)/shard_map/ppermute | solution.py:91
  200.8 2.4 %collective-permute-start.31 = (bf16[1,96,768]{2,1,0:T(8,128)(2,1)S(1)}, bf16[1,96,768]{2,1,0:T(8,128)(2,1)S(1)}, u32[]{:S(2)}, u32[]{:S(2)}) collective-permute-start(bf16[1,96,768]{2,1,0:T(8,128)(2,1)S(1)} %get-tuple-element.108), channel_id=1, source_target_pairs={{0,16},{1,17},{2,18},{3,19},{4,20},{5,21},{6,22},{7,23},{8,24},{9,... | collective-permute-start | bytes 442376 | tf_op jit(solution)/shard_map/ppermute | solution.py:91
  203.2 4.6 %collective-permute-done.27.other_up.other_low = bf16[2,24,3840]{2,1,0:T(8,128)(2,1)S(1)} collective-permute-done((bf16[2,24,3840]{2,1,0:T(8,128)(2,1)S(1)}, bf16[2,24,3840]{2,1,0:T(8,128)(2,1)S(1)}, u32[]{:S(2)}, u32[]{:S(2)}) %collective-permute-start.27) | collective-permute-done | bytes 368672 | tf_op jit(solution)/shard_map/ppermute | solution.py:91
  209.2 1.9 collective-permute-start.28
  212.2 1.1 collective-permute-start.30
  213.3 5.7 %collective-permute-done.28.other_up.other_low = bf16[2,24,2432]{2,1,0:T(8,128)(2,1)S(1)} collective-permute-done((bf16[2,24,2432]{2,1,0:T(8,128)(2,1)S(1)}, bf16[2,24,2432]{2,1,0:T(8,128)(2,1)S(1)}, u32[]{:S(2)}, u32[]{:S(2)}) %collective-permute-start.28) | collective-permute-done | bytes 233504 | tf_op jit(solution)/shard_map/ppermute | solution.py:91
  219.6 2.0 collective-permute-start.29
  221.6 5.2 %collective-permute-done.30 = bf16[1,24,3840]{2,1,0:T(8,128)(2,1)S(1)} collective-permute-done((bf16[1,24,3840]{2,1,0:T(8,128)(2,1)S(1)}, bf16[1,24,3840]{2,1,0:T(8,128)(2,1)S(1)}, u32[]{:S(2)}, u32[]{:S(2)}) %collective-permute-start.30) | collective-permute-done | bytes 184352 | tf_op jit(solution)/shard_map/ppermute | solution.py:91
  (154 shorter events, 35.3 us)
Async XLA Ops:
  0.7 5.8 %copy-start.11 = (bf16[394,768]{1,0:T(8,128)(2,1)S(1)}, bf16[394,768]{1,0:T(8,128)(2,1)}, u32[]{:S(2)}) copy-start(bf16[394,768]{1,0:T(8,128)(2,1)} %block_in.1) | copy-start | bytes 1815556
  0.7 5.7 %copy-start.12 = (bf16[394,768]{1,0:T(8,128)(2,1)S(1)}, bf16[394,768]{1,0:T(8,128)(2,1)}, u32[]{:S(2)}) copy-start(bf16[394,768]{1,0:T(8,128)(2,1)} %cotangent.1) | copy-start | bytes 1815556
  0.7 5.7 %copy-start.21 = (s32[394]{0:T(512)S(1)}, s32[394]{0:T(512)}, u32[]{:S(2)}) copy-start(s32[394]{0:T(512)} %live.3) | copy-start | bytes 4732
  0.7 9.8 %copy-start.28 = (bf16[24,2304]{1,0:T(8,128)(2,1)S(1)}, bf16[24,2304]{1,0:T(8,128)(2,1)}, u32[]{:S(2)}) copy-start(bf16[24,2304]{1,0:T(8,128)(2,1)} %param.20) | copy-start | bytes 331780
  0.7 9.7 %collective-permute-start = (bf16[1,24,2304]{2,1,0:T(8,128)(2,1)}, bf16[1,24,2304]{2,1,0:T(8,128)(2,1)S(1)}, u32[]{:S(2)}, u32[]{:S(2)}) collective-permute-start(bf16[1,24,2304]{2,1,0:T(8,128)(2,1)} %bitcast.64), channel_id=1, source_target_pairs={{0,16},{1,17},{2,18},{3,19},{4,20},{5,21},{6,22},{7,23},{8,24},{9,... | collective-permute-start | bytes 331784 | tf_op jit(solution)/shard_map/ppermute | solution.py:91
  7.9 90.6 %copy-start.9 = (bf16[416,768]{1,0:T(8,128)(2,1)}, bf16[416,768]{1,0:T(8,128)(2,1)S(1)}, u32[]{:S(2)}) copy-start(bf16[416,768]{1,0:T(8,128)(2,1)S(1)} %get-tuple-element.63.refs_2_.x_ref) | copy-start | bytes 1916932
  11.0 5.8 %copy-start.20 = (bf16[1,24,128]{2,1,0:T(8,128)(2,1)S(1)}, bf16[1,24,128]{2,1,0:T(8,128)(2,1)}, u32[]{:S(2)}) copy-start(bf16[1,24,128]{2,1,0:T(8,128)(2,1)} %line_up.1.earlier.refs_0_) | copy-start | bytes 18436
  11.0 20.0 %collective-permute-start.2 = (bf16[2,24,2304]{2,1,0:T(8,128)(2,1)S(1)}, bf16[2,24,2304]{2,1,0:T(8,128)(2,1)S(1)}, u32[]{:S(2)}, u32[]{:S(2)}) collective-permute-start(bf16[2,24,2304]{2,1,0:T(8,128)(2,1)S(1)} %bitcast.62), channel_id=1, source_target_pairs={{0,8},{1,9},{2,10},{3,11},{4,12},{5,13},{6,14},{7,15},{8,0},{9,1},... | collective-permute-start | bytes 663560 | tf_op jit(solution)/shard_map/ppermute | solution.py:91
  13.6 17.5 %copy-start.26 = (bf16[2,1,24,2304]{3,2,1,0:T(8,128)(2,1)S(1)}, bf16[2,1,24,2304]{3,2,1,0:T(8,128)(2,1)}, u32[]{:S(2)}) copy-start(bf16[2,1,24,2304]{3,2,1,0:T(8,128)(2,1)} %copy-done.25) | copy-start | bytes 663556
  13.6 19.6 %collective-permute-start.5 = (bf16[1,24,3840]{2,1,0:T(8,128)(2,1)}, bf16[1,24,3840]{2,1,0:T(8,128)(2,1)S(1)}, u32[]{:S(2)}, u32[]{:S(2)}) collective-permute-start(bf16[1,24,3840]{2,1,0:T(8,128)(2,1)} %join.2.refs_2_.refs_0_), channel_id=1, source_target_pairs={{0,16},{1,17},{2,18},{3,19},{4,20},{5,21},{6,22},{7,23},{8,24},{9,... | collective-permute-start | bytes 552968 | tf_op jit(solution)/shard_map/ppermute | solution.py:91
  16.8 9.0 %collective-permute-start.1 = (bf16[1,24,128]{2,1,0:T(8,128)(2,1)S(1)}, bf16[1,24,128]{2,1,0:T(8,128)(2,1)S(1)}, u32[]{:S(2)}, u32[]{:S(2)}) collective-permute-start(bf16[1,24,128]{2,1,0:T(8,128)(2,1)S(1)} %copy-done.20), channel_id=1, source_target_pairs={{0,16},{1,17},{2,18},{3,19},{4,20},{5,21},{6,22},{7,23},{8,24},{9,... | collective-permute-start | bytes 18440 | tf_op jit(solution)/shard_map/ppermute | solution.py:91
  27.3 3.8 %collective-permute-start.3 = (bf16[2,24,128]{2,1,0:T(8,128)(2,1)S(1)}, bf16[2,24,128]{2,1,0:T(8,128)(2,1)S(1)}, u32[]{:S(2)}, u32[]{:S(2)}) collective-permute-start(bf16[2,24,128]{2,1,0:T(8,128)(2,1)S(1)} %bitcast.66), channel_id=1, source_target_pairs={{0,8},{1,9},{2,10},{3,11},{4,12},{5,13},{6,14},{7,15},{8,0},{9,1},... | collective-permute-start | bytes 36872 | tf_op jit(solution)/shard_map/ppermute | solution.py:91
  31.7 8.6 %collective-permute-start.4 = (bf16[4,24,2432]{2,1,0:T(8,128)(2,1)S(1)}, bf16[4,24,2432]{2,1,0:T(8,128)(2,1)S(1)}, u32[]{:S(2)}, u32[]{:S(2)}) collective-permute-start(bf16[4,24,2432]{2,1,0:T(8,128)(2,1)S(1)} %bitcast.52), channel_id=1, source_target_pairs={{0,2},{1,5},{2,0},{3,7},{4,6},{5,1},{6,4},{7,3},{8,10},{9,13},{10,... | collective-permute-start | bytes 1400840 | tf_op jit(solution)/shard_map/ppermute | solution.py:91
  34.5 11.6 %collective-permute-start.8 = (bf16[2,24,3840]{2,1,0:T(8,128)(2,1)}, bf16[2,24,3840]{2,1,0:T(8,128)(2,1)S(1)}, u32[]{:S(2)}, u32[]{:S(2)}) collective-permute-start(bf16[2,24,3840]{2,1,0:T(8,128)(2,1)} %bitcast.10.refs_0_), channel_id=1, source_target_pairs={{0,8},{1,9},{2,10},{3,11},{4,12},{5,13},{6,14},{7,15},{8,0},{9,1},... | collective-permute-start | bytes 1105928 | tf_op jit(solution)/shard_map/ppermute | solution.py:91
  36.3 12.5 %collective-permute-start.7 = (bf16[1,96,768]{2,1,0:T(8,128)(2,1)}, bf16[1,96,768]{2,1,0:T(8,128)(2,1)S(1)}, u32[]{:S(2)}, u32[]{:S(2)}) collective-permute-start(bf16[1,96,768]{2,1,0:T(8,128)(2,1)} %join.3.refs_2_.refs_0_), channel_id=1, source_target_pairs={{0,16},{1,17},{2,18},{3,19},{4,20},{5,21},{6,22},{7,23},{8,24},{9,... | collective-permute-start | bytes 442376 | tf_op jit(solution)/shard_map/ppermute | solution.py:91
  41.8 21.2 %collective-permute-start.6 = (bf16[8,24,2432]{2,1,0:T(8,128)(2,1)S(1)}, bf16[8,24,2432]{2,1,0:T(8,128)(2,1)S(1)}, u32[]{:S(2)}, u32[]{:S(2)}) collective-permute-start(bf16[8,24,2432]{2,1,0:T(8,128)(2,1)S(1)} %bitcast.48), channel_id=1, source_target_pairs={{0,4},{1,3},{2,6},{3,1},{4,0},{5,7},{6,2},{7,5},{8,12},{9,11},{10,... | collective-permute-start | bytes 2801672 | tf_op jit(solution)/shard_map/ppermute | solution.py:91
  47.2 16.6 %collective-permute-start.11 = (bf16[4,24,3840]{2,1,0:T(8,128)(2,1)S(1)}, bf16[4,24,3840]{2,1,0:T(8,128)(2,1)S(1)}, u32[]{:S(2)}, u32[]{:S(2)}) collective-permute-start(bf16[4,24,3840]{2,1,0:T(8,128)(2,1)S(1)} %bitcast.58), channel_id=1, source_target_pairs={{0,2},{1,5},{2,0},{3,7},{4,6},{5,1},{6,4},{7,3},{8,10},{9,13},{10,... | collective-permute-start | bytes 2211848 | tf_op jit(solution)/shard_map/ppermute | solution.py:91
  49.3 15.6 %collective-permute-start.10 = (bf16[2,96,768]{2,1,0:T(8,128)(2,1)S(1)}, bf16[2,96,768]{2,1,0:T(8,128)(2,1)S(1)}, u32[]{:S(2)}, u32[]{:S(2)}) collective-permute-start(bf16[2,96,768]{2,1,0:T(8,128)(2,1)S(1)} %bitcast.60), channel_id=1, source_target_pairs={{0,8},{1,9},{2,10},{3,11},{4,12},{5,13},{6,14},{7,15},{8,0},{9,1},... | collective-permute-start | bytes 884744 | tf_op jit(solution)/shard_map/ppermute | solution.py:91
  63.7 4.8 %copy-start.5 = (bf16[2,8,24,2432]{3,2,1,0:T(8,128)(2,1)}, bf16[2,8,24,2432]{3,2,1,0:T(8,128)(2,1)S(1)}, u32[]{:S(2)}) copy-start(bf16[2,8,24,2432]{3,2,1,0:T(8,128)(2,1)S(1)} %pair.20.refs_2_) | copy-start | bytes 5603332
  63.8 4.8 %collective-permute-start.9 = (bf16[4,4,24,2432]{3,2,1,0:T(8,128)(2,1)S(1)}, bf16[4,4,24,2432]{3,2,1,0:T(8,128)(2,1)S(1)}, u32[]{:S(2)}, u32[]{:S(2)}) collective-permute-start(bf16[4,4,24,2432]{3,2,1,0:T(8,128)(2,1)S(1)} %bitcast.43), channel_id=1, source_target_pairs={{0,1},{1,0},{2,3},{3,2},{4,5},{5,4},{6,7},{7,6},{8,9},{9,8},{10,11... | collective-permute-start | bytes 5603336 | tf_op jit(solution)/shard_map/ppermute | solution.py:91
  64.5 25.7 %collective-permute-start.12 = (bf16[8,24,3840]{2,1,0:T(8,128)(2,1)S(1)}, bf16[8,24,3840]{2,1,0:T(8,128)(2,1)S(1)}, u32[]{:S(2)}, u32[]{:S(2)}) collective-permute-start(bf16[8,24,3840]{2,1,0:T(8,128)(2,1)S(1)} %bitcast.46), channel_id=1, source_target_pairs={{0,4},{1,3},{2,6},{3,1},{4,0},{5,7},{6,2},{7,5},{8,12},{9,11},{10,... | collective-permute-start | bytes 4423688 | tf_op jit(solution)/shard_map/ppermute | solution.py:91
  65.6 17.3 %collective-permute-start.13 = (bf16[4,96,768]{2,1,0:T(8,128)(2,1)S(1)}, bf16[4,96,768]{2,1,0:T(8,128)(2,1)S(1)}, u32[]{:S(2)}, u32[]{:S(2)}) collective-permute-start(bf16[4,96,768]{2,1,0:T(8,128)(2,1)S(1)} %bitcast.50), channel_id=1, source_target_pairs={{0,2},{1,5},{2,0},{3,7},{4,6},{5,1},{6,4},{7,3},{8,10},{9,13},{10,... | collective-permute-start | bytes 1769480 | tf_op jit(solution)/shard_map/ppermute | solution.py:91
  68.6 13.6 %copy-start.7 = (bf16[4,4,24,2432]{3,2,1,0:T(8,128)(2,1)}, bf16[4,4,24,2432]{3,2,1,0:T(8,128)(2,1)S(1)}, u32[]{:S(2)}) copy-start(bf16[4,4,24,2432]{3,2,1,0:T(8,128)(2,1)S(1)} %collective-permute-done.9.other.refs_3_) | copy-start | bytes 5603332
  82.1 10.6 %copy-start.3 = (bf16[416,768]{1,0:T(8,128)(2,1)}, bf16[416,768]{1,0:T(8,128)(2,1)S(1)}, u32[]{:S(2)}) copy-start(bf16[416,768]{1,0:T(8,128)(2,1)S(1)} %get-tuple-element.65.refs_2_.normed) | copy-start | bytes 1916932
  82.2 10.5 %copy-start.32 = (bf16[416,768]{1,0:T(8,128)(2,1)}, bf16[416,768]{1,0:T(8,128)(2,1)S(1)}, u32[]{:S(2)}) copy-start(bf16[416,768]{1,0:T(8,128)(2,1)S(1)} %get-tuple-element.64.attended) | copy-start | bytes 1916932
  82.2 10.5 %copy-start.37 = (bf16[416,2304]{1,0:T(8,128)(2,1)}, bf16[416,2304]{1,0:T(8,128)(2,1)S(1)}, u32[]{:S(2)}) copy-start(bf16[416,2304]{1,0:T(8,128)(2,1)S(1)} %get-tuple-element.76.qkv) | copy-start | bytes 5750788
  82.2 10.5 %copy-start.39 = (f32[416,128]{1,0:T(8,128)}, f32[416,128]{1,0:T(8,128)S(1)}, u32[]{:S(2)}) copy-start(f32[416,128]{1,0:T(8,128)S(1)} %get-tuple-element.78.lse) | copy-start | bytes 638980
  82.2 16.3 %copy-start.14 = (f32[16,768]{1,0:T(8,128)}, f32[16,768]{1,0:T(8,128)S(1)}, u32[]{:S(2)}) copy-start(f32[16,768]{1,0:T(8,128)S(1)} %get-tuple-element.66.vec.refs_4_) | copy-start | bytes 147460
  92.7 5.8 %collective-permute-start.14 = (bf16[4,4,24,3840]{3,2,1,0:T(8,128)(2,1)}, bf16[4,4,24,3840]{3,2,1,0:T(8,128)(2,1)}, u32[]{:S(2)}, u32[]{:S(2)}) collective-permute-start(bf16[4,4,24,3840]{3,2,1,0:T(8,128)(2,1)} %bitcast.16.held), channel_id=1, source_target_pairs={{0,1},{1,0},{2,3},{3,2},{4,5},{5,4},{6,7},{7,6},{8,9},{9,8},{10,11... | collective-permute-start | bytes 8847368 | tf_op jit(solution)/shard_map/ppermute | solution.py:91
  93.1 20.9 %collective-permute-start.15 = (bf16[8,96,768]{2,1,0:T(8,128)(2,1)S(1)}, bf16[8,96,768]{2,1,0:T(8,128)(2,1)S(1)}, u32[]{:S(2)}, u32[]{:S(2)}) collective-permute-start(bf16[8,96,768]{2,1,0:T(8,128)(2,1)S(1)} %bitcast.39), channel_id=1, source_target_pairs={{0,4},{1,3},{2,6},{3,1},{4,0},{5,7},{6,2},{7,5},{8,12},{9,11},{10,... | collective-permute-start | bytes 3538952 | tf_op jit(solution)/shard_map/ppermute | solution.py:91
  113.8 4.5 %collective-permute-start.17 = (bf16[4,4,96,768]{3,2,1,0:T(8,128)(2,1)S(1)}, bf16[4,4,96,768]{3,2,1,0:T(8,128)(2,1)S(1)}, u32[]{:S(2)}, u32[]{:S(2)}) collective-permute-start(bf16[4,4,96,768]{3,2,1,0:T(8,128)(2,1)S(1)} %get-tuple-element.72), channel_id=1, source_target_pairs={{0,1},{1,0},{2,3},{3,2},{4,5},{5,4},{6,7},{7,6},{8,9},{9,8},{10,11... | collective-permute-start | bytes 7077896 | tf_op jit(solution)/shard_map/ppermute | solution.py:91
  115.2 6.5 %collective-permute-start.16 = (bf16[4,4,96,768]{3,2,1,0:T(8,128)(2,1)S(1)}, bf16[4,4,96,768]{3,2,1,0:T(8,128)(2,1)S(1)}, u32[]{:S(2)}, u32[]{:S(2)}) collective-permute-start(bf16[4,4,96,768]{3,2,1,0:T(8,128)(2,1)S(1)} %bitcast.41), channel_id=1, source_target_pairs={{0,1},{1,0},{2,3},{3,2},{4,5},{5,4},{6,7},{7,6},{8,9},{9,8},{10,11... | collective-permute-start | bytes 7077896 | tf_op jit(solution)/shard_map/ppermute | solution.py:91
  120.7 24.5 %collective-permute-start.18 = (bf16[8,96,768]{2,1,0:T(8,128)(2,1)}, bf16[8,96,768]{2,1,0:T(8,128)(2,1)S(1)}, u32[]{:S(2)}, u32[]{:S(2)}) collective-permute-start(bf16[8,96,768]{2,1,0:T(8,128)(2,1)} %get-tuple-element.79), channel_id=1, source_target_pairs={{0,4},{1,3},{2,6},{3,1},{4,0},{5,7},{6,2},{7,5},{8,12},{9,11},{10,... | collective-permute-start | bytes 3538952 | tf_op jit(solution)/shard_map/ppermute | solution.py:91
  141.4 13.6 %collective-permute-start.19 = (bf16[4,4,24,3840]{3,2,1,0:T(8,128)(2,1)}, bf16[4,4,24,3840]{3,2,1,0:T(8,128)(2,1)}, u32[]{:S(2)}, u32[]{:S(2)}) collective-permute-start(bf16[4,4,24,3840]{3,2,1,0:T(8,128)(2,1)} %get-tuple-element.82), channel_id=1, source_target_pairs={{0,1},{1,0},{2,3},{3,2},{4,5},{5,4},{6,7},{7,6},{8,9},{9,8},{10,11... | collective-permute-start | bytes 8847368 | tf_op jit(solution)/shard_map/ppermute | solution.py:91
  147.4 18.1 %collective-permute-start.20 = (bf16[4,96,768]{2,1,0:T(8,128)(2,1)S(1)}, bf16[4,96,768]{2,1,0:T(8,128)(2,1)S(1)}, u32[]{:S(2)}, u32[]{:S(2)}) collective-permute-start(bf16[4,96,768]{2,1,0:T(8,128)(2,1)S(1)} %get-tuple-element.86), channel_id=1, source_target_pairs={{0,2},{1,5},{2,0},{3,7},{4,6},{5,1},{6,4},{7,3},{8,10},{9,13},{10,... | collective-permute-start | bytes 1769480 | tf_op jit(solution)/shard_map/ppermute | solution.py:91
  149.3 5.8 %copy-start.29 = (bf16[4,4,24,3840]{3,2,1,0:T(8,128)(2,1)S(1)}, bf16[4,4,24,3840]{3,2,1,0:T(8,128)(2,1)}, u32[]{:S(2)}) copy-start(bf16[4,4,24,3840]{3,2,1,0:T(8,128)(2,1)} %get-tuple-element.81) | copy-start | bytes 8847364
  158.5 19.4 %collective-permute-start.23 = (bf16[8,24,3840]{2,1,0:T(8,128)(2,1)S(1)}, bf16[8,24,3840]{2,1,0:T(8,128)(2,1)S(1)}, u32[]{:S(2)}, u32[]{:S(2)}) collective-permute-start(bf16[8,24,3840]{2,1,0:T(8,128)(2,1)S(1)} %get-tuple-element.92), channel_id=1, source_target_pairs={{0,4},{1,3},{2,6},{3,1},{4,0},{5,7},{6,2},{7,5},{8,12},{9,11},{10,... | collective-permute-start | bytes 4423688 | tf_op jit(solution)/shard_map/ppermute | solution.py:91
  159.6 6.8 %copy-start.8 = (bf16[4,4,24,2432]{3,2,1,0:T(8,128)(2,1)S(1)}, bf16[4,4,24,2432]{3,2,1,0:T(8,128)(2,1)}, u32[]{:S(2)}) copy-start(bf16[4,4,24,2432]{3,2,1,0:T(8,128)(2,1)} %copy-done.7) | copy-start | bytes 5603332
  166.2 13.5 %collective-permute-start.22 = (bf16[2,96,768]{2,1,0:T(8,128)(2,1)S(1)}, bf16[2,96,768]{2,1,0:T(8,128)(2,1)S(1)}, u32[]{:S(2)}, u32[]{:S(2)}) collective-permute-start(bf16[2,96,768]{2,1,0:T(8,128)(2,1)S(1)} %get-tuple-element.91), channel_id=1, source_target_pairs={{0,8},{1,9},{2,10},{3,11},{4,12},{5,13},{6,14},{7,15},{8,0},{9,1},... | collective-permute-start | bytes 884744 | tf_op jit(solution)/shard_map/ppermute | solution.py:91
  173.6 6.7 %collective-permute-start.21 = (bf16[4,4,24,2432]{3,2,1,0:T(8,128)(2,1)S(1)}, bf16[4,4,24,2432]{3,2,1,0:T(8,128)(2,1)S(1)}, u32[]{:S(2)}, u32[]{:S(2)}) collective-permute-start(bf16[4,4,24,2432]{3,2,1,0:T(8,128)(2,1)S(1)} %get-tuple-element.90), channel_id=1, source_target_pairs={{0,1},{1,0},{2,3},{3,2},{4,5},{5,4},{6,7},{7,6},{8,9},{9,8},{10,11... | collective-permute-start | bytes 5603336 | tf_op jit(solution)/shard_map/ppermute | solution.py:91
  178.8 19.1 %collective-permute-start.25 = (bf16[4,24,3840]{2,1,0:T(8,128)(2,1)S(1)}, bf16[4,24,3840]{2,1,0:T(8,128)(2,1)S(1)}, u32[]{:S(2)}, u32[]{:S(2)}) collective-permute-start(bf16[4,24,3840]{2,1,0:T(8,128)(2,1)S(1)} %get-tuple-element.97), channel_id=1, source_target_pairs={{0,2},{1,5},{2,0},{3,7},{4,6},{5,1},{6,4},{7,3},{8,10},{9,13},{10,... | collective-permute-start | bytes 2211848 | tf_op jit(solution)/shard_map/ppermute | solution.py:91
  181.4 17.6 %collective-permute-start.24 = (bf16[8,24,2432]{2,1,0:T(8,128)(2,1)S(1)}, bf16[8,24,2432]{2,1,0:T(8,128)(2,1)S(1)}, u32[]{:S(2)}, u32[]{:S(2)}) collective-permute-start(bf16[8,24,2432]{2,1,0:T(8,128)(2,1)S(1)} %get-tuple-element.96), channel_id=1, source_target_pairs={{0,4},{1,3},{2,6},{3,1},{4,0},{5,7},{6,2},{7,5},{8,12},{9,11},{10,... | collective-permute-start | bytes 2801672 | tf_op jit(solution)/shard_map/ppermute | solution.py:91
  198.7 9.1 %collective-permute-start.27 = (bf16[2,24,3840]{2,1,0:T(8,128)(2,1)S(1)}, bf16[2,24,3840]{2,1,0:T(8,128)(2,1)S(1)}, u32[]{:S(2)}, u32[]{:S(2)}) collective-permute-start(bf16[2,24,3840]{2,1,0:T(8,128)(2,1)S(1)} %get-tuple-element.101), channel_id=1, source_target_pairs={{0,8},{1,9},{2,10},{3,11},{4,12},{5,13},{6,14},{7,15},{8,0},{9,1},... | collective-permute-start | bytes 1105928 | tf_op jit(solution)/shard_map/ppermute | solution.py:91
  199.8 8.7 %collective-permute-start.26 = (bf16[4,24,2432]{2,1,0:T(8,128)(2,1)S(1)}, bf16[4,24,2432]{2,1,0:T(8,128)(2,1)S(1)}, u32[]{:S(2)}, u32[]{:S(2)}) collective-permute-start(bf16[4,24,2432]{2,1,0:T(8,128)(2,1)S(1)} %get-tuple-element.100), channel_id=1, source_target_pairs={{0,2},{1,5},{2,0},{3,7},{4,6},{5,1},{6,4},{7,3},{8,10},{9,13},{10,... | collective-permute-start | bytes 1400840 | tf_op jit(solution)/shard_map/ppermute | solution.py:91
  200.8 10.6 %collective-permute-start.31 = (bf16[1,96,768]{2,1,0:T(8,128)(2,1)S(1)}, bf16[1,96,768]{2,1,0:T(8,128)(2,1)S(1)}, u32[]{:S(2)}, u32[]{:S(2)}) collective-permute-start(bf16[1,96,768]{2,1,0:T(8,128)(2,1)S(1)} %get-tuple-element.108), channel_id=1, source_target_pairs={{0,16},{1,17},{2,18},{3,19},{4,20},{5,21},{6,22},{7,23},{8,24},{9,... | collective-permute-start | bytes 442376 | tf_op jit(solution)/shard_map/ppermute | solution.py:91
  209.2 9.8 %collective-permute-start.28 = (bf16[2,24,2432]{2,1,0:T(8,128)(2,1)S(1)}, bf16[2,24,2432]{2,1,0:T(8,128)(2,1)S(1)}, u32[]{:S(2)}, u32[]{:S(2)}) collective-permute-start(bf16[2,24,2432]{2,1,0:T(8,128)(2,1)S(1)} %get-tuple-element.104), channel_id=1, source_target_pairs={{0,8},{1,9},{2,10},{3,11},{4,12},{5,13},{6,14},{7,15},{8,0},{9,1},... | collective-permute-start | bytes 700424 | tf_op jit(solution)/shard_map/ppermute | solution.py:91
  212.2 14.6 %collective-permute-start.30 = (bf16[1,24,3840]{2,1,0:T(8,128)(2,1)S(1)}, bf16[1,24,3840]{2,1,0:T(8,128)(2,1)S(1)}, u32[]{:S(2)}, u32[]{:S(2)}) collective-permute-start(bf16[1,24,3840]{2,1,0:T(8,128)(2,1)S(1)} %get-tuple-element.107), channel_id=1, source_target_pairs={{0,16},{1,17},{2,18},{3,19},{4,20},{5,21},{6,22},{7,23},{8,24},{9,... | collective-permute-start | bytes 552968 | tf_op jit(solution)/shard_map/ppermute | solution.py:91
  219.6 9.0 %collective-permute-start.29 = (bf16[1,24,2432]{2,1,0:T(8,128)(2,1)S(1)}, bf16[1,24,2432]{2,1,0:T(8,128)(2,1)S(1)}, u32[]{:S(2)}, u32[]{:S(2)}) collective-permute-start(bf16[1,24,2432]{2,1,0:T(8,128)(2,1)S(1)} %get-tuple-element.106), channel_id=1, source_target_pairs={{0,16},{1,17},{2,18},{3,19},{4,20},{5,21},{6,22},{7,23},{8,24},{9,... | collective-permute-start | bytes 350216 | tf_op jit(solution)/shard_map/ppermute | solution.py:91
  (25 other events, 46.0 us)
where the time goes:
time: 232 us; the launch traced here: 231 us
  Pallas kernels  89 us (38%)
  waiting for transfers between devices  83.4 us (36%)
  starting transfers between devices  36.7 us (16%)
  local copies, waits for them, and re-layouts  19.8 us (9%)
    ppermute x32, waiting for transfers between devices, swap(): return lax.ppermute(value, 'dp', pairs)  83.4 us
    ppermute x32, starting transfers between devices, swap(): return lax.ppermute(value, 'dp', pairs)  36.7 us
    pallas_call x1, Pallas kernels, shards(): pl.pallas_call(functools.partial(down_kernel, slots, plane_slots, rows, f...  17.2 us
    pallas_call x1, Pallas kernels, shards(): pl.pallas_call(functools.partial(attend_kernel, slots, rows), out_shape=(...  13.5 us
    pallas_call x12, Pallas kernels, kernel(): pl.pallas_call(body, grid_spec=pltpu.PrefetchScalarGridSpec(num_scalar_pr...  13.3 us
    unnamed x82, local copies, waits for them, and re-layouts  12.7 us
    pallas_call x2, Pallas kernels, heads(): pl.pallas_call(heads_kernel, grid=(1,), out_shape=shape((SLOT, 3 * D), BF...  11.6 us
    pallas_call x13, Pallas kernels, kernel(): pl.pallas_call(body, out_shape=jax.ShapeDtypeStruct((2, count, rows, sum(...  11 us
  transfers between devices with their start and end apart: 32, of which 18 were waited for; matrix products, arithmetic and copies ran while one was open for 2% of the time, Pallas kernels for 37%

commit v1 on v0

v1 whole, which is shorter than its diff:
```python
import functools

import jax
import jax.numpy as jnp
from jax import lax
from jax.experimental import pallas as pl
from jax.experimental.pallas import tpu as pltpu
from jax.sharding import PartitionSpec as P

D = 768
HEADS = 12
HEAD_DIM = 64
FF = 3072
LEN = 197
SLOT = 208
SPEED = 1.15e9
LENGTHS = (12, 0.25, 0.25, 1, 1, 0.5, 12, 1, 0.25, 24, 0.25, 0.25, 16, 6, 16, 0.25, 16, 3, 0.5, 0.25, 16, 6, 3, 2, 8, 0.5, 6, 2, 2, 6, 1, 1, 24, 0.5, 0.25, 1, 3, 32, 0.25, 0.25, 2, 0.5, 0.5, 0.25)
ORDERS = {'a': 'fnxx', 'b': 'nxfx', 'e': 'fxnx', 'c': 'fxxn', 'd': 'xxnf', 'u': 'xxnf', 'i': 'xxnf', 'j': 'xxfn'}
GATHERS = ("a", "b", "e", "c")
FIRST = 2
PINNED = {}
SCALE = HEAD_DIM ** (-0.5)
F32 = jnp.float32
BF16 = jnp.bfloat16
VMEM = pl.BlockSpec(memory_space=pltpu.VMEM)
SMEM = pl.BlockSpec(memory_space=pltpu.SMEM)
ANY = pl.BlockSpec(memory_space=pl.ANY)
TOKEN = pltpu.HBM((8, 128), F32)


def params(megabytes):
    return pltpu.CompilerParams(
        vmem_limit_bytes=megabytes << 20, dimension_semantics=("arbitrary",)
    )


def cost(length):
    return pl.CostEstimate(flops=int(length * SPEED), transcendentals=0, bytes_accessed=D)


def mul(a, b):
    return jnp.dot(a, b, preferred_element_type=F32)


def mul_t(a, b):
    return lax.dot_general(a, b, (((1,), (1,)), ((), ())), preferred_element_type=F32)


def t_mul(a, b):
    return lax.dot_general(a, b, (((0,), (0,)), ((), ())), preferred_element_type=F32)


class Links:
    def __init__(self, count):
        chips = count // 2
        z = min(4, chips)
        plane = chips // z
        x = 1
        while x * x < plane:
            x *= 2
        self.count, self.z, self.plane = count, z, plane
        bit = 2
        x_bits, y_bits, z_bits = [], [], []
        for bits, extent in ((x_bits, x), (y_bits, plane // x), (z_bits, z)):
            size = 1
            while size < extent:
                bits.append(bit)
                bit *= 2
                size *= 2
        across = list(zip(x_bits + y_bits, y_bits + x_bits))
        half = (len(across) + 1) // 2
        self.near = [(b, b) for b in z_bits[:1]]
        self.far = [(b, b) for b in z_bits[1:]]
        self.across = across[:half], across[half:]
        self.all = self.near + self.far + across
        index = lax.axis_index("dp")
        core = index % 2
        sides = [((index & jnp.where(core == 0, *step)) != 0).astype(jnp.int32) for step in self.all]
        self.place = jnp.stack([core.astype(jnp.int32)] + sides)
        self.last = None
        self.lengths = iter(LENGTHS + (1,) * 64)

    def length(self):
        return next(self.lengths)

    def hops(self, order):
        found, crossed = [], 0
        for kind in order:
            if kind == "x":
                found.append(self.across[crossed])
                crossed += 1
            else:
                found.append(self.far if kind == "f" else self.near)
        return found

    def steps(self, order, scatter):
        steps = [step for hop in self.hops(order) for step in hop]
        return steps[::-1] if scatter else steps

    def slots(self, order, scatter):
        steps = self.steps(order, scatter)
        found = []
        for device in range(self.count):
            bits = [1 if device & step[device % 2] else 0 for step in steps]
            found.append((device % 2, sum(b << weight for weight, b in enumerate(bits))))
        return tuple(found)

    def tiles(self, order, scatter):
        steps = self.steps(order, scatter)[::-1]
        along = [step in self.near or step in self.far for step in steps]
        block = tuple(1 if z else 2 for z in along)

        def index(t):
            return tuple((t % 2 if step in self.near else t // 2) if z else 0 for step, z in zip(steps, along))

        found = []
        for device in range(self.count // self.z):
            found.append((device % 2, tuple(1 if device & step[device % 2] else 0 for step in steps)))
        return (2,) * len(steps), block, index, tuple(found)

    def run(self, kernel, *args, **options):
        *out, self.last = kernel(self.last, *args, **options)
        return tuple(out)

    def swap(self, value, even, odd):
        pairs = [(i, i ^ (odd if i % 2 else even)) for i in range(self.count)]
        return lax.ppermute(value, "dp", pairs)

    def pair(self, step, held, other):
        count, rows, width = held.shape
        at = self.all.index(step)

        def body(place, held, other, *refs):
            out = refs[-2]
            high = place[1 + at]

            def copy(i, carry):
                out[high, i] = held[i]
                out[1 - high, i] = other[i]
                return carry

            lax.fori_loop(0, count, copy, 0)

        def kernel(last):
            return pl.pallas_call(
                body,
                out_shape=(jax.ShapeDtypeStruct((2, count, rows, width), BF16), TOKEN),
                in_specs=[SMEM, VMEM, VMEM] + ([] if last is None else [ANY]),
                out_specs=(VMEM, ANY),
                compiler_params=pltpu.CompilerParams(vmem_limit_bytes=10 << 20),
                cost_estimate=cost(self.length()),
                name="pair",
            )(self.place, held, other, *([] if last is None else [pinned(last)]))

        return self.run(kernel)[0].reshape(2 * count, rows, width)

    def advance(self, held, hop):
        for step in hop:
            held = self.pair(step, held, self.swap(held, *step))
        return held

    def exchange(self, kept, sent):
        other = self.swap(sent, 1, 1)
        shape = (-1,) + kept.shape[-2:]
        return kept.reshape(shape), other.reshape(shape)

    def halve(self, step, kept, other):
        at = self.all.index(step)
        half = kept.shape[0] // 2
        chunk = max(1, half // 4)
        grid = half // chunk
        block = (chunk,) + kept.shape[1:]
        upper = pl.BlockSpec(block, lambda i, place: (place[1 + at] * grid + i, 0, 0))
        lower = pl.BlockSpec(block, lambda i, place: ((1 - place[1 + at]) * grid + i, 0, 0))
        straight = pl.BlockSpec(block, lambda i, place: (i, 0, 0))

        def body(place, kept_up, kept_low, other_up, other_low, last, stay, leave, token):
            stay[...] = kept_up[...].astype(F32) + other_up[...].astype(F32)
            leave[...] = (kept_low[...].astype(F32) + other_low[...].astype(F32)).astype(BF16)

        def kernel(last):
            return pl.pallas_call(
                body,
                grid_spec=pltpu.PrefetchScalarGridSpec(
                    num_scalar_prefetch=1,
                    grid=(grid,),
                    in_specs=[upper, lower, upper, lower, ANY],
                    out_specs=(straight, straight, ANY),
                ),
                out_shape=(
                    jax.ShapeDtypeStruct((half,) + kept.shape[1:], F32),
                    jax.ShapeDtypeStruct((half,) + kept.shape[1:], BF16),
                    TOKEN,
                ),
                compiler_params=params(12),
                cost_estimate=cost(self.length()),
                name="halve",
            )(self.place, kept, kept, other, other, pinned(last))

        return self.run(kernel)

    def reduce(self, parts, hop):
        for step in hop:
            kept, low = self.halve(step, *parts)
            parts = kept, self.swap(low, *step)
        return parts


def pinned(value):
    return pltpu.with_memory_space_constraint(value, pltpu.HBM)


def settle(parts):
    return parts[0][0].astype(F32) + parts[1][0].astype(F32)


def collect(into, rows, slots, core, held, other, cols=slice(None)):
    @pl.when(core == 0)
    def _():
        for place, (parity, piece) in enumerate(slots):
            source = other if parity else held
            into[place * rows : (place + 1) * rows, :] = source[piece + (slice(None), cols)]

    @pl.when(core == 1)
    def _():
        for place, (parity, piece) in enumerate(slots):
            source = held if parity else other
            into[place * rows : (place + 1) * rows, :] = source[piece + (slice(None), cols)]


def deal(values, rows, slots, core, kept, sent, cols=slice(None)):
    halves = ({}, {})
    for place, (parity, piece) in enumerate(slots):
        halves[parity][piece] = values[place * rows : (place + 1) * rows, :]
    for piece, even in halves[0].items():
        odd = halves[1][piece]
        kept[piece + (slice(None), cols)] = jnp.where(core == 0, even, odd)
        sent[piece + (slice(None), cols)] = jnp.where(core == 0, odd, even)


def standard(values):
    centred = values - jnp.mean(values, axis=-1, keepdims=True)
    rate = lax.rsqrt(jnp.mean(centred * centred, axis=-1, keepdims=True) + 1e-06)
    return centred * rate, rate


def standard_back(grad, gain, standardised, rate):
    pushed = grad * gain
    along = jnp.mean(pushed * standardised, axis=-1, keepdims=True)
    inner = pushed - jnp.mean(pushed, axis=-1, keepdims=True) - standardised * along
    sums = (jnp.sum(grad * standardised, axis=0, keepdims=True), jnp.sum(grad, axis=0, keepdims=True))
    return (rate * inner,) + sums


def first_half(width):
    return lax.broadcasted_iota(jnp.int32, (SLOT, 2 * HEAD_DIM), 1) < HEAD_DIM


def line_up_kernel(weight, *refs):
    lines, bias, out = refs[:8], refs[8], refs[-1]
    rows = weight.shape[0]
    out[0, :, : 3 * D] = weight[...]
    lines = [line[...].astype(F32).reshape(1, rows) for line in lines]
    bias = bias[...].astype(F32).reshape(1, -1)
    lines += [bias[:, at : at + rows] for at in range(0, bias.shape[1], rows)]
    lines.append(jnp.zeros((128 - len(lines), rows), F32))
    out[0, :, 3 * D :] = jnp.concatenate(lines, axis=0).T.astype(BF16)


def spread_kernel(images, live, block_in, cotangent, earlier, x_ref, dm_ref):
    for ref, into in ((block_in, x_ref), (cotangent, dm_ref)):
        values = ref[...].astype(F32)
        for image in range(images):
            part = values[image * LEN : (image + 1) * LEN]
            if into is dm_ref:
                part = jnp.where(live[image * LEN] != 0, part, 0.0)
            part = jnp.concatenate([part, jnp.zeros((SLOT - LEN, D), F32)], axis=0)
            into[image * SLOT : (image + 1) * SLOT, :] = part.astype(BF16)


def trim(values):
    parts = [values[at : at + LEN] for at in range(0, values.shape[0], SLOT)]
    return jnp.concatenate(parts, axis=0)


def join_kernel(ranges, *refs):
    out = refs[-1]
    start = 0
    for part, (first, last) in zip(refs, ranges):
        out[0, :, start : start + last - first] = part[:, first:last]
        start += last - first


def attend_kernel(slots, rows, place, x_ref, held, other, earlier, normed, qkv, attended, lse, vec, weight, columns):
    core = place[0]
    collect(weight, rows, slots, core, held, other, slice(0, 3 * D))
    collect(columns, rows, slots, core, held, other, slice(3 * D, 3 * D + 128))
    vec[...] = columns[...].astype(F32).T[: vec.shape[0], :]
    shaped, _ = standard(x_ref[...].astype(F32))
    low = (shaped * vec[0:1, :] + vec[1:2, :]).astype(BF16)
    normed[...] = low
    for part, row in ((0, 2), (1, None), (2, 3)):
        cols = pl.ds(part * D, D)
        packed = mul(low, weight[:, cols])
        if row is not None:
            packed = packed + vec[row : row + 1, :]
        qkv[:, cols] = packed.astype(BF16)
    left = first_half(0)
    real = lax.broadcasted_iota(jnp.int32, (SLOT, SLOT), 1) < LEN
    lane = lax.broadcasted_iota(jnp.int32, (SLOT, 128), 1)
    images = x_ref.shape[0] // SLOT
    lse[...] = jnp.zeros_like(lse)

    def pair_step(at, carry):
        image, pair = at // (HEADS // 2), at % (HEADS // 2)
        tokens = pl.ds(pl.multiple_of(image * SLOT, 16), SLOT)
        cols = lambda part: pl.ds(pl.multiple_of(part * D + pair * 128, 128), 128)
        query, key, value = qkv[tokens, cols(0)], qkv[tokens, cols(1)], qkv[tokens, cols(2)]
        mixed, logs = [], lse[tokens, :]
        for side in range(2):
            chosen = left if side == 0 else ~left
            scores = mul_t(jnp.where(chosen, query, jnp.zeros_like(query)), key) * SCALE
            scores = jnp.where(real, scores, -1e30)
            top = jnp.max(scores, axis=-1, keepdims=True)
            raised = jnp.exp(scores - top)
            total = jnp.sum(raised, axis=-1, keepdims=True)
            logs = jnp.where(lane == pair * 2 + side, top + jnp.log(total), logs)
            mixed.append(mul((raised * (1.0 / total)).astype(BF16), value))
        lse[tokens, :] = logs
        attended[tokens, cols(0)] = jnp.where(left, mixed[0], mixed[1]).astype(BF16)
        return carry

    lax.fori_loop(0, images * (HEADS // 2), pair_step, 0, unroll=HEADS // 2)


def up_kernel(slots_b, slots_e, slots_d, rows, ff_rows, place, x_ref, attended, dm, held, other, held_e, other_e, vec, ubias, earlier, middle, normed, active, slope, kept, sent, weight):
    core = place[0]
    step = pl.program_id(0)

    @pl.when(step <= FIRST)
    def _():
        collect(weight, rows, slots_b, core, held, other)

    @pl.when(step > FIRST)
    def _():
        collect(weight, rows, slots_e, core, held_e, other_e)

    @pl.when(step == 0)
    def _():
        total = x_ref[...].astype(F32) + mul(attended[...], weight[...]) + vec[4:5, :]
        middle[...] = total
        shaped, _ = standard(total)
        normed[...] = (shaped * vec[5:6, :] + vec[6:7, :]).astype(BF16)

    @pl.when(step > 0)
    def _():
        pre = mul(normed[...], weight[...]) + ubias[0:1, :]
        share = 0.5 + 0.5 * lax.erf(pre * (0.5**0.5))
        low = (pre * share).astype(BF16)
        active[...] = low
        slope[...] = share + pre * (jnp.exp(pre * pre * -0.5) * 0.3989422804014327)
        grad = t_mul(low, dm[...]).astype(BF16)

        deal(grad, ff_rows, slots_d, core, kept, sent)


def slope_kernel(slots_u, slots_c, rows, ff_rows, place, dm, normed, slope, held, other, earlier, low, kept, sent, sums, weight):
    core = place[0]
    collect(weight, ff_rows, slots_c, core, held, other)
    grad = (mul_t(dm[...], weight[...]) * slope[...]).astype(BF16)
    low[...] = grad
    deal(t_mul(normed[...], grad).astype(BF16), rows, slots_u, core, kept, sent)
    lines = jnp.broadcast_to(jnp.sum(grad.astype(F32), axis=0, keepdims=True), (128, grad.shape[1])).T
    lane = lax.broadcasted_iota(jnp.int32, (rows, 128), 1)
    for device in range(grad.shape[1] // ff_rows):
        total = jnp.zeros((rows, 128), F32)
        for at in range(ff_rows // rows):
            start = device * ff_rows + at * rows
            total = jnp.where(lane == 8 + at, lines[start : start + rows, :], total)
        sums[device * rows : (device + 1) * rows, :] = total


def middle_kernel(slots_b, slots_e, slots_i, rows, place, low, middle, dm, attended, held, other, held_e, other_e, vec, earlier, datt, dmid, kept, sent, sums, weight, back):
    core = place[0]
    step = pl.program_id(0)
    last = pl.num_programs(0) - 1

    @pl.when((step < FIRST) | (step == last))
    def _():
        collect(weight, rows, slots_b, core, held, other)

    @pl.when((step >= FIRST) & (step < last))
    def _():
        collect(weight, rows, slots_e, core, held_e, other_e)

    @pl.when(step == 0)
    def _():
        back[...] = mul_t(low[...], weight[...])

    @pl.when((step > 0) & (step < last))
    def _():
        back[...] += mul_t(low[...], weight[...])

    @pl.when(step == last)
    def _():
        source = dm[...].astype(F32)
        shaped, rate = standard(middle[...])
        inner, ggain, gshift = standard_back(back[...], vec[5:6, :], shaped, rate)
        total = source + inner
        dmid[...] = total
        branch = total.astype(BF16)
        datt[...] = mul_t(branch, weight[...]).astype(BF16)
        deal(t_mul(attended[...], branch).astype(BF16), rows, slots_i, core, kept, sent)
        gout = jnp.sum(branch.astype(F32), axis=0, keepdims=True)
        gdown = jnp.sum(source, axis=0, keepdims=True)
        sums[...] = jnp.concatenate([gout, ggain, gshift, gdown] * 2, axis=0)


def down_kernel(slots_c, ff_rows, place, live, active, middle, held, other, vec, earlier, result, weight, mixed):
    core = place[0]
    step = pl.program_id(0)
    collect(weight, ff_rows, slots_c, core, held, other)
    more = mul(active[...], weight[...])

    @pl.when(step == 0)
    def _():
        mixed[...] = more

    @pl.when(step > 0)
    def _():
        mixed[...] += more

    @pl.when(step == pl.num_programs(0) - 1)
    def _():
        full = middle[...] + mixed[...] + vec[7:8, :]
        images = full.shape[0] // SLOT
        keep = [jnp.where(live[i * LEN] != 0, full[i * SLOT : i * SLOT + LEN], 0.0) for i in range(images)]
        result[...] = jnp.concatenate(keep, axis=0).astype(BF16)


def heads_kernel(slots, rows, first, beside, place, qkv, datt, lse, normed, *refs):
    more, (earlier, dqkv, kept, sent) = refs[:-4], refs[-4:]
    core = place[0]
    left = first_half(0)
    real = lax.broadcasted_iota(jnp.int32, (SLOT, SLOT), 1) < LEN
    lane = lax.broadcasted_iota(jnp.int32, (SLOT, 128), 1)
    pairs = HEADS // 4
    images = qkv.shape[0] // SLOT
    for source, into in zip(more, (kept, sent)):
        into[:, :, :beside] = source[...]

    def pair_step(at, carry):
        image, local = at // pairs, at % pairs
        pair = first + local
        tokens = pl.ds(pl.multiple_of(image * SLOT, 16), SLOT)
        cols = lambda part: pl.ds(pl.multiple_of(part * D + pair * 128, 128), 128)
        query, key, value = qkv[tokens, cols(0)], qkv[tokens, cols(1)], qkv[tokens, cols(2)]
        grad, logs = datt[tokens, cols(0)], lse[tokens, :]
        dq, dk, dv = [], [], []
        for side in range(2):
            chosen = left if side == 0 else ~left
            scores = mul_t(jnp.where(chosen, query, jnp.zeros_like(query)), key) * SCALE
            log = jnp.sum(jnp.where(lane == pair * 2 + side, logs, 0.0), axis=-1, keepdims=True)
            attn = jnp.where(real, jnp.exp(scores - log), 0.0)
            dattn = mul_t(jnp.where(chosen, grad, jnp.zeros_like(grad)), value)
            dscores = (attn * (dattn - jnp.sum(attn * dattn, axis=-1, keepdims=True))).astype(BF16)
            dv.append(t_mul(attn.astype(BF16), grad))
            dq.append(mul(dscores, key) * SCALE)
            dk.append(t_mul(dscores, query) * SCALE)
        for part, halves in ((0, dq), (1, dk), (2, dv)):
            into = pl.ds(pl.multiple_of(part * (D // 2) + local * 128, 128), 128)
            dqkv[tokens, into] = jnp.where(left, halves[0], halves[1]).astype(BF16)
        return carry

    lax.fori_loop(0, images * pairs, pair_step, 0, unroll=images * pairs)
    grad = t_mul(normed[...], dqkv[...]).astype(BF16)
    deal(grad, rows, slots, core, kept, sent, slice(beside, beside + 3 * D // 2))


def input_kernel(slots_a, slots_j, rows, place, x_ref, dmid, half_a, half_b, kept_b, sent_b, held, other, vec, sums, usums, earlier, kept, sent, igrad, weight):
    core = place[0]
    for source, into in ((kept_b, kept), (sent_b, sent)):
        into[:, :, : source.shape[2]] = source[...]
    collect(weight, rows, slots_a, core, held, other, slice(0, 3 * D))
    back = None
    rowsums = []
    for part in range(3):
        cols = pl.ds(part * (D // 2), D // 2)
        low = jnp.concatenate([half_a[:, cols], half_b[:, cols]], axis=1)
        rowsums.append(jnp.sum(low.astype(F32), axis=0, keepdims=True))
        more = mul_t(low, weight[:, pl.ds(part * D, D)])
        back = more if back is None else back + more
    shaped, rate = standard(x_ref[...].astype(F32))
    inner, ggain, gshift = standard_back(back, vec[0:1, :], shaped, rate)
    igrad[...] = trim(dmid[...] + inner)
    lines = [ggain, gshift, rowsums[0], rowsums[2], sums[0:4, :]]
    lines.append(jnp.zeros((128 - 8, D), F32))
    columns = (jnp.concatenate(lines, axis=0).T + usums[...]).astype(BF16)
    deal(columns, rows, slots_j, core, kept, sent, slice(kept_b.shape[2], kept_b.shape[2] + 128))


def zeroed(piece, part):
    return tuple(0 if extent == 1 else bit for bit, extent in zip(piece, part))


def shards(
    block_in,
    slot_mask,
    gain_first,
    shift_first,
    packed_weight,
    query_bias,
    value_bias,
    out_weight,
    out_bias,
    gain_second,
    shift_second,
    up_weight,
    up_bias,
    down_weight,
    down_bias,
    cotangent,
):
    links = Links(lax.axis_size("dp"))
    rows = packed_weight.shape[0]
    ff_rows = down_weight.shape[0]
    wide = ff_rows // rows
    count, depth = links.count, links.z
    number = count // 2
    place = links.place
    tokens = block_in.shape[0]
    images = tokens // LEN
    size = images * SLOT
    hops = {group: links.hops(order) for group, order in ORDERS.items()}
    slots = {group: links.slots(order, group not in GATHERS) for group, order in ORDERS.items()}
    flat = {group: tuple((parity, (piece,)) for parity, piece in found) for group, found in slots.items()}
    shape = jax.ShapeDtypeStruct
    pieces = lambda cols: shape((number, rows, cols), BF16)
    fixed = lambda height, width: pl.BlockSpec((height, width), lambda t: (0, 0))
    tile = FF // depth
    tiled = lambda height, at: pl.BlockSpec((height, tile), lambda t: (0, at(t)))
    whole = lambda cols: pl.BlockSpec((number, rows, cols), lambda t: (0, 0, 0))
    before = lambda t: jnp.maximum(t - 1, 0)
    upto = lambda t: jnp.minimum(t, depth - 1)
    same = lambda t: t
    view_c, part_c, at_c, slots_c = links.tiles(ORDERS["c"], False)
    view_d, part_d, at_d, slots_d = links.tiles(ORDERS["d"], True)
    slots_c, slots_d = (tuple((parity, zeroed(piece, part)) for parity, piece in found) for found, part in ((slots_c, part_c), (slots_d, part_d)))
    zeros = (0, 0)
    block_c = pl.BlockSpec(part_c + (ff_rows, D), lambda t: at_c(t) + zeros)

    def call(name, kernel, ins, specs, outs, out_specs, megabytes, grid=None, scratch=()):
        many = isinstance(outs, tuple)
        if specs is None:
            specs = [SMEM if v is place or v is slot_mask else VMEM for v in ins]
            out_specs = (VMEM,) * (len(outs) if many else 1)
        elif not many:
            out_specs = (out_specs,)
        outs = outs if many else (outs,)
        body = kernel
        token = len(ins) + (links.last is not None) + len(outs)

        def kernel(*refs):
            return body(*refs[:token], *refs[token + 1 :])

        far = {(size, FF)} if name not in PINNED else {(size, FF)} | PINNED[name](size)
        outs = tuple(pltpu.HBM(o.shape, o.dtype) if o.shape in far else o for o in outs)
        streamed = lambda v: v.shape in far or (v.ndim > 2 and name in ("up", "slope", "middle", "down"))
        ins = tuple(pinned(v) if streamed(v) else v for v in ins)
        if grid is not None:
            compiler = params(megabytes)
        else:
            compiler = pltpu.CompilerParams(vmem_limit_bytes=megabytes << 20)

        def launch(last):
            return pl.pallas_call(
                kernel,
                out_shape=outs + (TOKEN,),
                in_specs=list(specs) + ([] if last is None else [ANY]),
                out_specs=tuple(out_specs) + (ANY,),
                scratch_shapes=list(scratch),
                compiler_params=compiler,
                cost_estimate=cost(links.length()),
                name=name,
                **({} if grid is None else {"grid": grid}),
            )(*ins, *([] if last is None else [pinned(last)]))

        out = links.run(launch)
        return out if many else out[0]

    def joined(*parts):
        arrays = tuple(part[0] for part in parts)
        ranges = tuple((first, last) for _, first, last in parts)
        width = sum(last - first for first, last in ranges)
        out = shape((1, arrays[0].shape[0], width), BF16)
        return call("join", functools.partial(join_kernel, ranges), arrays, None, out, None, 8)

    split = FIRST * tile
    vectors = (gain_first, shift_first, query_bias, value_bias, out_bias, gain_second, shift_second, down_bias, up_bias)
    wide_a = 3 * D + 128
    gather_b = joined((out_weight, 0, D), (up_weight, 0, split))
    gather_e = joined((up_weight, split, FF))
    x, dm = call(
        "spread",
        functools.partial(spread_kernel, images),
        (slot_mask, block_in, cotangent),
        None,
        (shape((size, D), BF16), shape((size, D), BF16)),
        None,
        16,
    )
    gather_a = call("line_up", line_up_kernel, (packed_weight,) + vectors, None, shape((1, rows, wide_a), BF16), None, 60)
    gather_c = down_weight[None]
    gather_c = links.advance(gather_c, hops["c"][0])
    gather_e = links.advance(gather_e, hops["e"][0])
    gather_b = links.advance(gather_b, hops["b"][0])
    gather_a = links.advance(gather_a, hops["a"][0])
    gather_c = links.advance(gather_c, hops["c"][1])
    gather_b = links.advance(gather_b, hops["b"][1])
    gather_e = links.advance(gather_e, hops["e"][1])
    gather_a = links.advance(gather_a, hops["a"][1])
    gather_c = links.advance(gather_c, hops["c"][2])
    gather_a = links.advance(gather_a, hops["a"][2])
    gather_e = links.advance(gather_e, hops["e"][2])
    gather_a = links.advance(gather_a, hops["a"][3])
    held_a, other_a = gather_a, links.swap(gather_a, 1, 1)
    gather_b = links.advance(gather_b, hops["b"][2])
    gather_e = links.advance(gather_e, hops["e"][3])
    held_e, other_e = gather_e, links.swap(gather_e, 1, 1)
    normed, qkv, attended, lse, vec = call(
        "attend",
        functools.partial(attend_kernel, flat["a"], rows),
        (place, x, held_a, other_a),
        None,
        (
            shape((size, D), BF16),
            shape((size, 3 * D), BF16),
            shape((size, D), BF16),
            shape((size, 128), F32),
            shape((16, D), F32),
        ),
        None,
        20,
        scratch=[pltpu.VMEM((D, 3 * D), BF16), pltpu.VMEM((D, 128), BF16)],
    )
    ubias = vec[8 : 8 + wide].reshape(wide, count, rows).transpose(1, 0, 2).reshape(1, FF)
    gather_b = links.advance(gather_b, hops["b"][3])
    held_b, other_b = gather_b, links.swap(gather_b, 1, 1)
    gather_c = links.advance(gather_c, hops["c"][3])
    held_c, other_c = gather_c.reshape(view_c + (ff_rows, D)), links.swap(gather_c, 1, 1).reshape(view_c + (ff_rows, D))
    block_b = pl.BlockSpec((number, rows, D), lambda t: (0, 0, jnp.minimum(t, FIRST)))
    block_e = pl.BlockSpec((number, rows, D), lambda t: (0, 0, jnp.maximum(t - FIRST - 1, 0)))
    dealt = pl.BlockSpec(part_d + (ff_rows, D), lambda t: at_d(before(t)) + zeros)
    middle, normed_two, active, slope, kept_d, sent_d = call(
        "up",
        functools.partial(up_kernel, flat["b"], flat["e"], slots_d, rows, ff_rows),
        (place, x, attended, dm, held_b, other_b, held_e, other_e, vec, ubias),
        [SMEM] + [fixed(size, D)] * 3 + [block_b, block_b, block_e, block_e, fixed(16, D), tiled(1, before)],
        (
            shape((size, D), F32),
            shape((size, D), BF16),
            shape((size, FF), BF16),
            shape((size, FF), F32),
            shape(view_d + (ff_rows, D), BF16),
            shape(view_d + (ff_rows, D), BF16),
        ),
        (fixed(size, D), fixed(size, D), tiled(size, before), tiled(size, before), dealt, dealt),
        30,
        grid=(depth + 1,),
        scratch=[pltpu.VMEM((D, D), BF16)],
    )
    parts_d = links.exchange(kept_d, sent_d)
    block_u = pl.BlockSpec((number, rows, D), lambda t: (0, 0, t))
    low, kept_u, sent_u, usums = call(
        "slope",
        functools.partial(slope_kernel, flat["u"], slots_c, rows, ff_rows),
        (place, dm, normed_two, slope, held_c, other_c),
        [SMEM, fixed(size, D), fixed(size, D), tiled(size, same), block_c, block_c],
        (shape((size, FF), BF16), pieces(FF), pieces(FF), shape((D, 128), F32)),
        (tiled(size, same), block_u, block_u, pl.BlockSpec((D // depth, 128), lambda t: (t, 0))),
        22,
        grid=(depth,),
        scratch=[pltpu.VMEM((D, D), BF16)],
    )
    parts_u = links.exchange(kept_u, sent_u)
    parts_d = links.reduce(parts_d, hops["d"][0])
    block_b = pl.BlockSpec((number, rows, D), lambda t: (0, 0, jnp.where(t == depth, 0, jnp.minimum(t + 1, FIRST))))
    block_e = pl.BlockSpec((number, rows, D), lambda t: (0, 0, jnp.clip(t - FIRST, 0, depth - FIRST - 1)))
    datt, dmid, kept_o, sent_o, sums = call(
        "middle",
        functools.partial(middle_kernel, flat["b"], flat["e"], flat["i"], rows),
        (place, low, middle, dm, attended, held_b, other_b, held_e, other_e, vec),
        [SMEM, tiled(size, upto)] + [fixed(size, D)] * 3 + [block_b, block_b, block_e, block_e, fixed(16, D)],
        (shape((size, D), BF16), shape((size, D), F32), pieces(D), pieces(D), shape((8, D), F32)),
        (fixed(size, D), fixed(size, D), whole(D), whole(D), fixed(8, D)),
        26,
        grid=(depth + 1,),
        scratch=[pltpu.VMEM((D, D), BF16), pltpu.VMEM((size, D), F32)],
    )
    parts_u = links.reduce(parts_u, hops["u"][0])
    def heads(group, first, beside, *more):
        cols = beside + 3 * D // 2
        return call(
            "heads",
            functools.partial(heads_kernel, flat[group], rows, first, beside),
            (place, qkv, datt, lse, normed) + more,
            None,
            (shape((size, 3 * D // 2), BF16), pieces(cols), pieces(cols)),
            None,
            16,
        )

    half_a, kept_i, sent_i = heads("i", 0, D, kept_o, sent_o)
    parts_i = links.exchange(kept_i, sent_i)
    parts_d = links.reduce(parts_d, hops["d"][1])
    half_b, kept_h, sent_h = heads("j", HEADS // 4, 0)
    parts_u = links.reduce(parts_u, hops["u"][1])
    parts_i = links.reduce(parts_i, hops["i"][0])
    wide_j = 3 * D // 2 + 128
    kept_j, sent_j, igrad = call(
        "inward",
        functools.partial(input_kernel, flat["a"], flat["j"], rows),
        (place, x, dmid, half_a, half_b, kept_h, sent_h, held_a, other_a, vec, sums, usums),
        None,
        (pieces(wide_j), pieces(wide_j), shape((tokens, D), F32)),
        None,
        22,
        scratch=[pltpu.VMEM((D, 3 * D), BF16)],
    )
    parts_j = links.exchange(kept_j, sent_j)
    parts_d = links.reduce(parts_d, hops["d"][2])
    parts_j = links.reduce(parts_j, hops["j"][0])
    parts_u = links.reduce(parts_u, hops["u"][2])
    parts_i = links.reduce(parts_i, hops["i"][1])
    parts_d = links.reduce(parts_d, hops["d"][3])
    parts_j = links.reduce(parts_j, hops["j"][1])
    parts_i = links.reduce(parts_i, hops["i"][2])
    parts_j = links.reduce(parts_j, hops["j"][2])
    parts_u = links.reduce(parts_u, hops["u"][3])
    block_out = call(
        "down",
        functools.partial(down_kernel, slots_c, ff_rows),
        (place, slot_mask, active, middle, held_c, other_c, vec),
        [SMEM, SMEM, tiled(size, same), fixed(size, D), block_c, block_c, fixed(16, D)],
        shape((tokens, D), BF16),
        fixed(tokens, D),
        18,
        grid=(depth,),
        scratch=[pltpu.VMEM((D, D), BF16), pltpu.VMEM((size, D), F32)],
    )
    parts_i = links.reduce(parts_i, hops["i"][3])
    parts_j = links.reduce(parts_j, hops["j"][3])
    grads_d, grads_u, grads_i, grads_j = (settle(parts) for parts in (parts_d, parts_u, parts_i, parts_j))
    half = D // 2
    grads_packed = []
    for part in range(3):
        grads_packed += [grads_i[:, D + part * half : D + (part + 1) * half], grads_j[:, part * half : (part + 1) * half]]
    small = grads_j[:, 3 * half : 3 * half + 8 + wide].T
    return (
        block_out,
        igrad,
        small[0],
        small[1],
        jnp.concatenate(grads_packed, axis=1),
        small[2],
        small[3],
        grads_i[:, :D],
        small[4],
        small[5],
        small[6],
        grads_u,
        small[8:].reshape(-1),
        grads_d,
        small[7],
    )


def solution(mesh):
    row, flat = P("dp", None), P("dp")
    in_specs = (row, flat, flat, flat, row, flat, flat, row, flat, flat, flat, row, flat, row, flat, row)
    out_specs = (row, row, flat, flat, row, flat, flat, row, flat, flat, flat, row, flat, row, flat)
    return jax.shard_map(shards, mesh=mesh, in_specs=in_specs, out_specs=out_specs, check_vma=False)
```

time: 232 us -> 199 us (0.86)
  waiting for transfers between devices: 83.4 us -> 56.4 us
  local copies, waits for them, and re-layouts: 19.8 us -> 7.06 us
  starting transfers between devices: 36.7 us -> 44 us
    ppermute x32 -> x40, waiting for transfers between devices: 83.4 us -> 56.4 us  [swap(): return lax.ppermute(value, 'dp', pairs)]
    unnamed x82 -> x43, local copies, waits for them, and re-layouts: 12.7 us -> 4.49 us
    ppermute x32 -> x40, starting transfers between devices: 36.7 us -> 44 us  [swap(): return lax.ppermute(value, 'dp', pairs)]
    pallas_call x12 -> x16, Pallas kernels: 13.3 us -> 12.7 us  [kernel(): pl.pallas_call(body, grid_spec=pltpu.PrefetchScalarGridSpec(num_scalar_pr...]
    pallas_call x23 -> x28, Pallas kernels: 75.6 us -> 75.3 us  [the longest x12 61.7 us: launch(): pl.pallas_call(kernel, out_shape=outs + (TOKEN,), in_specs=list(specs) +...]
  transfers between devices with their start and end apart: 32 -> 40, of which waited for: 18 -> 18; matrix products, arithmetic and copies ran while one was open for 2% -> 1% of each run, Pallas kernels for 37% -> 44%
where the time goes in v1:
time: 199 us; the launch traced here: 198 us
  Pallas kernels  88 us (44%)
  waiting for transfers between devices  56.4 us (28%)
  starting transfers between devices  44 us (22%)
  local copies, waits for them, and re-layouts  7.06 us (4%)
    pallas_call x12, Pallas kernels, launch(): pl.pallas_call(kernel, out_shape=outs + (TOKEN,), in_specs=list(specs) +...  61.7 us
    ppermute x40, waiting for transfers between devices, swap(): return lax.ppermute(value, 'dp', pairs)  56.4 us
    ppermute x40, starting transfers between devices, swap(): return lax.ppermute(value, 'dp', pairs)  44 us
    pallas_call x16, Pallas kernels, kernel(): pl.pallas_call(body, out_shape=(jax.ShapeDtypeStruct((2, count, rows, wid...  13.6 us
    pallas_call x16, Pallas kernels, kernel(): pl.pallas_call(body, grid_spec=pltpu.PrefetchScalarGridSpec(num_scalar_pr...  12.7 us
    unnamed x43, local copies, waits for them, and re-layouts  4.49 us
  transfers between devices with their start and end apart: 40, of which 18 were waited for; matrix products, arithmetic and copies ran while one was open for 1% of the time, Pallas kernels for 44%

profile of v1, /device:TPU:0, one launch (start us, length us, event | category | flops | bytes accessed | tf_op | source)
XLA Modules:
  0.0 198.2 jit_solution(10445044577959295968)
XLA Ops:
  0.7 4.1 %collective-permute-start.3 = (bf16[1,96,768]{2,1,0:T(8,128)(2,1)}, bf16[1,96,768]{2,1,0:T(8,128)(2,1)S(1)}, u32[]{:S(2)}, u32[]{:S(2)}) collective-permute-start(bf16[1,96,768]{2,1,0:T(8,128)(2,1)} %bitcast.66), channel_id=1, source_target_pairs={{0,16},{1,17},{2,18},{3,19},{4,20},{5,21},{6,22},{7,23},{8,24},{9,... | collective-permute-start | bytes 442376 | tf_op jit(solution)/shard_map/ppermute | solution.py:127
  7.5 1.8 collective-permute-start.1
  10.1 1.8 line_up.1
  11.9 2.6 %collective-permute-start = (bf16[1,24,2432]{2,1,0:T(8,128)(2,1)}, bf16[1,24,2432]{2,1,0:T(8,128)(2,1)S(1)}, u32[]{:S(2)}, u32[]{:S(2)}) collective-permute-start(bf16[1,24,2432]{2,1,0:T(8,128)(2,1)} %get-tuple-element.145.held), channel_id=1, source_target_pairs={{0,16},{1,17},{2,18},{3,19},{4,20},{5,21},{6,22},{7,23},{8,24},{9,... | collective-permute-start | bytes 350216 | tf_op jit(solution)/shard_map/ppermute | solution.py:127
  15.2 1.6 collective-permute-start.7
  16.7 1.5 collective-permute-done.2.other
  19.3 1.6 collective-permute-start.6
  22.7 1.7 collective-permute-start.9
  24.4 1.6 collective-permute-done.6.other
  26.5 2.6 %collective-permute-done.5.other = bf16[2,24,1536]{2,1,0:T(8,128)(2,1)S(1)} collective-permute-done((bf16[2,24,1536]{2,1,0:T(8,128)(2,1)S(1)}, bf16[2,24,1536]{2,1,0:T(8,128)(2,1)S(1)}, u32[]{:S(2)}, u32[]{:S(2)}) %collective-permute-start.5) | collective-permute-done | bytes 147488 | tf_op jit(solution)/shard_map/ppermute | solution.py:127
  29.8 1.5 collective-permute-start.14
  31.9 1.6 collective-permute-start.8
  34.1 6.4 %collective-permute-done.8.other = bf16[4,24,2432]{2,1,0:T(8,128)(2,1)S(1)} collective-permute-done((bf16[4,24,2432]{2,1,0:T(8,128)(2,1)S(1)}, bf16[4,24,2432]{2,1,0:T(8,128)(2,1)S(1)}, u32[]{:S(2)}, u32[]{:S(2)}) %collective-permute-start.8) | collective-permute-done | bytes 466976 | tf_op jit(solution)/shard_map/ppermute | solution.py:127
  41.2 1.6 collective-permute-start.10
  44.4 10.4 %collective-permute-done.10.other = bf16[8,24,2432]{2,1,0:T(8,128)(2,1)S(1)} collective-permute-done((bf16[8,24,2432]{2,1,0:T(8,128)(2,1)S(1)}, bf16[8,24,2432]{2,1,0:T(8,128)(2,1)S(1)}, u32[]{:S(2)}, u32[]{:S(2)}) %collective-permute-start.10) | collective-permute-done | bytes 933920 | tf_op jit(solution)/shard_map/ppermute | solution.py:127
  56.2 1.6 collective-permute-start.15
  57.8 3.3 %collective-permute-done.13.other = bf16[8,24,1536]{2,1,0:T(8,128)(2,1)S(1)} collective-permute-done((bf16[8,24,1536]{2,1,0:T(8,128)(2,1)S(1)}, bf16[8,24,1536]{2,1,0:T(8,128)(2,1)S(1)}, u32[]{:S(2)}, u32[]{:S(2)}) %collective-permute-start.13) | collective-permute-done | bytes 589856 | tf_op jit(solution)/shard_map/ppermute | solution.py:127
  61.1 1.7 pair.29
  62.8 6.7 %attend.1 = (bf16[416,768]{1,0:T(8,128)(2,1)S(1)}, bf16[416,2304]{1,0:T(8,128)(2,1)S(1)}, bf16[416,768]{1,0:T(8,128)(2,1)S(1)}, f32[416,128]{1,0:T(8,128)S(1)}, f32[16,768]{1,0:T(8,128)S(1)}, /*index=5*/f32[8,128]{1,0:T(8,128)}) custom-call(s32[5]{0:T(128)S(1)} %stack.39.place.refs_0_, bf16[416,768]{1,0:T(8,128)(2,1)S(1)} %get-tuple-element.143.refs_1_, ...), custom_call_target="tpu_custom_call" | custom-call | flops 575000000 | bytes 768 | tf_op jit(solution)/shard_map/attend/pallas_call | solution.py:576
  69.6 1.0 collective-permute-done.15.other
  70.6 1.9 pair.30
  72.5 2.3 %pair.31 = (bf16[2,8,96,768]{3,2,1,0:T(8,128)(2,1)}, f32[8,128]{1,0:T(8,128)}) custom-call(s32[5]{0:T(128)S(1)} %stack.39.place.refs_0_, bf16[8,96,768]{2,1,0:T(8,128)(2,1)S(1)} %bitcast.49, bf16[8,96,768]{2,1,0:T(8,128)(2,1)S(1)} %collective-permute-done.18.other, f32[8,128]{1,0:T(8,128)} %get-tuple-element.182.refs_0_), custom_call_target="tpu_custom_call" | custom-call | flops 18400000000 | bytes 768 | tf_op jit(solution)/shard_map/pair/pallas_call | solution.py:145
  76.6 1.1 copy-done.11
  77.6 12.2 %up.1 = (f32[416,768]{1,0:T(8,128)S(1)}, bf16[416,768]{1,0:T(8,128)(2,1)S(1)}, bf16[416,3072]{1,0:T(8,128)(2,1)}, f32[416,3072]{1,0:T(8,128)}, bf16[2,2,2,2,96,7...) custom-call(s32[5]{0:T(128)S(1)} %stack.39.place.refs_0_, ...), custom_call_target="tpu_custom_call" | custom-call | flops 6899999744 | bytes 768 | tf_op jit(solution)/shard_map/up/pallas_call | solution.py:576
  90.0 8.4 %slope.1 = (bf16[416,3072]{1,0:T(8,128)(2,1)}, bf16[16,24,3072]{2,1,0:T(8,128)(2,1)S(1)}, bf16[16,24,3072]{2,1,0:T(8,128)(2,1)S(1)}, f32[768,128]{1,0:T(8,128)S(1)}, f32[8,128]{1,0:T(8,128)}) custom-call(s32[5]{0:T(128)S(1)} %stack.39.place.refs_0_, bf16[416,768]{1,0:T(8,128)(2,1)S(1)} %get-tuple-element.175.refs_3_.refs_1_, ...), custom_call_target="tpu_custom_call" | custom-call | flops 3449999872 | bytes 768 | tf_op jit(solution)/shard_map/slope/pallas_call | solution.py:576
  98.8 1.2 halve.16
  100.0 1.6 collective-permute-start.23
  101.5 8.1 %middle.1 = (bf16[416,768]{1,0:T(8,128)(2,1)S(1)}, f32[416,768]{1,0:T(8,128)S(1)}, bf16[16,24,768]{2,1,0:T(8,128)(2,1)S(1)}, bf16[16,24,768]{2,1,0:T(8,128)(2,1)...) custom-call(s32[5]{0:T(128)S(1)} %stack.39.place.refs_0_, bf16[416,3072]{1,0:T(8,128)(2,1)} %get-tuple-element.192.refs_1_, ...), custom_call_target="tpu_custom_call" | custom-call | flops 9200000000 | bytes 768 | tf_op jit(solution)/shard_map/middle/pallas_call | solution.py:576
  109.7 1.3 halve.17
  111.6 6.2 %heads.2 = (bf16[416,1152]{1,0:T(8,128)(2,1)S(1)}, bf16[16,24,1920]{2,1,0:T(8,128)(2,1)S(1)}, bf16[16,24,1920]{2,1,0:T(8,128)(2,1)S(1)}, f32[8,128]{1,0:T(8,128)}) custom-call(s32[5]{0:T(128)S(1)} %stack.39.place.refs_0_, bf16[416,2304]{1,0:T(8,128)(2,1)S(1)} %copy-done.7, bf16[416,768]{1,0:T(8,128)(2,1)S(1)} %get-tuple-element.201.refs_2_, ...), custom_call_target="tpu_custom_call" | custom-call | flops 6899999744 | bytes 768 | tf_op jit(solution)/shard_map/heads/pallas_call | solution.py:576
  118.9 1.6 collective-permute-start.27
  120.5 6.2 %heads.3 = (bf16[416,1152]{1,0:T(8,128)(2,1)S(1)}, bf16[16,24,1152]{2,1,0:T(8,128)(2,1)S(1)}, bf16[16,24,1152]{2,1,0:T(8,128)(2,1)S(1)}, f32[8,128]{1,0:T(8,128)}) custom-call(s32[5]{0:T(128)S(1)} %stack.39.place.refs_0_, bf16[416,2304]{1,0:T(8,128)(2,1)S(1)} %copy-done.7, bf16[416,768]{1,0:T(8,128)(2,1)S(1)} %get-tuple-element.201.refs_2_, ...), custom_call_target="tpu_custom_call" | custom-call | flops 2300000000 | bytes 768 | tf_op jit(solution)/shard_map/heads/pallas_call | solution.py:576
  126.6 8.6 %collective-permute-done.22.other_up.other_low = bf16[8,24,3072]{2,1,0:T(8,128)(2,1)S(1)} collective-permute-done((bf16[8,24,3072]{2,1,0:T(8,128)(2,1)S(1)}, bf16[8,24,3072]{2,1,0:T(8,128)(2,1)S(1)}, u32[]{:S(2)}, u32[]{:S(2)}) %collective-permute-start.22) | collective-permute-done | bytes 1179680 | tf_op jit(solution)/shard_map/ppermute | solution.py:127
  136.0 1.6 collective-permute-start.24
  138.6 1.6 collective-permute-start.31
  140.2 4.6 %inward.1 = (bf16[16,24,1280]{2,1,0:T(8,128)(2,1)S(1)}, bf16[16,24,1280]{2,1,0:T(8,128)(2,1)S(1)}, f32[394,768]{1,0:T(8,128)}, f32[8,128]{1,0:T(8,128)}) custom-call(s32[5]{0:T(128)S(1)} %stack.39.place.refs_0_, bf16[416,768]{1,0:T(8,128)(2,1)S(1)} %get-tuple-element.143.refs_1_, f32[416,768]{1,0:T(8,128)S(1)} %get-tuple-element.214.refs_2_, ...), custom_call_target="tpu_custom_call" | custom-call | flops 1150000000 | bytes 768 | tf_op jit(solution)/shard_map/inward/pallas_call | solution.py:576
  146.1 1.2 collective-permute-done.26.other_up.other_low
  148.8 3.5 %collective-permute-done.24.other_up.other_low = bf16[4,24,3072]{2,1,0:T(8,128)(2,1)S(1)} collective-permute-done((bf16[4,24,3072]{2,1,0:T(8,128)(2,1)S(1)}, bf16[4,24,3072]{2,1,0:T(8,128)(2,1)S(1)}, u32[]{:S(2)}, u32[]{:S(2)}) %collective-permute-start.24) | collective-permute-done | bytes 589856 | tf_op jit(solution)/shard_map/ppermute | solution.py:127
  154.4 1.7 collective-permute-start.33
  157.8 1.1 collective-permute-start.32
  158.9 3.2 %collective-permute-start.39 = (bf16[1,96,768]{2,1,0:T(8,128)(2,1)S(1)}, bf16[1,96,768]{2,1,0:T(8,128)(2,1)S(1)}, u32[]{:S(2)}, u32[]{:S(2)}) collective-permute-start(bf16[1,96,768]{2,1,0:T(8,128)(2,1)S(1)} %get-tuple-element.266), channel_id=1, source_target_pairs={{0,16},{1,17},{2,18},{3,19},{4,20},{5,21},{6,22},{7,23},{8,24},{9,... | collective-permute-start | bytes 442376 | tf_op jit(solution)/shard_map/ppermute | solution.py:127
  164.2 1.2 collective-permute-done.32.other_up.other_low
  166.8 6.7 %down.1 = (bf16[394,768]{1,0:T(8,128)(2,1)}, f32[8,128]{1,0:T(8,128)}) custom-call(s32[5]{0:T(128)S(1)} %stack.39.place.refs_0_, s32[394]{0:T(512)S(1)} %copy-done.5, bf16[416,3072]{1,0:T(8,128)(2,1)} %get-tuple-element.184.refs_2_, f32[416,768]{1,0:T(8,128)S(1)} %get-tuple-element.185.refs_2_.refs_3_, bf16[2,2,2,2,96,768]{5,4,3,2,1,0:T(8,128)(2,1)} %bitcast.22.refs_4_, ...), custom_call_target="tpu_custom_call" | custom-call | flops 575000000 | bytes 768 | tf_op jit(solution)/shard_map/down/pallas_call | solution.py:576
  174.0 2.8 %collective-permute-start.37 = (bf16[1,24,1920]{2,1,0:T(8,128)(2,1)S(1)}, bf16[1,24,1920]{2,1,0:T(8,128)(2,1)S(1)}, u32[]{:S(2)}, u32[]{:S(2)}) collective-permute-start(bf16[1,24,1920]{2,1,0:T(8,128)(2,1)S(1)} %get-tuple-element.262), channel_id=1, source_target_pairs={{0,16},{1,17},{2,18},{3,19},{4,20},{5,21},{6,22},{7,23},{8,24},{9,... | collective-permute-start | bytes 276488 | tf_op jit(solution)/shard_map/ppermute | solution.py:127
  177.8 2.8 %collective-permute-start.38 = (bf16[1,24,3072]{2,1,0:T(8,128)(2,1)S(1)}, bf16[1,24,3072]{2,1,0:T(8,128)(2,1)S(1)}, u32[]{:S(2)}, u32[]{:S(2)}) collective-permute-start(bf16[1,24,3072]{2,1,0:T(8,128)(2,1)S(1)} %get-tuple-element.264), channel_id=1, source_target_pairs={{0,16},{1,17},{2,18},{3,19},{4,20},{5,21},{6,22},{7,23},{8,24},{9,... | collective-permute-start | bytes 442376 | tf_op jit(solution)/shard_map/ppermute | solution.py:127
  180.6 2.0 collective-permute-done.37
  183.2 7.8 %collective-permute-done.34.other_up.other_low = bf16[2,24,1280]{2,1,0:T(8,128)(2,1)S(1)} collective-permute-done((bf16[2,24,1280]{2,1,0:T(8,128)(2,1)S(1)}, bf16[2,24,1280]{2,1,0:T(8,128)(2,1)S(1)}, u32[]{:S(2)}, u32[]{:S(2)}) %collective-permute-start.34) | collective-permute-done | bytes 122912 | tf_op jit(solution)/shard_map/ppermute | solution.py:127
  191.6 2.5 %collective-permute-done.38 = bf16[1,24,3072]{2,1,0:T(8,128)(2,1)S(1)} collective-permute-done((bf16[1,24,3072]{2,1,0:T(8,128)(2,1)S(1)}, bf16[1,24,3072]{2,1,0:T(8,128)(2,1)S(1)}, u32[]{:S(2)}, u32[]{:S(2)}) %collective-permute-start.38) | collective-permute-done | bytes 147488 | tf_op jit(solution)/shard_map/ppermute | solution.py:127
  (135 shorter events, 35.6 us)
Async XLA Ops:
  0.6 8.6 %copy-start.2 = (bf16[394,768]{1,0:T(8,128)(2,1)S(1)}, bf16[394,768]{1,0:T(8,128)(2,1)}, u32[]{:S(2)}) copy-start(bf16[394,768]{1,0:T(8,128)(2,1)} %refs_1_.5) | copy-start | bytes 1815556
  0.7 8.6 %copy-start.3 = (bf16[394,768]{1,0:T(8,128)(2,1)S(1)}, bf16[394,768]{1,0:T(8,128)(2,1)}, u32[]{:S(2)}) copy-start(bf16[394,768]{1,0:T(8,128)(2,1)} %refs_2_.2) | copy-start | bytes 1815556
  0.7 8.6 %copy-start.4 = (s32[394]{0:T(512)S(1)}, s32[394]{0:T(512)}, u32[]{:S(2)}) copy-start(s32[394]{0:T(512)} %refs_1_.7) | copy-start | bytes 4732
  0.7 13.9 %collective-permute-start.3 = (bf16[1,96,768]{2,1,0:T(8,128)(2,1)}, bf16[1,96,768]{2,1,0:T(8,128)(2,1)S(1)}, u32[]{:S(2)}, u32[]{:S(2)}) collective-permute-start(bf16[1,96,768]{2,1,0:T(8,128)(2,1)} %bitcast.66), channel_id=1, source_target_pairs={{0,16},{1,17},{2,18},{3,19},{4,20},{5,21},{6,22},{7,23},{8,24},{9,... | collective-permute-start | bytes 442376 | tf_op jit(solution)/shard_map/ppermute | solution.py:127
  7.4 10.8 %collective-permute-start.2 = (bf16[1,24,1536]{2,1,0:T(8,128)(2,1)S(1)}, bf16[1,24,1536]{2,1,0:T(8,128)(2,1)S(1)}, u32[]{:S(2)}, u32[]{:S(2)}) collective-permute-start(bf16[1,24,1536]{2,1,0:T(8,128)(2,1)S(1)} %get-tuple-element.147.held), channel_id=1, source_target_pairs={{0,16},{1,17},{2,18},{3,19},{4,20},{5,21},{6,22},{7,23},{8,24},{9,... | collective-permute-start | bytes 221192 | tf_op jit(solution)/shard_map/ppermute | solution.py:127
  7.5 11.3 %collective-permute-start.1 = (bf16[1,24,2304]{2,1,0:T(8,128)(2,1)S(1)}, bf16[1,24,2304]{2,1,0:T(8,128)(2,1)S(1)}, u32[]{:S(2)}, u32[]{:S(2)}) collective-permute-start(bf16[1,24,2304]{2,1,0:T(8,128)(2,1)S(1)} %get-tuple-element.146.held), channel_id=1, source_target_pairs={{0,8},{1,9},{2,10},{3,11},{4,12},{5,13},{6,14},{7,15},{8,0},{9,1},... | collective-permute-start | bytes 331784 | tf_op jit(solution)/shard_map/ppermute | solution.py:127
  10.1 4.5 %copy-start.15 = (bf16[96,768]{1,0:T(8,128)(2,1)S(1)}, bf16[96,768]{1,0:T(8,128)(2,1)}, u32[]{:S(2)}) copy-start(bf16[96,768]{1,0:T(8,128)(2,1)} %param.29) | copy-start | bytes 442372
  11.9 9.5 %collective-permute-start = (bf16[1,24,2432]{2,1,0:T(8,128)(2,1)}, bf16[1,24,2432]{2,1,0:T(8,128)(2,1)S(1)}, u32[]{:S(2)}, u32[]{:S(2)}) collective-permute-start(bf16[1,24,2432]{2,1,0:T(8,128)(2,1)} %get-tuple-element.145.held), channel_id=1, source_target_pairs={{0,16},{1,17},{2,18},{3,19},{4,20},{5,21},{6,22},{7,23},{8,24},{9,... | collective-permute-start | bytes 350216 | tf_op jit(solution)/shard_map/ppermute | solution.py:127
  15.2 6.9 %collective-permute-start.7 = (bf16[2,96,768]{2,1,0:T(8,128)(2,1)S(1)}, bf16[2,96,768]{2,1,0:T(8,128)(2,1)S(1)}, u32[]{:S(2)}, u32[]{:S(2)}) collective-permute-start(bf16[2,96,768]{2,1,0:T(8,128)(2,1)S(1)} %bitcast.60), channel_id=1, source_target_pairs={{0,2},{1,5},{2,0},{3,7},{4,6},{5,1},{6,4},{7,3},{8,10},{9,13},{10,... | collective-permute-start | bytes 884744 | tf_op jit(solution)/shard_map/ppermute | solution.py:127
  19.3 6.6 %collective-permute-start.6 = (bf16[2,24,2304]{2,1,0:T(8,128)(2,1)S(1)}, bf16[2,24,2304]{2,1,0:T(8,128)(2,1)S(1)}, u32[]{:S(2)}, u32[]{:S(2)}) collective-permute-start(bf16[2,24,2304]{2,1,0:T(8,128)(2,1)S(1)} %bitcast.64), channel_id=1, source_target_pairs={{0,2},{1,5},{2,0},{3,7},{4,6},{5,1},{6,4},{7,3},{8,10},{9,13},{10,... | collective-permute-start | bytes 663560 | tf_op jit(solution)/shard_map/ppermute | solution.py:127
  21.0 8.1 %collective-permute-start.5 = (bf16[2,24,1536]{2,1,0:T(8,128)(2,1)S(1)}, bf16[2,24,1536]{2,1,0:T(8,128)(2,1)S(1)}, u32[]{:S(2)}, u32[]{:S(2)}) collective-permute-start(bf16[2,24,1536]{2,1,0:T(8,128)(2,1)S(1)} %bitcast.68), channel_id=1, source_target_pairs={{0,2},{1,5},{2,0},{3,7},{4,6},{5,1},{6,4},{7,3},{8,10},{9,13},{10,... | collective-permute-start | bytes 442376 | tf_op jit(solution)/shard_map/ppermute | solution.py:127
  22.0 9.3 %collective-permute-start.4 = (bf16[2,24,2432]{2,1,0:T(8,128)(2,1)S(1)}, bf16[2,24,2432]{2,1,0:T(8,128)(2,1)S(1)}, u32[]{:S(2)}, u32[]{:S(2)}) collective-permute-start(bf16[2,24,2432]{2,1,0:T(8,128)(2,1)S(1)} %bitcast.62), channel_id=1, source_target_pairs={{0,8},{1,9},{2,10},{3,11},{4,12},{5,13},{6,14},{7,15},{8,0},{9,1},... | collective-permute-start | bytes 700424 | tf_op jit(solution)/shard_map/ppermute | solution.py:127
  22.7 10.7 %collective-permute-start.9 = (bf16[4,96,768]{2,1,0:T(8,128)(2,1)S(1)}, bf16[4,96,768]{2,1,0:T(8,128)(2,1)S(1)}, u32[]{:S(2)}, u32[]{:S(2)}) collective-permute-start(bf16[4,96,768]{2,1,0:T(8,128)(2,1)S(1)} %bitcast.50), channel_id=1, source_target_pairs={{0,4},{1,3},{2,6},{3,1},{4,0},{5,7},{6,2},{7,5},{8,12},{9,11},{10,... | collective-permute-start | bytes 1769480 | tf_op jit(solution)/shard_map/ppermute | solution.py:127
  29.7 13.1 %collective-permute-start.11 = (bf16[4,24,1536]{2,1,0:T(8,128)(2,1)S(1)}, bf16[4,24,1536]{2,1,0:T(8,128)(2,1)S(1)}, u32[]{:S(2)}, u32[]{:S(2)}) collective-permute-start(bf16[4,24,1536]{2,1,0:T(8,128)(2,1)S(1)} %bitcast.58), channel_id=1, source_target_pairs={{0,8},{1,9},{2,10},{3,11},{4,12},{5,13},{6,14},{7,15},{8,0},{9,1},... | collective-permute-start | bytes 884744 | tf_op jit(solution)/shard_map/ppermute | solution.py:127
  29.8 25.8 %collective-permute-start.14 = (bf16[4,24,2304]{2,1,0:T(8,128)(2,1)S(1)}, bf16[4,24,2304]{2,1,0:T(8,128)(2,1)S(1)}, u32[]{:S(2)}, u32[]{:S(2)}) collective-permute-start(bf16[4,24,2304]{2,1,0:T(8,128)(2,1)S(1)} %bitcast.56), channel_id=1, source_target_pairs={{0,16},{1,17},{2,18},{3,19},{4,20},{5,21},{6,22},{7,23},{8,24},{9,... | collective-permute-start | bytes 1327112 | tf_op jit(solution)/shard_map/ppermute | solution.py:127
  31.9 8.6 %collective-permute-start.8 = (bf16[4,24,2432]{2,1,0:T(8,128)(2,1)S(1)}, bf16[4,24,2432]{2,1,0:T(8,128)(2,1)S(1)}, u32[]{:S(2)}, u32[]{:S(2)}) collective-permute-start(bf16[4,24,2432]{2,1,0:T(8,128)(2,1)S(1)} %bitcast.54), channel_id=1, source_target_pairs={{0,2},{1,5},{2,0},{3,7},{4,6},{5,1},{6,4},{7,3},{8,10},{9,13},{10,... | collective-permute-start | bytes 1400840 | tf_op jit(solution)/shard_map/ppermute | solution.py:127
  41.2 13.6 %collective-permute-start.10 = (bf16[8,24,2432]{2,1,0:T(8,128)(2,1)S(1)}, bf16[8,24,2432]{2,1,0:T(8,128)(2,1)S(1)}, u32[]{:S(2)}, u32[]{:S(2)}) collective-permute-start(bf16[8,24,2432]{2,1,0:T(8,128)(2,1)S(1)} %bitcast.44), channel_id=1, source_target_pairs={{0,4},{1,3},{2,6},{3,1},{4,0},{5,7},{6,2},{7,5},{8,12},{9,11},{10,... | collective-permute-start | bytes 2801672 | tf_op jit(solution)/shard_map/ppermute | solution.py:127
  43.4 17.8 %collective-permute-start.13 = (bf16[8,24,1536]{2,1,0:T(8,128)(2,1)S(1)}, bf16[8,24,1536]{2,1,0:T(8,128)(2,1)S(1)}, u32[]{:S(2)}, u32[]{:S(2)}) collective-permute-start(bf16[8,24,1536]{2,1,0:T(8,128)(2,1)S(1)} %bitcast.52), channel_id=1, source_target_pairs={{0,4},{1,3},{2,6},{3,1},{4,0},{5,7},{6,2},{7,5},{8,12},{9,11},{10,... | collective-permute-start | bytes 1769480 | tf_op jit(solution)/shard_map/ppermute | solution.py:127
  43.9 28.6 %collective-permute-start.18 = (bf16[8,96,768]{2,1,0:T(8,128)(2,1)S(1)}, bf16[8,96,768]{2,1,0:T(8,128)(2,1)S(1)}, u32[]{:S(2)}, u32[]{:S(2)}) collective-permute-start(bf16[8,96,768]{2,1,0:T(8,128)(2,1)S(1)} %bitcast.48), channel_id=1, source_target_pairs={{0,8},{1,9},{2,10},{3,11},{4,12},{5,13},{6,14},{7,15},{8,0},{9,1},... | collective-permute-start | bytes 3538952 | tf_op jit(solution)/shard_map/ppermute | solution.py:127
  55.5 7.3 %collective-permute-start.12 = (bf16[16,24,2432]{2,1,0:T(8,128)(2,1)S(1)}, bf16[16,24,2432]{2,1,0:T(8,128)(2,1)S(1)}, u32[]{:S(2)}, u32[]{:S(2)}) collective-permute-start(bf16[16,24,2432]{2,1,0:T(8,128)(2,1)S(1)} %bitcast.41), channel_id=1, source_target_pairs={{0,1},{1,0},{2,3},{3,2},{4,5},{5,4},{6,7},{7,6},{8,9},{9,8},{10,11... | collective-permute-start | bytes 5603336 | tf_op jit(solution)/shard_map/ppermute | solution.py:127
  56.2 14.4 %collective-permute-start.15 = (bf16[8,24,2304]{2,1,0:T(8,128)(2,1)S(1)}, bf16[8,24,2304]{2,1,0:T(8,128)(2,1)S(1)}, u32[]{:S(2)}, u32[]{:S(2)}) collective-permute-start(bf16[8,24,2304]{2,1,0:T(8,128)(2,1)S(1)} %bitcast.46), channel_id=1, source_target_pairs={{0,4},{1,3},{2,6},{3,1},{4,0},{5,7},{6,2},{7,5},{8,12},{9,11},{10,... | collective-permute-start | bytes 2654216 | tf_op jit(solution)/shard_map/ppermute | solution.py:127
  62.8 12.9 %collective-permute-start.17 = (bf16[16,24,1536]{2,1,0:T(8,128)(2,1)}, bf16[16,24,1536]{2,1,0:T(8,128)(2,1)}, u32[]{:S(2)}, u32[]{:S(2)}) collective-permute-start(bf16[16,24,1536]{2,1,0:T(8,128)(2,1)} %bitcast.19.refs_6_.refs_7_), channel_id=1, source_target_pairs={{0,1},{1,0},{2,3},{3,2},{4,5},{5,4},{6,7},{7,6},{8,9},{9,8},{10,11... | collective-permute-start | bytes 3538952 | tf_op jit(solution)/shard_map/ppermute | solution.py:127
  62.8 6.7 %copy-start = (bf16[16,24,2432]{2,1,0:T(8,128)(2,1)}, bf16[16,24,2432]{2,1,0:T(8,128)(2,1)S(1)}, u32[]{:S(2)}) copy-start(bf16[16,24,2432]{2,1,0:T(8,128)(2,1)S(1)} %collective-permute-done.12.refs_3_.refs_8_) | copy-start | bytes 5603332
  69.5 5.2 %copy-start.6 = (bf16[416,2304]{1,0:T(8,128)(2,1)}, bf16[416,2304]{1,0:T(8,128)(2,1)S(1)}, u32[]{:S(2)}) copy-start(bf16[416,2304]{1,0:T(8,128)(2,1)S(1)} %get-tuple-element.200.refs_1_) | copy-start | bytes 5750788
  69.5 5.2 %copy-start.8 = (bf16[416,768]{1,0:T(8,128)(2,1)}, bf16[416,768]{1,0:T(8,128)(2,1)S(1)}, u32[]{:S(2)}) copy-start(bf16[416,768]{1,0:T(8,128)(2,1)S(1)} %get-tuple-element.203.refs_4_) | copy-start | bytes 1916932
  69.6 5.2 %copy-start.10 = (bf16[416,768]{1,0:T(8,128)(2,1)}, bf16[416,768]{1,0:T(8,128)(2,1)S(1)}, u32[]{:S(2)}) copy-start(bf16[416,768]{1,0:T(8,128)(2,1)S(1)} %get-tuple-element.174.refs_2_.refs_4_) | copy-start | bytes 1916932
  72.5 4.0 %collective-permute-start.16 = (bf16[16,24,2304]{2,1,0:T(8,128)(2,1)}, bf16[16,24,2304]{2,1,0:T(8,128)(2,1)}, u32[]{:S(2)}, u32[]{:S(2)}) collective-permute-start(bf16[16,24,2304]{2,1,0:T(8,128)(2,1)} %bitcast.18.refs_4_.refs_5_), channel_id=1, source_target_pairs={{0,1},{1,0},{2,3},{3,2},{4,5},{5,4},{6,7},{7,6},{8,9},{9,8},{10,11... | collective-permute-start | bytes 5308424 | tf_op jit(solution)/shard_map/ppermute | solution.py:127
  74.8 15.2 %collective-permute-start.19 = (bf16[16,96,768]{2,1,0:T(8,128)(2,1)}, bf16[16,96,768]{2,1,0:T(8,128)(2,1)}, u32[]{:S(2)}, u32[]{:S(2)}) collective-permute-start(bf16[16,96,768]{2,1,0:T(8,128)(2,1)} %bitcast.23), channel_id=1, source_target_pairs={{0,1},{1,0},{2,3},{3,2},{4,5},{5,4},{6,7},{7,6},{8,9},{9,8},{10,11... | collective-permute-start | bytes 7077896 | tf_op jit(solution)/shard_map/ppermute | solution.py:127
  89.9 8.9 %collective-permute-start.21 = (bf16[2,2,2,2,96,768]{5,4,3,2,1,0:T(8,128)(2,1)S(1)}, bf16[2,2,2,2,96,768]{5,4,3,2,1,0:T(8,128)(2,1)S(1)}, u32[]{:S(2)}, u32[]{:S(2)}) collective-permute-start(bf16[2,2,2,2,96,768]{5,4,3,2,1,0:T(8,128)(2,1)S(1)} %get-tuple-element.194), channel_id=1, source_target_pairs={{0,1},{1,0},{2,3},{3,2},{4,5},{5,4},{6,7},{7,6},{8,9},{9,8},{10,11... | collective-permute-start | bytes 7077896 | tf_op jit(solution)/shard_map/ppermute | solution.py:127
  98.4 11.3 %collective-permute-start.20 = (bf16[16,24,3072]{2,1,0:T(8,128)(2,1)S(1)}, bf16[16,24,3072]{2,1,0:T(8,128)(2,1)S(1)}, u32[]{:S(2)}, u32[]{:S(2)}) collective-permute-start(bf16[16,24,3072]{2,1,0:T(8,128)(2,1)S(1)} %get-tuple-element.191), channel_id=1, source_target_pairs={{0,1},{1,0},{2,3},{3,2},{4,5},{5,4},{6,7},{7,6},{8,9},{9,8},{10,11... | collective-permute-start | bytes 7077896 | tf_op jit(solution)/shard_map/ppermute | solution.py:127
  100.0 18.0 %collective-permute-start.23 = (bf16[8,96,768]{2,1,0:T(8,128)(2,1)S(1)}, bf16[8,96,768]{2,1,0:T(8,128)(2,1)S(1)}, u32[]{:S(2)}, u32[]{:S(2)}) collective-permute-start(bf16[8,96,768]{2,1,0:T(8,128)(2,1)S(1)} %get-tuple-element.205), channel_id=1, source_target_pairs={{0,2},{1,5},{2,0},{3,7},{4,6},{5,1},{6,4},{7,3},{8,10},{9,13},{10,... | collective-permute-start | bytes 3538952 | tf_op jit(solution)/shard_map/ppermute | solution.py:127
  111.0 24.2 %collective-permute-start.22 = (bf16[8,24,3072]{2,1,0:T(8,128)(2,1)S(1)}, bf16[8,24,3072]{2,1,0:T(8,128)(2,1)S(1)}, u32[]{:S(2)}, u32[]{:S(2)}) collective-permute-start(bf16[8,24,3072]{2,1,0:T(8,128)(2,1)S(1)} %get-tuple-element.199), channel_id=1, source_target_pairs={{0,2},{1,5},{2,0},{3,7},{4,6},{5,1},{6,4},{7,3},{8,10},{9,13},{10,... | collective-permute-start | bytes 3538952 | tf_op jit(solution)/shard_map/ppermute | solution.py:127
  117.9 19.8 %collective-permute-start.25 = (bf16[16,24,1920]{2,1,0:T(8,128)(2,1)S(1)}, bf16[16,24,1920]{2,1,0:T(8,128)(2,1)S(1)}, u32[]{:S(2)}, u32[]{:S(2)}) collective-permute-start(bf16[16,24,1920]{2,1,0:T(8,128)(2,1)S(1)} %get-tuple-element.222), channel_id=1, source_target_pairs={{0,1},{1,0},{2,3},{3,2},{4,5},{5,4},{6,7},{7,6},{8,9},{9,8},{10,11... | collective-permute-start | bytes 4423688 | tf_op jit(solution)/shard_map/ppermute | solution.py:127
  118.9 25.9 %collective-permute-start.27 = (bf16[4,96,768]{2,1,0:T(8,128)(2,1)S(1)}, bf16[4,96,768]{2,1,0:T(8,128)(2,1)S(1)}, u32[]{:S(2)}, u32[]{:S(2)}) collective-permute-start(bf16[4,96,768]{2,1,0:T(8,128)(2,1)S(1)} %get-tuple-element.228), channel_id=1, source_target_pairs={{0,4},{1,3},{2,6},{3,1},{4,0},{5,7},{6,2},{7,5},{8,12},{9,11},{10,... | collective-permute-start | bytes 1769480 | tf_op jit(solution)/shard_map/ppermute | solution.py:127
  136.0 16.3 %collective-permute-start.24 = (bf16[4,24,3072]{2,1,0:T(8,128)(2,1)S(1)}, bf16[4,24,3072]{2,1,0:T(8,128)(2,1)S(1)}, u32[]{:S(2)}, u32[]{:S(2)}) collective-permute-start(bf16[4,24,3072]{2,1,0:T(8,128)(2,1)S(1)} %get-tuple-element.213), channel_id=1, source_target_pairs={{0,4},{1,3},{2,6},{3,1},{4,0},{5,7},{6,2},{7,5},{8,12},{9,11},{10,... | collective-permute-start | bytes 1769480 | tf_op jit(solution)/shard_map/ppermute | solution.py:127
  138.6 15.0 %collective-permute-start.31 = (bf16[8,24,1920]{2,1,0:T(8,128)(2,1)S(1)}, bf16[8,24,1920]{2,1,0:T(8,128)(2,1)S(1)}, u32[]{:S(2)}, u32[]{:S(2)}) collective-permute-start(bf16[8,24,1920]{2,1,0:T(8,128)(2,1)S(1)} %get-tuple-element.239), channel_id=1, source_target_pairs={{0,2},{1,5},{2,0},{3,7},{4,6},{5,1},{6,4},{7,3},{8,10},{9,13},{10,... | collective-permute-start | bytes 2211848 | tf_op jit(solution)/shard_map/ppermute | solution.py:127
  144.8 2.6 %collective-permute-start.26 = (bf16[16,24,1280]{2,1,0:T(8,128)(2,1)S(1)}, bf16[16,24,1280]{2,1,0:T(8,128)(2,1)S(1)}, u32[]{:S(2)}, u32[]{:S(2)}) collective-permute-start(bf16[16,24,1280]{2,1,0:T(8,128)(2,1)S(1)} %get-tuple-element.226), channel_id=1, source_target_pairs={{0,1},{1,0},{2,3},{3,2},{4,5},{5,4},{6,7},{7,6},{8,9},{9,8},{10,11... | collective-permute-start | bytes 2949128 | tf_op jit(solution)/shard_map/ppermute | solution.py:127
  145.5 10.7 %collective-permute-start.30 = (bf16[2,96,768]{2,1,0:T(8,128)(2,1)S(1)}, bf16[2,96,768]{2,1,0:T(8,128)(2,1)S(1)}, u32[]{:S(2)}, u32[]{:S(2)}) collective-permute-start(bf16[2,96,768]{2,1,0:T(8,128)(2,1)S(1)} %get-tuple-element.237), channel_id=1, source_target_pairs={{0,8},{1,9},{2,10},{3,11},{4,12},{5,13},{6,14},{7,15},{8,0},{9,1},... | collective-permute-start | bytes 884744 | tf_op jit(solution)/shard_map/ppermute | solution.py:127
  148.2 8.9 %collective-permute-start.29 = (bf16[8,24,1280]{2,1,0:T(8,128)(2,1)S(1)}, bf16[8,24,1280]{2,1,0:T(8,128)(2,1)S(1)}, u32[]{:S(2)}, u32[]{:S(2)}) collective-permute-start(bf16[8,24,1280]{2,1,0:T(8,128)(2,1)S(1)} %get-tuple-element.235), channel_id=1, source_target_pairs={{0,2},{1,5},{2,0},{3,7},{4,6},{5,1},{6,4},{7,3},{8,10},{9,13},{10,... | collective-permute-start | bytes 1474568 | tf_op jit(solution)/shard_map/ppermute | solution.py:127
  153.0 13.1 %collective-permute-start.28 = (bf16[2,24,3072]{2,1,0:T(8,128)(2,1)S(1)}, bf16[2,24,3072]{2,1,0:T(8,128)(2,1)S(1)}, u32[]{:S(2)}, u32[]{:S(2)}) collective-permute-start(bf16[2,24,3072]{2,1,0:T(8,128)(2,1)S(1)} %get-tuple-element.233), channel_id=1, source_target_pairs={{0,8},{1,9},{2,10},{3,11},{4,12},{5,13},{6,14},{7,15},{8,0},{9,1},... | collective-permute-start | bytes 884744 | tf_op jit(solution)/shard_map/ppermute | solution.py:127
  154.4 8.4 %collective-permute-start.33 = (bf16[4,24,1920]{2,1,0:T(8,128)(2,1)S(1)}, bf16[4,24,1920]{2,1,0:T(8,128)(2,1)S(1)}, u32[]{:S(2)}, u32[]{:S(2)}) collective-permute-start(bf16[4,24,1920]{2,1,0:T(8,128)(2,1)S(1)} %get-tuple-element.246), channel_id=1, source_target_pairs={{0,4},{1,3},{2,6},{3,1},{4,0},{5,7},{6,2},{7,5},{8,12},{9,11},{10,... | collective-permute-start | bytes 1105928 | tf_op jit(solution)/shard_map/ppermute | solution.py:127
  157.8 7.7 %collective-permute-start.32 = (bf16[4,24,1280]{2,1,0:T(8,128)(2,1)S(1)}, bf16[4,24,1280]{2,1,0:T(8,128)(2,1)S(1)}, u32[]{:S(2)}, u32[]{:S(2)}) collective-permute-start(bf16[4,24,1280]{2,1,0:T(8,128)(2,1)S(1)} %get-tuple-element.244), channel_id=1, source_target_pairs={{0,4},{1,3},{2,6},{3,1},{4,0},{5,7},{6,2},{7,5},{8,12},{9,11},{10,... | collective-permute-start | bytes 737288 | tf_op jit(solution)/shard_map/ppermute | solution.py:127
  158.9 18.0 %collective-permute-start.39 = (bf16[1,96,768]{2,1,0:T(8,128)(2,1)S(1)}, bf16[1,96,768]{2,1,0:T(8,128)(2,1)S(1)}, u32[]{:S(2)}, u32[]{:S(2)}) collective-permute-start(bf16[1,96,768]{2,1,0:T(8,128)(2,1)S(1)} %get-tuple-element.266), channel_id=1, source_target_pairs={{0,16},{1,17},{2,18},{3,19},{4,20},{5,21},{6,22},{7,23},{8,24},{9,... | collective-permute-start | bytes 442376 | tf_op jit(solution)/shard_map/ppermute | solution.py:127
  163.5 10.0 %collective-permute-start.35 = (bf16[2,24,1920]{2,1,0:T(8,128)(2,1)S(1)}, bf16[2,24,1920]{2,1,0:T(8,128)(2,1)S(1)}, u32[]{:S(2)}, u32[]{:S(2)}) collective-permute-start(bf16[2,24,1920]{2,1,0:T(8,128)(2,1)S(1)} %get-tuple-element.256), channel_id=1, source_target_pairs={{0,8},{1,9},{2,10},{3,11},{4,12},{5,13},{6,14},{7,15},{8,0},{9,1},... | collective-permute-start | bytes 552968 | tf_op jit(solution)/shard_map/ppermute | solution.py:127
  174.0 8.5 %collective-permute-start.37 = (bf16[1,24,1920]{2,1,0:T(8,128)(2,1)S(1)}, bf16[1,24,1920]{2,1,0:T(8,128)(2,1)S(1)}, u32[]{:S(2)}, u32[]{:S(2)}) collective-permute-start(bf16[1,24,1920]{2,1,0:T(8,128)(2,1)S(1)} %get-tuple-element.262), channel_id=1, source_target_pairs={{0,16},{1,17},{2,18},{3,19},{4,20},{5,21},{6,22},{7,23},{8,24},{9,... | collective-permute-start | bytes 276488 | tf_op jit(solution)/shard_map/ppermute | solution.py:127
  177.6 13.3 %collective-permute-start.34 = (bf16[2,24,1280]{2,1,0:T(8,128)(2,1)S(1)}, bf16[2,24,1280]{2,1,0:T(8,128)(2,1)S(1)}, u32[]{:S(2)}, u32[]{:S(2)}) collective-permute-start(bf16[2,24,1280]{2,1,0:T(8,128)(2,1)S(1)} %get-tuple-element.254), channel_id=1, source_target_pairs={{0,16},{1,17},{2,18},{3,19},{4,20},{5,21},{6,22},{7,23},{8,24},{9,... | collective-permute-start | bytes 368648 | tf_op jit(solution)/shard_map/ppermute | solution.py:127
  177.8 16.3 %collective-permute-start.38 = (bf16[1,24,3072]{2,1,0:T(8,128)(2,1)S(1)}, bf16[1,24,3072]{2,1,0:T(8,128)(2,1)S(1)}, u32[]{:S(2)}, u32[]{:S(2)}) collective-permute-start(bf16[1,24,3072]{2,1,0:T(8,128)(2,1)S(1)} %get-tuple-element.264), channel_id=1, source_target_pairs={{0,16},{1,17},{2,18},{3,19},{4,20},{5,21},{6,22},{7,23},{8,24},{9,... | collective-permute-start | bytes 442376 | tf_op jit(solution)/shard_map/ppermute | solution.py:127
  191.5 4.3 %collective-permute-start.36 = (bf16[1,24,1280]{2,1,0:T(8,128)(2,1)S(1)}, bf16[1,24,1280]{2,1,0:T(8,128)(2,1)S(1)}, u32[]{:S(2)}, u32[]{:S(2)}) collective-permute-start(bf16[1,24,1280]{2,1,0:T(8,128)(2,1)S(1)} %get-tuple-element.260), channel_id=1, source_target_pairs={{0,8},{1,9},{2,10},{3,11},{4,12},{5,13},{6,14},{7,15},{8,0},{9,1},... | collective-permute-start | bytes 184328 | tf_op jit(solution)/shard_map/ppermute | solution.py:127
  (11 other events, 17.0 us)

commit v2 on v1

--- a/solution.py
+++ b/solution.py
@@ -14,8 +14,8 @@
 LEN = 197
 SLOT = 208
 SPEED = 1.15e9
-LENGTHS = (12, 0.25, 0.25, 1, 1, 0.5, 12, 1, 0.25, 24, 0.25, 0.25, 16, 6, 16, 0.25, 16, 3, 0.5, 0.25, 16, 6, 3, 2, 8, 0.5, 6, 2, 2, 6, 1, 1, 24, 0.5, 0.25, 1, 3, 32, 0.25, 0.25, 2, 0.5, 0.5, 0.25)
-ORDERS = {'a': 'fnxx', 'b': 'nxfx', 'e': 'fxnx', 'c': 'fxxn', 'd': 'xxnf', 'u': 'xxnf', 'i': 'xxnf', 'j': 'xxfn'}
+LENGTHS = (1, 8, 0.25, 0.5, 24, 1, 1, 24, 0.25, 1, 2, 0.25, 1, 8, 3, 24, 1, 0.25, 0.25, 8, 2, 6, 0.25, 12, 1, 2, 1, 16, 2, 1, 32, 2, 32, 0.25, 4, 0.5, 0.25, 0.5, 6, 24, 0.5, 2, 1, 8)
+ORDERS = {'a': 'fnxx', 'b': 'fxnx', 'e': 'xfxn', 'c': 'nxfx', 'd': 'xnfx', 'u': 'xnxf', 'i': 'xxfn', 'j': 'xxnf'}
 GATHERS = ("a", "b", "e", "c")
 FIRST = 2
 PINNED = {}
@@ -598,8 +598,16 @@
     split = FIRST * tile
     vectors = (gain_first, shift_first, query_bias, value_bias, out_bias, gain_second, shift_second, down_bias, up_bias)
     wide_a = 3 * D + 128
+    gather_a = call("line_up", line_up_kernel, (packed_weight,) + vectors, None, shape((1, rows, wide_a), BF16), None, 60)
+    gather_e = joined((up_weight, split, FF))
     gather_b = joined((out_weight, 0, D), (up_weight, 0, split))
-    gather_e = joined((up_weight, split, FF))
+    gather_a = links.advance(gather_a, hops["a"][0])
+    gather_c = down_weight[None]
+    gather_c = links.advance(gather_c, hops["c"][0])
+    gather_b = links.advance(gather_b, hops["b"][0])
+    gather_e = links.advance(gather_e, hops["e"][0])
+    gather_a = links.advance(gather_a, hops["a"][1])
+    gather_b = links.advance(gather_b, hops["b"][1])
     x, dm = call(
         "spread",
         functools.partial(spread_kernel, images),
@@ -609,24 +617,14 @@
         None,
         16,
     )
-    gather_a = call("line_up", line_up_kernel, (packed_weight,) + vectors, None, shape((1, rows, wide_a), BF16), None, 60)
-    gather_c = down_weight[None]
-    gather_c = links.advance(gather_c, hops["c"][0])
-    gather_e = links.advance(gather_e, hops["e"][0])
-    gather_b = links.advance(gather_b, hops["b"][0])
-    gather_a = links.advance(gather_a, hops["a"][0])
     gather_c = links.advance(gather_c, hops["c"][1])
-    gather_b = links.advance(gather_b, hops["b"][1])
+    gather_a = links.advance(gather_a, hops["a"][2])
     gather_e = links.advance(gather_e, hops["e"][1])
-    gather_a = links.advance(gather_a, hops["a"][1])
-    gather_c = links.advance(gather_c, hops["c"][2])
-    gather_a = links.advance(gather_a, hops["a"][2])
-    gather_e = links.advance(gather_e, hops["e"][2])
+    gather_b = links.advance(gather_b, hops["b"][2])
     gather_a = links.advance(gather_a, hops["a"][3])
     held_a, other_a = gather_a, links.swap(gather_a, 1, 1)
-    gather_b = links.advance(gather_b, hops["b"][2])
-    gather_e = links.advance(gather_e, hops["e"][3])
-    held_e, other_e = gather_e, links.swap(gather_e, 1, 1)
+    gather_e = links.advance(gather_e, hops["e"][2])
+    gather_c = links.advance(gather_c, hops["c"][2])
     normed, qkv, attended, lse, vec = call(
         "attend",
         functools.partial(attend_kernel, flat["a"], rows),
@@ -646,6 +644,8 @@
     ubias = vec[8 : 8 + wide].reshape(wide, count, rows).transpose(1, 0, 2).reshape(1, FF)
     gather_b = links.advance(gather_b, hops["b"][3])
     held_b, other_b = gather_b, links.swap(gather_b, 1, 1)
+    gather_e = links.advance(gather_e, hops["e"][3])
+    held_e, other_e = gather_e, links.swap(gather_e, 1, 1)
     gather_c = links.advance(gather_c, hops["c"][3])
     held_c, other_c = gather_c.reshape(view_c + (ff_rows, D)), links.swap(gather_c, 1, 1).reshape(view_c + (ff_rows, D))
     block_b = pl.BlockSpec((number, rows, D), lambda t: (0, 0, jnp.minimum(t, FIRST)))
@@ -714,8 +714,8 @@
     parts_i = links.exchange(kept_i, sent_i)
     parts_d = links.reduce(parts_d, hops["d"][1])
     half_b, kept_h, sent_h = heads("j", HEADS // 4, 0)
+    parts_i = links.reduce(parts_i, hops["i"][0])
     parts_u = links.reduce(parts_u, hops["u"][1])
-    parts_i = links.reduce(parts_i, hops["i"][0])
     wide_j = 3 * D // 2 + 128
     kept_j, sent_j, igrad = call(
         "inward",
@@ -729,14 +729,8 @@
     )
     parts_j = links.exchange(kept_j, sent_j)
     parts_d = links.reduce(parts_d, hops["d"][2])
+    parts_i = links.reduce(parts_i, hops["i"][1])
     parts_j = links.reduce(parts_j, hops["j"][0])
-    parts_u = links.reduce(parts_u, hops["u"][2])
-    parts_i = links.reduce(parts_i, hops["i"][1])
-    parts_d = links.reduce(parts_d, hops["d"][3])
-    parts_j = links.reduce(parts_j, hops["j"][1])
-    parts_i = links.reduce(parts_i, hops["i"][2])
-    parts_j = links.reduce(parts_j, hops["j"][2])
-    parts_u = links.reduce(parts_u, hops["u"][3])
     block_out = call(
         "down",
         functools.partial(down_kernel, slots_c, ff_rows),
@@ -748,7 +742,13 @@
         grid=(depth,),
         scratch=[pltpu.VMEM((D, D), BF16), pltpu.VMEM((size, D), F32)],
     )
+    parts_i = links.reduce(parts_i, hops["i"][2])
+    parts_j = links.reduce(parts_j, hops["j"][1])
+    parts_u = links.reduce(parts_u, hops["u"][2])
+    parts_j = links.reduce(parts_j, hops["j"][2])
+    parts_u = links.reduce(parts_u, hops["u"][3])
     parts_i = links.reduce(parts_i, hops["i"][3])
+    parts_d = links.reduce(parts_d, hops["d"][3])
     parts_j = links.reduce(parts_j, hops["j"][3])
     grads_d, grads_u, grads_i, grads_j = (settle(parts) for parts in (parts_d, parts_u, parts_i, parts_j))
     half = D // 2

time: 199 us -> 187 us (0.940)
  waiting for transfers between devices: 56.4 us -> 49.2 us
  local copies, waits for them, and re-layouts: 7.06 us -> 4.07 us
  starting transfers between devices: 44 us -> 41.5 us
    ppermute x40, waiting for transfers between devices: 56.4 us -> 49.2 us  [swap(): return lax.ppermute(value, 'dp', pairs)]
    unnamed x43, local copies, waits for them, and re-layouts: 4.49 us -> 1.5 us
    ppermute x40, starting transfers between devices: 44 us -> 41.5 us  [swap(): return lax.ppermute(value, 'dp', pairs)]
  transfers between devices with their start and end apart: 40 -> 40, of which waited for: 18 -> 14; matrix products, arithmetic and copies ran while one was open for 1% -> 2% of each run, Pallas kernels for 44% -> 47%
where the time goes in v2:
time: 187 us
  Pallas kernels  89.5 us (48%)
  waiting for transfers between devices  49.2 us (26%)
  starting transfers between devices  41.5 us (22%)
  local copies, waits for them, and re-layouts  4.07 us (2%)
    pallas_call x12, Pallas kernels, launch(): pl.pallas_call(kernel, out_shape=outs + (TOKEN,), in_specs=list(specs) +...  62.3 us
    ppermute x40, waiting for transfers between devices, swap(): return lax.ppermute(value, 'dp', pairs)  49.2 us
    ppermute x40, starting transfers between devices, swap(): return lax.ppermute(value, 'dp', pairs)  41.5 us
    pallas_call x16, Pallas kernels, kernel(): pl.pallas_call(body, out_shape=(jax.ShapeDtypeStruct((2, count, rows, wid...  14.5 us
    pallas_call x16, Pallas kernels, kernel(): pl.pallas_call(body, grid_spec=pltpu.PrefetchScalarGridSpec(num_scalar_pr...  12.7 us
  transfers between devices with their start and end apart: 40, of which 14 were waited for; matrix products, arithmetic and copies ran while one was open for 2% of the time, Pallas kernels for 47%

profile of v2, /device:TPU:0, one launch (start us, length us, event | category | flops | bytes accessed | tf_op | source)
XLA Modules:
  0.0 187.0 jit_solution(14174463267685127968)
XLA Ops:
  0.7 1.8 line_up.1
  2.5 4.0 %collective-permute-start.2 = (bf16[1,24,2432]{2,1,0:T(8,128)(2,1)}, bf16[1,24,2432]{2,1,0:T(8,128)(2,1)S(1)}, u32[]{:S(2)}, u32[]{:S(2)}) collective-permute-start(bf16[1,24,2432]{2,1,0:T(8,128)(2,1)} %get-tuple-element.144.held), channel_id=1, source_target_pairs={{0,16},{1,17},{2,18},{3,19},{4,20},{5,21},{6,22},{7,23},{8,24},{9,... | collective-permute-start | bytes 350216 | tf_op jit(solution)/shard_map/ppermute | solution.py:127
  6.5 1.6 collective-permute-start.1
  8.1 1.6 collective-permute-start.5
  10.2 2.4 %collective-permute-done.2.other = bf16[1,24,2432]{2,1,0:T(8,128)(2,1)S(1)} collective-permute-done((bf16[1,24,2432]{2,1,0:T(8,128)(2,1)}, bf16[1,24,2432]{2,1,0:T(8,128)(2,1)S(1)}, u32[]{:S(2)}, u32[]{:S(2)}) %collective-permute-start.2) | collective-permute-done | bytes 116768 | tf_op jit(solution)/shard_map/ppermute | solution.py:127
  13.2 1.1 collective-permute-start.4
  15.1 2.3 %collective-permute-done.other = bf16[1,24,2304]{2,1,0:T(8,128)(2,1)S(1)} collective-permute-done((bf16[1,24,2304]{2,1,0:T(8,128)(2,1)S(1)}, bf16[1,24,2304]{2,1,0:T(8,128)(2,1)S(1)}, u32[]{:S(2)}, u32[]{:S(2)}) %collective-permute-start) | collective-permute-done | bytes 110624 | tf_op jit(solution)/shard_map/ppermute | solution.py:127
  17.9 1.6 collective-permute-start.3
  21.2 1.6 collective-permute-start.6
  22.8 3.1 %collective-permute-start.10 = (bf16[2,24,1536]{2,1,0:T(8,128)(2,1)S(1)}, bf16[2,24,1536]{2,1,0:T(8,128)(2,1)S(1)}, u32[]{:S(2)}, u32[]{:S(2)}) collective-permute-start(bf16[2,24,1536]{2,1,0:T(8,128)(2,1)S(1)} %bitcast.67), channel_id=1, source_target_pairs={{0,16},{1,17},{2,18},{3,19},{4,20},{5,21},{6,22},{7,23},{8,24},{9,... | collective-permute-start | bytes 442376 | tf_op jit(solution)/shard_map/ppermute | solution.py:127
  26.5 2.5 %collective-permute-start.9 = (bf16[4,24,2304]{2,1,0:T(8,128)(2,1)S(1)}, bf16[4,24,2304]{2,1,0:T(8,128)(2,1)S(1)}, u32[]{:S(2)}, u32[]{:S(2)}) collective-permute-start(bf16[4,24,2304]{2,1,0:T(8,128)(2,1)S(1)} %bitcast.55), channel_id=1, source_target_pairs={{0,8},{1,9},{2,10},{3,11},{4,12},{5,13},{6,14},{7,15},{8,0},{9,1},... | collective-permute-start | bytes 1327112 | tf_op jit(solution)/shard_map/ppermute | solution.py:127
  30.5 1.5 collective-permute-done.6.other
  32.7 1.6 collective-permute-start.8
  35.4 12.5 %collective-permute-done.9.other = bf16[4,24,2304]{2,1,0:T(8,128)(2,1)S(1)} collective-permute-done((bf16[4,24,2304]{2,1,0:T(8,128)(2,1)S(1)}, bf16[4,24,2304]{2,1,0:T(8,128)(2,1)S(1)}, u32[]{:S(2)}, u32[]{:S(2)}) %collective-permute-start.9) | collective-permute-done | bytes 442400 | tf_op jit(solution)/shard_map/ppermute | solution.py:127
  51.1 7.4 %collective-permute-done.12.other = bf16[4,96,768]{2,1,0:T(8,128)(2,1)S(1)} collective-permute-done((bf16[4,96,768]{2,1,0:T(8,128)(2,1)S(1)}, bf16[4,96,768]{2,1,0:T(8,128)(2,1)S(1)}, u32[]{:S(2)}, u32[]{:S(2)}) %collective-permute-start.12) | collective-permute-done | bytes 589856 | tf_op jit(solution)/shard_map/ppermute | solution.py:127
  58.5 1.6 pair.28
  60.9 6.7 %attend.1 = (bf16[416,768]{1,0:T(8,128)(2,1)S(1)}, bf16[416,2304]{1,0:T(8,128)(2,1)S(1)}, bf16[416,768]{1,0:T(8,128)(2,1)S(1)}, f32[416,128]{1,0:T(8,128)S(1)}, f32[16,768]{1,0:T(8,128)S(1)}, /*index=5*/f32[8,128]{1,0:T(8,128)}) custom-call(s32[5]{0:T(128)S(1)} %stack.39.place.refs_0_, bf16[416,768]{1,0:T(8,128)(2,1)S(1)} %get-tuple-element.155.refs_1_, ...), custom_call_target="tpu_custom_call" | custom-call | flops 287500000 | bytes 768 | tf_op jit(solution)/shard_map/attend/pallas_call | solution.py:576
  67.7 2.2 %pair.29 = (bf16[2,8,24,2304]{3,2,1,0:T(8,128)(2,1)}, f32[8,128]{1,0:T(8,128)}) custom-call(s32[5]{0:T(128)S(1)} %stack.39.place.refs_0_, bf16[8,24,2304]{2,1,0:T(8,128)(2,1)S(1)} %bitcast.44, bf16[8,24,2304]{2,1,0:T(8,128)(2,1)S(1)} %collective-permute-done.14.other, f32[8,128]{1,0:T(8,128)} %get-tuple-element.175.refs_0_), custom_call_target="tpu_custom_call" | custom-call | flops 287500000 | bytes 768 | tf_op jit(solution)/shard_map/pair/pallas_call | solution.py:145
  69.9 1.1 collective-permute-done.16.other
  71.0 1.7 pair.30
  73.1 3.6 %collective-permute-done.18.other = bf16[8,96,768]{2,1,0:T(8,128)(2,1)} collective-permute-done((bf16[8,96,768]{2,1,0:T(8,128)(2,1)}, bf16[8,96,768]{2,1,0:T(8,128)(2,1)}, u32[]{:S(2)}, u32[]{:S(2)}) %collective-permute-start.18) | collective-permute-done | bytes 1179680 | tf_op jit(solution)/shard_map/ppermute | solution.py:127
  76.7 1.9 %pair.31 = (bf16[2,8,96,768]{3,2,1,0:T(8,128)(2,1)S(1)}, f32[8,128]{1,0:T(8,128)}) custom-call(s32[5]{0:T(128)S(1)} %stack.39.place.refs_0_, bf16[8,96,768]{2,1,0:T(8,128)(2,1)} %bitcast.21.held, bf16[8,96,768]{2,1,0:T(8,128)(2,1)} %collective-permute-done.18.other, f32[8,128]{1,0:T(8,128)} %get-tuple-element.182.refs_0_), custom_call_target="tpu_custom_call" | custom-call | flops 2300000000 | bytes 768 | tf_op jit(solution)/shard_map/pair/pallas_call | solution.py:145
  78.7 13.0 %up.1 = (f32[416,768]{1,0:T(8,128)S(1)}, bf16[416,768]{1,0:T(8,128)(2,1)S(1)}, bf16[416,3072]{1,0:T(8,128)(2,1)}, f32[416,3072]{1,0:T(8,128)}, bf16[2,2,2,2,96,7...) custom-call(s32[5]{0:T(128)S(1)} %stack.39.place.refs_0_, ...), custom_call_target="tpu_custom_call" | custom-call | flops 6899999744 | bytes 768 | tf_op jit(solution)/shard_map/up/pallas_call | solution.py:576
  91.8 1.4 copy-done.17
  93.2 8.3 %slope.1 = (bf16[416,3072]{1,0:T(8,128)(2,1)}, bf16[16,24,3072]{2,1,0:T(8,128)(2,1)S(1)}, bf16[16,24,3072]{2,1,0:T(8,128)(2,1)S(1)}, f32[768,128]{1,0:T(8,128)S(1)}, f32[8,128]{1,0:T(8,128)}) custom-call(s32[5]{0:T(128)S(1)} %stack.39.place.refs_0_, bf16[416,768]{1,0:T(8,128)(2,1)S(1)} %get-tuple-element.173.refs_3_.refs_1_, ...), custom_call_target="tpu_custom_call" | custom-call | flops 287500000 | bytes 768 | tf_op jit(solution)/shard_map/slope/pallas_call | solution.py:576
  102.0 1.1 halve.16
  103.1 1.6 collective-permute-start.22
  104.7 8.1 %middle.1 = (bf16[416,768]{1,0:T(8,128)(2,1)S(1)}, f32[416,768]{1,0:T(8,128)S(1)}, bf16[16,24,768]{2,1,0:T(8,128)(2,1)S(1)}, bf16[16,24,768]{2,1,0:T(8,128)(2,1)...) custom-call(s32[5]{0:T(128)S(1)} %stack.39.place.refs_0_, bf16[416,3072]{1,0:T(8,128)(2,1)} %get-tuple-element.190.refs_1_, ...), custom_call_target="tpu_custom_call" | custom-call | flops 1150000000 | bytes 768 | tf_op jit(solution)/shard_map/middle/pallas_call | solution.py:576
  112.8 1.3 halve.17
  114.8 6.2 %heads.2 = (bf16[416,1152]{1,0:T(8,128)(2,1)S(1)}, bf16[16,24,1920]{2,1,0:T(8,128)(2,1)S(1)}, bf16[16,24,1920]{2,1,0:T(8,128)(2,1)S(1)}, f32[8,128]{1,0:T(8,128)}) custom-call(s32[5]{0:T(128)S(1)} %stack.39.place.refs_0_, bf16[416,2304]{1,0:T(8,128)(2,1)S(1)} %copy-done.4, bf16[416,768]{1,0:T(8,128)(2,1)S(1)} %get-tuple-element.197.refs_2_, ...), custom_call_target="tpu_custom_call" | custom-call | flops 1150000000 | bytes 768 | tf_op jit(solution)/shard_map/heads/pallas_call | solution.py:576
  121.1 0.9 halve.18
  122.4 6.2 %heads.3 = (bf16[416,1152]{1,0:T(8,128)(2,1)S(1)}, bf16[16,24,1152]{2,1,0:T(8,128)(2,1)S(1)}, bf16[16,24,1152]{2,1,0:T(8,128)(2,1)S(1)}, f32[8,128]{1,0:T(8,128)}) custom-call(s32[5]{0:T(128)S(1)} %stack.39.place.refs_0_, bf16[416,2304]{1,0:T(8,128)(2,1)S(1)} %copy-done.4, bf16[416,768]{1,0:T(8,128)(2,1)S(1)} %get-tuple-element.197.refs_2_, ...), custom_call_target="tpu_custom_call" | custom-call | flops 2300000000 | bytes 768 | tf_op jit(solution)/shard_map/heads/pallas_call | solution.py:576
  128.5 0.9 halve.19
  129.5 2.5 %collective-permute-done.23.other_up.other_low = bf16[8,24,3072]{2,1,0:T(8,128)(2,1)S(1)} collective-permute-done((bf16[8,24,3072]{2,1,0:T(8,128)(2,1)S(1)}, bf16[8,24,3072]{2,1,0:T(8,128)(2,1)S(1)}, u32[]{:S(2)}, u32[]{:S(2)}) %collective-permute-start.23) | collective-permute-done | bytes 1179680 | tf_op jit(solution)/shard_map/ppermute | solution.py:127
  132.0 0.9 halve.20
  133.3 1.5 collective-permute-start.26
  134.8 4.6 %inward.1 = (bf16[16,24,1280]{2,1,0:T(8,128)(2,1)S(1)}, bf16[16,24,1280]{2,1,0:T(8,128)(2,1)S(1)}, f32[394,768]{1,0:T(8,128)}, f32[8,128]{1,0:T(8,128)}) custom-call(s32[5]{0:T(128)S(1)} %stack.39.place.refs_0_, bf16[416,768]{1,0:T(8,128)(2,1)S(1)} %get-tuple-element.155.refs_1_, f32[416,768]{1,0:T(8,128)S(1)} %get-tuple-element.195.refs_2_, ...), custom_call_target="tpu_custom_call" | custom-call | flops 2300000000 | bytes 768 | tf_op jit(solution)/shard_map/inward/pallas_call | solution.py:576
  140.1 4.6 %collective-permute-done.26.other_up.other_low = bf16[8,24,1920]{2,1,0:T(8,128)(2,1)S(1)} collective-permute-done((bf16[8,24,1920]{2,1,0:T(8,128)(2,1)S(1)}, bf16[8,24,1920]{2,1,0:T(8,128)(2,1)S(1)}, u32[]{:S(2)}, u32[]{:S(2)}) %collective-permute-start.26) | collective-permute-done | bytes 737312 | tf_op jit(solution)/shard_map/ppermute | solution.py:127
  146.4 1.6 collective-permute-start.28
  148.5 3.4 %collective-permute-start.33 = (bf16[2,96,768]{2,1,0:T(8,128)(2,1)S(1)}, bf16[2,96,768]{2,1,0:T(8,128)(2,1)S(1)}, u32[]{:S(2)}, u32[]{:S(2)}) collective-permute-start(bf16[2,96,768]{2,1,0:T(8,128)(2,1)S(1)} %get-tuple-element.250), channel_id=1, source_target_pairs={{0,16},{1,17},{2,18},{3,19},{4,20},{5,21},{6,22},{7,23},{8,24},{9,... | collective-permute-start | bytes 884744 | tf_op jit(solution)/shard_map/ppermute | solution.py:127
  151.9 6.7 %down.1 = (bf16[394,768]{1,0:T(8,128)(2,1)}, f32[8,128]{1,0:T(8,128)}) custom-call(s32[5]{0:T(128)S(1)} %stack.39.place.refs_0_, s32[394]{0:T(512)S(1)} %copy-done.10, bf16[416,3072]{1,0:T(8,128)(2,1)} %get-tuple-element.184.refs_2_, f32[416,768]{1,0:T(8,128)S(1)} %get-tuple-element.185.refs_2_.refs_3_, bf16[2,2,2,2,96,768]{5,4,3,2,1,0:T(8,128)(2,1)} %bitcast.39, ...), custom_call_target="tpu_custom_call" | custom-call | flops 575000000 | bytes 768 | tf_op jit(solution)/shard_map/down/pallas_call | solution.py:576
  159.2 1.2 collective-permute-start.34
  162.5 1.6 collective-permute-start.35
  164.1 3.4 %collective-permute-done.30.other_up.other_low = bf16[4,24,1280]{2,1,0:T(8,128)(2,1)S(1)} collective-permute-done((bf16[4,24,1280]{2,1,0:T(8,128)(2,1)S(1)}, bf16[4,24,1280]{2,1,0:T(8,128)(2,1)S(1)}, u32[]{:S(2)}, u32[]{:S(2)}) %collective-permute-start.30) | collective-permute-done | bytes 245792 | tf_op jit(solution)/shard_map/ppermute | solution.py:127
  168.6 2.1 %collective-permute-done.35.other_up.other_low = bf16[2,24,3072]{2,1,0:T(8,128)(2,1)S(1)} collective-permute-done((bf16[2,24,3072]{2,1,0:T(8,128)(2,1)S(1)}, bf16[2,24,3072]{2,1,0:T(8,128)(2,1)S(1)}, u32[]{:S(2)}, u32[]{:S(2)}) %collective-permute-start.35) | collective-permute-done | bytes 294944 | tf_op jit(solution)/shard_map/ppermute | solution.py:127
  172.9 1.2 collective-permute-start.39
  174.2 2.6 %collective-permute-start.38 = (bf16[1,24,3072]{2,1,0:T(8,128)(2,1)S(1)}, bf16[1,24,3072]{2,1,0:T(8,128)(2,1)S(1)}, u32[]{:S(2)}, u32[]{:S(2)}) collective-permute-start(bf16[1,24,3072]{2,1,0:T(8,128)(2,1)S(1)} %get-tuple-element.264), channel_id=1, source_target_pairs={{0,16},{1,17},{2,18},{3,19},{4,20},{5,21},{6,22},{7,23},{8,24},{9,... | collective-permute-start | bytes 442376 | tf_op jit(solution)/shard_map/ppermute | solution.py:127
  178.4 5.5 %collective-permute-done.36 = bf16[1,24,1280]{2,1,0:T(8,128)(2,1)S(1)} collective-permute-done((bf16[1,24,1280]{2,1,0:T(8,128)(2,1)S(1)}, bf16[1,24,1280]{2,1,0:T(8,128)(2,1)S(1)}, u32[]{:S(2)}, u32[]{:S(2)}) %collective-permute-start.36) | collective-permute-done | bytes 61472 | tf_op jit(solution)/shard_map/ppermute | solution.py:127
  (135 shorter events, 28.2 us)
Async XLA Ops:
  0.7 5.9 %copy-start.14 = (bf16[96,768]{1,0:T(8,128)(2,1)S(1)}, bf16[96,768]{1,0:T(8,128)(2,1)}, u32[]{:S(2)}) copy-start(bf16[96,768]{1,0:T(8,128)(2,1)} %param.29) | copy-start | bytes 442372
  0.7 7.4 %copy-start.13 = (bf16[24,3072]{1,0:T(8,128)(2,1)S(1)}, bf16[24,3072]{1,0:T(8,128)(2,1)}, u32[]{:S(2)}) copy-start(bf16[24,3072]{1,0:T(8,128)(2,1)} %refs_1_.5) | copy-start | bytes 442372
  2.5 10.1 %collective-permute-start.2 = (bf16[1,24,2432]{2,1,0:T(8,128)(2,1)}, bf16[1,24,2432]{2,1,0:T(8,128)(2,1)S(1)}, u32[]{:S(2)}, u32[]{:S(2)}) collective-permute-start(bf16[1,24,2432]{2,1,0:T(8,128)(2,1)} %get-tuple-element.144.held), channel_id=1, source_target_pairs={{0,16},{1,17},{2,18},{3,19},{4,20},{5,21},{6,22},{7,23},{8,24},{9,... | collective-permute-start | bytes 350216 | tf_op jit(solution)/shard_map/ppermute | solution.py:127
  6.5 8.0 %collective-permute-start.1 = (bf16[1,96,768]{2,1,0:T(8,128)(2,1)S(1)}, bf16[1,96,768]{2,1,0:T(8,128)(2,1)S(1)}, u32[]{:S(2)}, u32[]{:S(2)}) collective-permute-start(bf16[1,96,768]{2,1,0:T(8,128)(2,1)S(1)} %bitcast.65), channel_id=1, source_target_pairs={{0,8},{1,9},{2,10},{3,11},{4,12},{5,13},{6,14},{7,15},{8,0},{9,1},... | collective-permute-start | bytes 442376 | tf_op jit(solution)/shard_map/ppermute | solution.py:127
  8.1 11.9 %collective-permute-start.5 = (bf16[1,24,1536]{2,1,0:T(8,128)(2,1)S(1)}, bf16[1,24,1536]{2,1,0:T(8,128)(2,1)S(1)}, u32[]{:S(2)}, u32[]{:S(2)}) collective-permute-start(bf16[1,24,1536]{2,1,0:T(8,128)(2,1)S(1)} %get-tuple-element.150.held), channel_id=1, source_target_pairs={{0,2},{1,5},{2,0},{3,7},{4,6},{5,1},{6,4},{7,3},{8,10},{9,13},{10,... | collective-permute-start | bytes 221192 | tf_op jit(solution)/shard_map/ppermute | solution.py:127
  9.7 7.6 %collective-permute-start = (bf16[1,24,2304]{2,1,0:T(8,128)(2,1)S(1)}, bf16[1,24,2304]{2,1,0:T(8,128)(2,1)S(1)}, u32[]{:S(2)}, u32[]{:S(2)}) collective-permute-start(bf16[1,24,2304]{2,1,0:T(8,128)(2,1)S(1)} %get-tuple-element.143.held), channel_id=1, source_target_pairs={{0,16},{1,17},{2,18},{3,19},{4,20},{5,21},{6,22},{7,23},{8,24},{9,... | collective-permute-start | bytes 331784 | tf_op jit(solution)/shard_map/ppermute | solution.py:127
  13.2 7.4 %collective-permute-start.4 = (bf16[2,24,2432]{2,1,0:T(8,128)(2,1)S(1)}, bf16[2,24,2432]{2,1,0:T(8,128)(2,1)S(1)}, u32[]{:S(2)}, u32[]{:S(2)}) collective-permute-start(bf16[2,24,2432]{2,1,0:T(8,128)(2,1)S(1)} %bitcast.61), channel_id=1, source_target_pairs={{0,8},{1,9},{2,10},{3,11},{4,12},{5,13},{6,14},{7,15},{8,0},{9,1},... | collective-permute-start | bytes 700424 | tf_op jit(solution)/shard_map/ppermute | solution.py:127
  17.9 8.0 %collective-permute-start.3 = (bf16[2,24,2304]{2,1,0:T(8,128)(2,1)S(1)}, bf16[2,24,2304]{2,1,0:T(8,128)(2,1)S(1)}, u32[]{:S(2)}, u32[]{:S(2)}) collective-permute-start(bf16[2,24,2304]{2,1,0:T(8,128)(2,1)S(1)} %bitcast.63), channel_id=1, source_target_pairs={{0,2},{1,5},{2,0},{3,7},{4,6},{5,1},{6,4},{7,3},{8,10},{9,13},{10,... | collective-permute-start | bytes 663560 | tf_op jit(solution)/shard_map/ppermute | solution.py:127
  19.5 10.4 %collective-permute-start.7 = (bf16[2,96,768]{2,1,0:T(8,128)(2,1)S(1)}, bf16[2,96,768]{2,1,0:T(8,128)(2,1)S(1)}, u32[]{:S(2)}, u32[]{:S(2)}) collective-permute-start(bf16[2,96,768]{2,1,0:T(8,128)(2,1)S(1)} %bitcast.57), channel_id=1, source_target_pairs={{0,2},{1,5},{2,0},{3,7},{4,6},{5,1},{6,4},{7,3},{8,10},{9,13},{10,... | collective-permute-start | bytes 884744 | tf_op jit(solution)/shard_map/ppermute | solution.py:127
  20.6 8.4 %copy-start.9 = (s32[394]{0:T(512)S(1)}, s32[394]{0:T(512)}, u32[]{:S(2)}) copy-start(s32[394]{0:T(512)} %refs_1_.7) | copy-start | bytes 4732
  20.6 8.4 %copy-start.11 = (bf16[394,768]{1,0:T(8,128)(2,1)S(1)}, bf16[394,768]{1,0:T(8,128)(2,1)}, u32[]{:S(2)}) copy-start(bf16[394,768]{1,0:T(8,128)(2,1)} %refs_1_.6) | copy-start | bytes 1815556
  20.6 8.4 %copy-start.12 = (bf16[394,768]{1,0:T(8,128)(2,1)S(1)}, bf16[394,768]{1,0:T(8,128)(2,1)}, u32[]{:S(2)}) copy-start(bf16[394,768]{1,0:T(8,128)(2,1)} %refs_2_.3) | copy-start | bytes 1815556
  21.2 10.8 %collective-permute-start.6 = (bf16[4,24,2432]{2,1,0:T(8,128)(2,1)S(1)}, bf16[4,24,2432]{2,1,0:T(8,128)(2,1)S(1)}, u32[]{:S(2)}, u32[]{:S(2)}) collective-permute-start(bf16[4,24,2432]{2,1,0:T(8,128)(2,1)S(1)} %bitcast.53), channel_id=1, source_target_pairs={{0,2},{1,5},{2,0},{3,7},{4,6},{5,1},{6,4},{7,3},{8,10},{9,13},{10,... | collective-permute-start | bytes 1400840 | tf_op jit(solution)/shard_map/ppermute | solution.py:127
  22.8 11.5 %collective-permute-start.10 = (bf16[2,24,1536]{2,1,0:T(8,128)(2,1)S(1)}, bf16[2,24,1536]{2,1,0:T(8,128)(2,1)S(1)}, u32[]{:S(2)}, u32[]{:S(2)}) collective-permute-start(bf16[2,24,1536]{2,1,0:T(8,128)(2,1)S(1)} %bitcast.67), channel_id=1, source_target_pairs={{0,16},{1,17},{2,18},{3,19},{4,20},{5,21},{6,22},{7,23},{8,24},{9,... | collective-permute-start | bytes 442376 | tf_op jit(solution)/shard_map/ppermute | solution.py:127
  26.5 21.4 %collective-permute-start.9 = (bf16[4,24,2304]{2,1,0:T(8,128)(2,1)S(1)}, bf16[4,24,2304]{2,1,0:T(8,128)(2,1)S(1)}, u32[]{:S(2)}, u32[]{:S(2)}) collective-permute-start(bf16[4,24,2304]{2,1,0:T(8,128)(2,1)S(1)} %bitcast.55), channel_id=1, source_target_pairs={{0,8},{1,9},{2,10},{3,11},{4,12},{5,13},{6,14},{7,15},{8,0},{9,1},... | collective-permute-start | bytes 1327112 | tf_op jit(solution)/shard_map/ppermute | solution.py:127
  30.4 28.1 %collective-permute-start.12 = (bf16[4,96,768]{2,1,0:T(8,128)(2,1)S(1)}, bf16[4,96,768]{2,1,0:T(8,128)(2,1)S(1)}, u32[]{:S(2)}, u32[]{:S(2)}) collective-permute-start(bf16[4,96,768]{2,1,0:T(8,128)(2,1)S(1)} %bitcast.49), channel_id=1, source_target_pairs={{0,16},{1,17},{2,18},{3,19},{4,20},{5,21},{6,22},{7,23},{8,24},{9,... | collective-permute-start | bytes 1769480 | tf_op jit(solution)/shard_map/ppermute | solution.py:127
  32.7 16.4 %collective-permute-start.8 = (bf16[8,24,2432]{2,1,0:T(8,128)(2,1)S(1)}, bf16[8,24,2432]{2,1,0:T(8,128)(2,1)S(1)}, u32[]{:S(2)}, u32[]{:S(2)}) collective-permute-start(bf16[8,24,2432]{2,1,0:T(8,128)(2,1)S(1)} %bitcast.47), channel_id=1, source_target_pairs={{0,4},{1,3},{2,6},{3,1},{4,0},{5,7},{6,2},{7,5},{8,12},{9,11},{10,... | collective-permute-start | bytes 2801672 | tf_op jit(solution)/shard_map/ppermute | solution.py:127
  34.9 15.6 %collective-permute-start.13 = (bf16[4,24,1536]{2,1,0:T(8,128)(2,1)S(1)}, bf16[4,24,1536]{2,1,0:T(8,128)(2,1)S(1)}, u32[]{:S(2)}, u32[]{:S(2)}) collective-permute-start(bf16[4,24,1536]{2,1,0:T(8,128)(2,1)S(1)} %bitcast.59), channel_id=1, source_target_pairs={{0,4},{1,3},{2,6},{3,1},{4,0},{5,7},{6,2},{7,5},{8,12},{9,11},{10,... | collective-permute-start | bytes 884744 | tf_op jit(solution)/shard_map/ppermute | solution.py:127
  48.5 19.2 %collective-permute-start.14 = (bf16[8,24,2304]{2,1,0:T(8,128)(2,1)S(1)}, bf16[8,24,2304]{2,1,0:T(8,128)(2,1)S(1)}, u32[]{:S(2)}, u32[]{:S(2)}) collective-permute-start(bf16[8,24,2304]{2,1,0:T(8,128)(2,1)S(1)} %bitcast.43), channel_id=1, source_target_pairs={{0,4},{1,3},{2,6},{3,1},{4,0},{5,7},{6,2},{7,5},{8,12},{9,11},{10,... | collective-permute-start | bytes 2654216 | tf_op jit(solution)/shard_map/ppermute | solution.py:127
  49.8 11.1 %collective-permute-start.11 = (bf16[16,24,2432]{2,1,0:T(8,128)(2,1)S(1)}, bf16[16,24,2432]{2,1,0:T(8,128)(2,1)S(1)}, u32[]{:S(2)}, u32[]{:S(2)}) collective-permute-start(bf16[16,24,2432]{2,1,0:T(8,128)(2,1)S(1)} %bitcast.40), channel_id=1, source_target_pairs={{0,1},{1,0},{2,3},{3,2},{4,5},{5,4},{6,7},{7,6},{8,9},{9,8},{10,11... | collective-permute-start | bytes 5603336 | tf_op jit(solution)/shard_map/ppermute | solution.py:127
  51.0 20.0 %collective-permute-start.16 = (bf16[8,24,1536]{2,1,0:T(8,128)(2,1)S(1)}, bf16[8,24,1536]{2,1,0:T(8,128)(2,1)S(1)}, u32[]{:S(2)}, u32[]{:S(2)}) collective-permute-start(bf16[8,24,1536]{2,1,0:T(8,128)(2,1)S(1)} %bitcast.51), channel_id=1, source_target_pairs={{0,8},{1,9},{2,10},{3,11},{4,12},{5,13},{6,14},{7,15},{8,0},{9,1},... | collective-permute-start | bytes 1769480 | tf_op jit(solution)/shard_map/ppermute | solution.py:127
  60.1 16.5 %collective-permute-start.18 = (bf16[8,96,768]{2,1,0:T(8,128)(2,1)}, bf16[8,96,768]{2,1,0:T(8,128)(2,1)}, u32[]{:S(2)}, u32[]{:S(2)}) collective-permute-start(bf16[8,96,768]{2,1,0:T(8,128)(2,1)} %bitcast.21.held), channel_id=1, source_target_pairs={{0,4},{1,3},{2,6},{3,1},{4,0},{5,7},{6,2},{7,5},{8,12},{9,11},{10,... | collective-permute-start | bytes 3538952 | tf_op jit(solution)/shard_map/ppermute | solution.py:127
  60.9 6.7 %copy-start.1 = (bf16[16,24,2432]{2,1,0:T(8,128)(2,1)}, bf16[16,24,2432]{2,1,0:T(8,128)(2,1)S(1)}, u32[]{:S(2)}) copy-start(bf16[16,24,2432]{2,1,0:T(8,128)(2,1)S(1)} %collective-permute-done.11.refs_3_.refs_8_) | copy-start | bytes 5603332
  69.9 8.8 %collective-permute-start.15 = (bf16[16,24,2304]{2,1,0:T(8,128)(2,1)}, bf16[16,24,2304]{2,1,0:T(8,128)(2,1)}, u32[]{:S(2)}, u32[]{:S(2)}) collective-permute-start(bf16[16,24,2304]{2,1,0:T(8,128)(2,1)} %bitcast.17.refs_4_.refs_5_), channel_id=1, source_target_pairs={{0,1},{1,0},{2,3},{3,2},{4,5},{5,4},{6,7},{7,6},{8,9},{9,8},{10,11... | collective-permute-start | bytes 5308424 | tf_op jit(solution)/shard_map/ppermute | solution.py:127
  72.7 6.0 %collective-permute-start.17 = (bf16[16,24,1536]{2,1,0:T(8,128)(2,1)}, bf16[16,24,1536]{2,1,0:T(8,128)(2,1)}, u32[]{:S(2)}, u32[]{:S(2)}) collective-permute-start(bf16[16,24,1536]{2,1,0:T(8,128)(2,1)} %bitcast.19.refs_6_.refs_7_), channel_id=1, source_target_pairs={{0,1},{1,0},{2,3},{3,2},{4,5},{5,4},{6,7},{7,6},{8,9},{9,8},{10,11... | collective-permute-start | bytes 3538952 | tf_op jit(solution)/shard_map/ppermute | solution.py:127
  78.6 13.1 %copy-start = (bf16[2,8,96,768]{3,2,1,0:T(8,128)(2,1)}, bf16[2,8,96,768]{3,2,1,0:T(8,128)(2,1)S(1)}, u32[]{:S(2)}) copy-start(bf16[2,8,96,768]{3,2,1,0:T(8,128)(2,1)S(1)} %get-tuple-element.186) | copy-start | bytes 7077892
  78.6 13.2 %collective-permute-start.19 = (bf16[16,96,768]{2,1,0:T(8,128)(2,1)S(1)}, bf16[16,96,768]{2,1,0:T(8,128)(2,1)S(1)}, u32[]{:S(2)}, u32[]{:S(2)}) collective-permute-start(bf16[16,96,768]{2,1,0:T(8,128)(2,1)S(1)} %bitcast.37), channel_id=1, source_target_pairs={{0,1},{1,0},{2,3},{3,2},{4,5},{5,4},{6,7},{7,6},{8,9},{9,8},{10,11... | collective-permute-start | bytes 7077896 | tf_op jit(solution)/shard_map/ppermute | solution.py:127
  91.7 10.3 %collective-permute-start.20 = (bf16[2,2,2,2,96,768]{5,4,3,2,1,0:T(8,128)(2,1)S(1)}, bf16[2,2,2,2,96,768]{5,4,3,2,1,0:T(8,128)(2,1)S(1)}, u32[]{:S(2)}, u32[]{:S(2)}) collective-permute-start(bf16[2,2,2,2,96,768]{5,4,3,2,1,0:T(8,128)(2,1)S(1)} %get-tuple-element.192), channel_id=1, source_target_pairs={{0,1},{1,0},{2,3},{3,2},{4,5},{5,4},{6,7},{7,6},{8,9},{9,8},{10,11... | collective-permute-start | bytes 7077896 | tf_op jit(solution)/shard_map/ppermute | solution.py:127
  101.5 11.3 %collective-permute-start.21 = (bf16[16,24,3072]{2,1,0:T(8,128)(2,1)S(1)}, bf16[16,24,3072]{2,1,0:T(8,128)(2,1)S(1)}, u32[]{:S(2)}, u32[]{:S(2)}) collective-permute-start(bf16[16,24,3072]{2,1,0:T(8,128)(2,1)S(1)} %get-tuple-element.203), channel_id=1, source_target_pairs={{0,1},{1,0},{2,3},{3,2},{4,5},{5,4},{6,7},{7,6},{8,9},{9,8},{10,11... | collective-permute-start | bytes 7077896 | tf_op jit(solution)/shard_map/ppermute | solution.py:127
  103.1 17.9 %collective-permute-start.22 = (bf16[8,96,768]{2,1,0:T(8,128)(2,1)S(1)}, bf16[8,96,768]{2,1,0:T(8,128)(2,1)S(1)}, u32[]{:S(2)}, u32[]{:S(2)}) collective-permute-start(bf16[8,96,768]{2,1,0:T(8,128)(2,1)S(1)} %get-tuple-element.208), channel_id=1, source_target_pairs={{0,2},{1,5},{2,0},{3,7},{4,6},{5,1},{6,4},{7,3},{8,10},{9,13},{10,... | collective-permute-start | bytes 3538952 | tf_op jit(solution)/shard_map/ppermute | solution.py:127
  114.2 17.9 %collective-permute-start.23 = (bf16[8,24,3072]{2,1,0:T(8,128)(2,1)S(1)}, bf16[8,24,3072]{2,1,0:T(8,128)(2,1)S(1)}, u32[]{:S(2)}, u32[]{:S(2)}) collective-permute-start(bf16[8,24,3072]{2,1,0:T(8,128)(2,1)S(1)} %get-tuple-element.217), channel_id=1, source_target_pairs={{0,2},{1,5},{2,0},{3,7},{4,6},{5,1},{6,4},{7,3},{8,10},{9,13},{10,... | collective-permute-start | bytes 3538952 | tf_op jit(solution)/shard_map/ppermute | solution.py:127
  121.0 7.6 %collective-permute-start.24 = (bf16[16,24,1920]{2,1,0:T(8,128)(2,1)S(1)}, bf16[16,24,1920]{2,1,0:T(8,128)(2,1)S(1)}, u32[]{:S(2)}, u32[]{:S(2)}) collective-permute-start(bf16[16,24,1920]{2,1,0:T(8,128)(2,1)S(1)} %get-tuple-element.219), channel_id=1, source_target_pairs={{0,1},{1,0},{2,3},{3,2},{4,5},{5,4},{6,7},{7,6},{8,9},{9,8},{10,11... | collective-permute-start | bytes 4423688 | tf_op jit(solution)/shard_map/ppermute | solution.py:127
  122.0 17.4 %collective-permute-start.27 = (bf16[4,96,768]{2,1,0:T(8,128)(2,1)S(1)}, bf16[4,96,768]{2,1,0:T(8,128)(2,1)S(1)}, u32[]{:S(2)}, u32[]{:S(2)}) collective-permute-start(bf16[4,96,768]{2,1,0:T(8,128)(2,1)S(1)} %get-tuple-element.228), channel_id=1, source_target_pairs={{0,8},{1,9},{2,10},{3,11},{4,12},{5,13},{6,14},{7,15},{8,0},{9,1},... | collective-permute-start | bytes 1769480 | tf_op jit(solution)/shard_map/ppermute | solution.py:127
  132.9 28.9 %collective-permute-start.31 = (bf16[4,24,3072]{2,1,0:T(8,128)(2,1)S(1)}, bf16[4,24,3072]{2,1,0:T(8,128)(2,1)S(1)}, u32[]{:S(2)}, u32[]{:S(2)}) collective-permute-start(bf16[4,24,3072]{2,1,0:T(8,128)(2,1)S(1)} %get-tuple-element.244), channel_id=1, source_target_pairs={{0,8},{1,9},{2,10},{3,11},{4,12},{5,13},{6,14},{7,15},{8,0},{9,1},... | collective-permute-start | bytes 1769480 | tf_op jit(solution)/shard_map/ppermute | solution.py:127
  133.3 11.5 %collective-permute-start.26 = (bf16[8,24,1920]{2,1,0:T(8,128)(2,1)S(1)}, bf16[8,24,1920]{2,1,0:T(8,128)(2,1)S(1)}, u32[]{:S(2)}, u32[]{:S(2)}) collective-permute-start(bf16[8,24,1920]{2,1,0:T(8,128)(2,1)S(1)} %get-tuple-element.226), channel_id=1, source_target_pairs={{0,2},{1,5},{2,0},{3,7},{4,6},{5,1},{6,4},{7,3},{8,10},{9,13},{10,... | collective-permute-start | bytes 2211848 | tf_op jit(solution)/shard_map/ppermute | solution.py:127
  139.4 6.2 %collective-permute-start.25 = (bf16[16,24,1280]{2,1,0:T(8,128)(2,1)S(1)}, bf16[16,24,1280]{2,1,0:T(8,128)(2,1)S(1)}, u32[]{:S(2)}, u32[]{:S(2)}) collective-permute-start(bf16[16,24,1280]{2,1,0:T(8,128)(2,1)S(1)} %get-tuple-element.224), channel_id=1, source_target_pairs={{0,1},{1,0},{2,3},{3,2},{4,5},{5,4},{6,7},{7,6},{8,9},{9,8},{10,11... | collective-permute-start | bytes 2949128 | tf_op jit(solution)/shard_map/ppermute | solution.py:127
  145.5 6.4 %copy-start.10 = (s32[394]{0:T(512)S(1)}, s32[394]{0:T(512)}, u32[]{:S(2)}) copy-start(s32[394]{0:T(512)} %refs_1_.7) | copy-start | bytes 4732
  146.4 14.1 %collective-permute-start.28 = (bf16[8,24,1280]{2,1,0:T(8,128)(2,1)S(1)}, bf16[8,24,1280]{2,1,0:T(8,128)(2,1)S(1)}, u32[]{:S(2)}, u32[]{:S(2)}) collective-permute-start(bf16[8,24,1280]{2,1,0:T(8,128)(2,1)S(1)} %get-tuple-element.236), channel_id=1, source_target_pairs={{0,2},{1,5},{2,0},{3,7},{4,6},{5,1},{6,4},{7,3},{8,10},{9,13},{10,... | collective-permute-start | bytes 1474568 | tf_op jit(solution)/shard_map/ppermute | solution.py:127
  148.0 10.6 %collective-permute-start.29 = (bf16[4,24,1920]{2,1,0:T(8,128)(2,1)S(1)}, bf16[4,24,1920]{2,1,0:T(8,128)(2,1)S(1)}, u32[]{:S(2)}, u32[]{:S(2)}) collective-permute-start(bf16[4,24,1920]{2,1,0:T(8,128)(2,1)S(1)} %get-tuple-element.238), channel_id=1, source_target_pairs={{0,4},{1,3},{2,6},{3,1},{4,0},{5,7},{6,2},{7,5},{8,12},{9,11},{10,... | collective-permute-start | bytes 1105928 | tf_op jit(solution)/shard_map/ppermute | solution.py:127
  148.5 23.8 %collective-permute-start.33 = (bf16[2,96,768]{2,1,0:T(8,128)(2,1)S(1)}, bf16[2,96,768]{2,1,0:T(8,128)(2,1)S(1)}, u32[]{:S(2)}, u32[]{:S(2)}) collective-permute-start(bf16[2,96,768]{2,1,0:T(8,128)(2,1)S(1)} %get-tuple-element.250), channel_id=1, source_target_pairs={{0,16},{1,17},{2,18},{3,19},{4,20},{5,21},{6,22},{7,23},{8,24},{9,... | collective-permute-start | bytes 884744 | tf_op jit(solution)/shard_map/ppermute | solution.py:127
  159.2 12.0 %collective-permute-start.34 = (bf16[2,24,1920]{2,1,0:T(8,128)(2,1)S(1)}, bf16[2,24,1920]{2,1,0:T(8,128)(2,1)S(1)}, u32[]{:S(2)}, u32[]{:S(2)}) collective-permute-start(bf16[2,24,1920]{2,1,0:T(8,128)(2,1)S(1)} %get-tuple-element.252), channel_id=1, source_target_pairs={{0,16},{1,17},{2,18},{3,19},{4,20},{5,21},{6,22},{7,23},{8,24},{9,... | collective-permute-start | bytes 552968 | tf_op jit(solution)/shard_map/ppermute | solution.py:127
  161.2 6.3 %collective-permute-start.30 = (bf16[4,24,1280]{2,1,0:T(8,128)(2,1)S(1)}, bf16[4,24,1280]{2,1,0:T(8,128)(2,1)S(1)}, u32[]{:S(2)}, u32[]{:S(2)}) collective-permute-start(bf16[4,24,1280]{2,1,0:T(8,128)(2,1)S(1)} %get-tuple-element.242), channel_id=1, source_target_pairs={{0,4},{1,3},{2,6},{3,1},{4,0},{5,7},{6,2},{7,5},{8,12},{9,11},{10,... | collective-permute-start | bytes 737288 | tf_op jit(solution)/shard_map/ppermute | solution.py:127
  162.5 8.1 %collective-permute-start.35 = (bf16[2,24,3072]{2,1,0:T(8,128)(2,1)S(1)}, bf16[2,24,3072]{2,1,0:T(8,128)(2,1)S(1)}, u32[]{:S(2)}, u32[]{:S(2)}) collective-permute-start(bf16[2,24,3072]{2,1,0:T(8,128)(2,1)S(1)} %get-tuple-element.254), channel_id=1, source_target_pairs={{0,4},{1,3},{2,6},{3,1},{4,0},{5,7},{6,2},{7,5},{8,12},{9,11},{10,... | collective-permute-start | bytes 884744 | tf_op jit(solution)/shard_map/ppermute | solution.py:127
  168.1 8.6 %collective-permute-start.32 = (bf16[2,24,1280]{2,1,0:T(8,128)(2,1)S(1)}, bf16[2,24,1280]{2,1,0:T(8,128)(2,1)S(1)}, u32[]{:S(2)}, u32[]{:S(2)}) collective-permute-start(bf16[2,24,1280]{2,1,0:T(8,128)(2,1)S(1)} %get-tuple-element.248), channel_id=1, source_target_pairs={{0,8},{1,9},{2,10},{3,11},{4,12},{5,13},{6,14},{7,15},{8,0},{9,1},... | collective-permute-start | bytes 368648 | tf_op jit(solution)/shard_map/ppermute | solution.py:127
  171.9 5.9 %collective-permute-start.37 = (bf16[1,24,1920]{2,1,0:T(8,128)(2,1)S(1)}, bf16[1,24,1920]{2,1,0:T(8,128)(2,1)S(1)}, u32[]{:S(2)}, u32[]{:S(2)}) collective-permute-start(bf16[1,24,1920]{2,1,0:T(8,128)(2,1)S(1)} %get-tuple-element.262), channel_id=1, source_target_pairs={{0,8},{1,9},{2,10},{3,11},{4,12},{5,13},{6,14},{7,15},{8,0},{9,1},... | collective-permute-start | bytes 276488 | tf_op jit(solution)/shard_map/ppermute | solution.py:127
  172.9 12.6 %collective-permute-start.39 = (bf16[1,96,768]{2,1,0:T(8,128)(2,1)S(1)}, bf16[1,96,768]{2,1,0:T(8,128)(2,1)S(1)}, u32[]{:S(2)}, u32[]{:S(2)}) collective-permute-start(bf16[1,96,768]{2,1,0:T(8,128)(2,1)S(1)} %get-tuple-element.266), channel_id=1, source_target_pairs={{0,4},{1,3},{2,6},{3,1},{4,0},{5,7},{6,2},{7,5},{8,12},{9,11},{10,... | collective-permute-start | bytes 442376 | tf_op jit(solution)/shard_map/ppermute | solution.py:127
  174.2 12.1 %collective-permute-start.38 = (bf16[1,24,3072]{2,1,0:T(8,128)(2,1)S(1)}, bf16[1,24,3072]{2,1,0:T(8,128)(2,1)S(1)}, u32[]{:S(2)}, u32[]{:S(2)}) collective-permute-start(bf16[1,24,3072]{2,1,0:T(8,128)(2,1)S(1)} %get-tuple-element.264), channel_id=1, source_target_pairs={{0,16},{1,17},{2,18},{3,19},{4,20},{5,21},{6,22},{7,23},{8,24},{9,... | collective-permute-start | bytes 442376 | tf_op jit(solution)/shard_map/ppermute | solution.py:127
  177.3 6.5 %collective-permute-start.36 = (bf16[1,24,1280]{2,1,0:T(8,128)(2,1)S(1)}, bf16[1,24,1280]{2,1,0:T(8,128)(2,1)S(1)}, u32[]{:S(2)}, u32[]{:S(2)}) collective-permute-start(bf16[1,24,1280]{2,1,0:T(8,128)(2,1)S(1)} %get-tuple-element.260), channel_id=1, source_target_pairs={{0,16},{1,17},{2,18},{3,19},{4,20},{5,21},{6,22},{7,23},{8,24},{9,... | collective-permute-start | bytes 184328 | tf_op jit(solution)/shard_map/ppermute | solution.py:127
  (11 other events, 34.3 us)

commit v3 on v2

--- a/solution.py
+++ b/solution.py
@@ -14,7 +14,7 @@
 LEN = 197
 SLOT = 208
 SPEED = 1.15e9
-LENGTHS = (1, 8, 0.25, 0.5, 24, 1, 1, 24, 0.25, 1, 2, 0.25, 1, 8, 3, 24, 1, 0.25, 0.25, 8, 2, 6, 0.25, 12, 1, 2, 1, 16, 2, 1, 32, 2, 32, 0.25, 4, 0.5, 0.25, 0.5, 6, 24, 0.5, 2, 1, 8)
+LENGTHS = (1, 8, 1, 0.5, 24, 1, 1, 24, 0.25, 1, 2, 0.25, 1, 8, 3, 24, 1, 0.25, 0.25, 8, 2, 6, 12, 32, 1, 2, 1, 16, 2, 1, 32, 2, 1, 32, 4, 0.5, 2, 0.5, 6, 8, 0.5, 2, 24, 12)
 ORDERS = {'a': 'fnxx', 'b': 'fxnx', 'e': 'xfxn', 'c': 'nxfx', 'd': 'xnfx', 'u': 'xnxf', 'i': 'xxfn', 'j': 'xxnf'}
 GATHERS = ("a", "b", "e", "c")
 FIRST = 2

time: 187 us -> 183 us (0.979)
  waiting for transfers between devices: 49.2 us -> 46 us
    ppermute x40, waiting for transfers between devices: 49.2 us -> 46 us  [swap(): return lax.ppermute(value, 'dp', pairs)]
  transfers between devices with their start and end apart: 40 -> 40, of which waited for: 14 -> 15; matrix products, arithmetic and copies ran while one was open for 2% -> 2% of each run, Pallas kernels for 47% -> 47%
where the time goes in v3:
time: 183 us
  Pallas kernels  88.1 us (48%)
  waiting for transfers between devices  46 us (25%)
  starting transfers between devices  42.1 us (23%)
  local copies, waits for them, and re-layouts  3.76 us (2%)
    pallas_call x12, Pallas kernels, launch(): pl.pallas_call(kernel, out_shape=outs + (TOKEN,), in_specs=list(specs) +...  61.5 us
    ppermute x40, waiting for transfers between devices, swap(): return lax.ppermute(value, 'dp', pairs)  46 us
    ppermute x40, starting transfers between devices, swap(): return lax.ppermute(value, 'dp', pairs)  42.1 us
    pallas_call x16, Pallas kernels, kernel(): pl.pallas_call(body, out_shape=(jax.ShapeDtypeStruct((2, count, rows, wid...  13.9 us
    pallas_call x16, Pallas kernels, kernel(): pl.pallas_call(body, grid_spec=pltpu.PrefetchScalarGridSpec(num_scalar_pr...  12.7 us
  transfers between devices with their start and end apart: 40, of which 15 were waited for; matrix products, arithmetic and copies ran while one was open for 2% of the time, Pallas kernels for 47%

profile of v3, /device:TPU:0, one launch (start us, length us, event | category | flops | bytes accessed | tf_op | source)
XLA Modules:
  0.0 182.8 jit_solution(9759136165266911015)
XLA Ops:
  0.7 1.8 line_up.1
  2.5 4.0 %collective-permute-start.2 = (bf16[1,24,2432]{2,1,0:T(8,128)(2,1)}, bf16[1,24,2432]{2,1,0:T(8,128)(2,1)S(1)}, u32[]{:S(2)}, u32[]{:S(2)}) collective-permute-start(bf16[1,24,2432]{2,1,0:T(8,128)(2,1)} %get-tuple-element.144.held), channel_id=1, source_target_pairs={{0,16},{1,17},{2,18},{3,19},{4,20},{5,21},{6,22},{7,23},{8,24},{9,... | collective-permute-start | bytes 350216 | tf_op jit(solution)/shard_map/ppermute | solution.py:127
  6.5 1.6 collective-permute-start.5
  8.1 1.6 collective-permute-start.1
  10.2 2.4 %collective-permute-done.2.other = bf16[1,24,2432]{2,1,0:T(8,128)(2,1)S(1)} collective-permute-done((bf16[1,24,2432]{2,1,0:T(8,128)(2,1)}, bf16[1,24,2432]{2,1,0:T(8,128)(2,1)S(1)}, u32[]{:S(2)}, u32[]{:S(2)}) %collective-permute-start.2) | collective-permute-done | bytes 116768 | tf_op jit(solution)/shard_map/ppermute | solution.py:127
  13.2 1.6 collective-permute-start.4
  14.7 3.0 %collective-permute-done.1.other = bf16[1,96,768]{2,1,0:T(8,128)(2,1)S(1)} collective-permute-done((bf16[1,96,768]{2,1,0:T(8,128)(2,1)S(1)}, bf16[1,96,768]{2,1,0:T(8,128)(2,1)S(1)}, u32[]{:S(2)}, u32[]{:S(2)}) %collective-permute-start.1) | collective-permute-done | bytes 147488 | tf_op jit(solution)/shard_map/ppermute | solution.py:127
  18.9 1.2 collective-permute-start.3
  22.4 1.6 collective-permute-start.6
  24.0 1.8 collective-permute-start.10
  26.4 2.5 %collective-permute-start.9 = (bf16[4,24,2304]{2,1,0:T(8,128)(2,1)S(1)}, bf16[4,24,2304]{2,1,0:T(8,128)(2,1)S(1)}, u32[]{:S(2)}, u32[]{:S(2)}) collective-permute-start(bf16[4,24,2304]{2,1,0:T(8,128)(2,1)S(1)} %bitcast.54), channel_id=1, source_target_pairs={{0,8},{1,9},{2,10},{3,11},{4,12},{5,13},{6,14},{7,15},{8,0},{9,1},... | collective-permute-start | bytes 1327112 | tf_op jit(solution)/shard_map/ppermute | solution.py:127
  30.5 2.6 %collective-permute-done.6.other = bf16[4,24,2432]{2,1,0:T(8,128)(2,1)S(1)} collective-permute-done((bf16[4,24,2432]{2,1,0:T(8,128)(2,1)S(1)}, bf16[4,24,2432]{2,1,0:T(8,128)(2,1)S(1)}, u32[]{:S(2)}, u32[]{:S(2)}) %collective-permute-start.6) | collective-permute-done | bytes 466976 | tf_op jit(solution)/shard_map/ppermute | solution.py:127
  34.8 1.6 collective-permute-start.13
  36.4 11.4 %collective-permute-done.9.other = bf16[4,24,2304]{2,1,0:T(8,128)(2,1)S(1)} collective-permute-done((bf16[4,24,2304]{2,1,0:T(8,128)(2,1)S(1)}, bf16[4,24,2304]{2,1,0:T(8,128)(2,1)S(1)}, u32[]{:S(2)}, u32[]{:S(2)}) %collective-permute-start.9) | collective-permute-done | bytes 442400 | tf_op jit(solution)/shard_map/ppermute | solution.py:127
  51.2 7.0 %collective-permute-done.12.other = bf16[4,96,768]{2,1,0:T(8,128)(2,1)S(1)} collective-permute-done((bf16[4,96,768]{2,1,0:T(8,128)(2,1)S(1)}, bf16[4,96,768]{2,1,0:T(8,128)(2,1)S(1)}, u32[]{:S(2)}, u32[]{:S(2)}) %collective-permute-start.12) | collective-permute-done | bytes 589856 | tf_op jit(solution)/shard_map/ppermute | solution.py:127
  58.8 1.0 collective-permute-start.18
  59.8 6.7 %attend.1 = (bf16[416,768]{1,0:T(8,128)(2,1)S(1)}, bf16[416,2304]{1,0:T(8,128)(2,1)S(1)}, bf16[416,768]{1,0:T(8,128)(2,1)S(1)}, f32[416,128]{1,0:T(8,128)S(1)}, f32[16,768]{1,0:T(8,128)S(1)}, /*index=5*/f32[8,128]{1,0:T(8,128)}) custom-call(s32[5]{0:T(128)S(1)} %stack.39.place.refs_0_, bf16[416,768]{1,0:T(8,128)(2,1)S(1)} %get-tuple-element.155.refs_1_, ...), custom_call_target="tpu_custom_call" | custom-call | flops 287500000 | bytes 768 | tf_op jit(solution)/shard_map/attend/pallas_call | solution.py:576
  66.6 2.3 %pair.29 = (bf16[2,8,24,2304]{3,2,1,0:T(8,128)(2,1)}, f32[8,128]{1,0:T(8,128)}) custom-call(s32[5]{0:T(128)S(1)} %stack.39.place.refs_0_, bf16[8,24,2304]{2,1,0:T(8,128)(2,1)S(1)} %bitcast.41, bf16[8,24,2304]{2,1,0:T(8,128)(2,1)S(1)} %collective-permute-done.14.other, f32[8,128]{1,0:T(8,128)} %get-tuple-element.175.refs_0_), custom_call_target="tpu_custom_call" | custom-call | flops 287500000 | bytes 768 | tf_op jit(solution)/shard_map/pair/pallas_call | solution.py:145
  68.9 1.8 collective-permute-done.16.other
  70.7 1.7 pair.30
  72.5 2.6 %collective-permute-done.18.other = bf16[8,96,768]{2,1,0:T(8,128)(2,1)S(1)} collective-permute-done((bf16[8,96,768]{2,1,0:T(8,128)(2,1)S(1)}, bf16[8,96,768]{2,1,0:T(8,128)(2,1)S(1)}, u32[]{:S(2)}, u32[]{:S(2)}) %collective-permute-start.18) | collective-permute-done | bytes 1179680 | tf_op jit(solution)/shard_map/ppermute | solution.py:127
  75.1 2.3 %pair.31 = (bf16[2,8,96,768]{3,2,1,0:T(8,128)(2,1)}, f32[8,128]{1,0:T(8,128)}) custom-call(s32[5]{0:T(128)S(1)} %stack.39.place.refs_0_, bf16[8,96,768]{2,1,0:T(8,128)(2,1)S(1)} %bitcast.45, bf16[8,96,768]{2,1,0:T(8,128)(2,1)S(1)} %collective-permute-done.18.other, f32[8,128]{1,0:T(8,128)} %get-tuple-element.182.refs_0_), custom_call_target="tpu_custom_call" | custom-call | flops 2300000000 | bytes 768 | tf_op jit(solution)/shard_map/pair/pallas_call | solution.py:145
  77.7 1.1 copy-done.7
  78.7 12.1 %up.1 = (f32[416,768]{1,0:T(8,128)S(1)}, bf16[416,768]{1,0:T(8,128)(2,1)S(1)}, bf16[416,3072]{1,0:T(8,128)(2,1)}, f32[416,3072]{1,0:T(8,128)}, bf16[2,2,2,2,96,7...) custom-call(s32[5]{0:T(128)S(1)} %stack.39.place.refs_0_, ...), custom_call_target="tpu_custom_call" | custom-call | flops 6899999744 | bytes 768 | tf_op jit(solution)/shard_map/up/pallas_call | solution.py:576
  91.3 8.4 %slope.1 = (bf16[416,3072]{1,0:T(8,128)(2,1)}, bf16[16,24,3072]{2,1,0:T(8,128)(2,1)S(1)}, bf16[16,24,3072]{2,1,0:T(8,128)(2,1)S(1)}, f32[768,128]{1,0:T(8,128)S(1)}, f32[8,128]{1,0:T(8,128)}) custom-call(s32[5]{0:T(128)S(1)} %stack.39.place.refs_0_, bf16[416,768]{1,0:T(8,128)(2,1)S(1)} %get-tuple-element.173.refs_3_.refs_1_, ...), custom_call_target="tpu_custom_call" | custom-call | flops 13799999488 | bytes 768 | tf_op jit(solution)/shard_map/slope/pallas_call | solution.py:576
  99.7 1.2 halve.16
  100.9 1.9 %collective-permute-start.22 = (bf16[8,96,768]{2,1,0:T(8,128)(2,1)S(1)}, bf16[8,96,768]{2,1,0:T(8,128)(2,1)S(1)}, u32[]{:S(2)}, u32[]{:S(2)}) collective-permute-start(bf16[8,96,768]{2,1,0:T(8,128)(2,1)S(1)} %get-tuple-element.208), channel_id=1, source_target_pairs={{0,2},{1,5},{2,0},{3,7},{4,6},{5,1},{6,4},{7,3},{8,10},{9,13},{10,... | collective-permute-start | bytes 3538952 | tf_op jit(solution)/shard_map/ppermute | solution.py:127
  102.8 8.1 %middle.1 = (bf16[416,768]{1,0:T(8,128)(2,1)S(1)}, f32[416,768]{1,0:T(8,128)S(1)}, bf16[16,24,768]{2,1,0:T(8,128)(2,1)S(1)}, bf16[16,24,768]{2,1,0:T(8,128)(2,1)...) custom-call(s32[5]{0:T(128)S(1)} %stack.39.place.refs_0_, bf16[416,3072]{1,0:T(8,128)(2,1)} %get-tuple-element.190.refs_1_, ...), custom_call_target="tpu_custom_call" | custom-call | flops 1150000000 | bytes 768 | tf_op jit(solution)/shard_map/middle/pallas_call | solution.py:576
  111.0 1.3 halve.17
  112.6 6.2 %heads.2 = (bf16[416,1152]{1,0:T(8,128)(2,1)S(1)}, bf16[16,24,1920]{2,1,0:T(8,128)(2,1)S(1)}, bf16[16,24,1920]{2,1,0:T(8,128)(2,1)S(1)}, f32[8,128]{1,0:T(8,128)}) custom-call(s32[5]{0:T(128)S(1)} %stack.39.place.refs_0_, bf16[416,2304]{1,0:T(8,128)(2,1)S(1)} %copy-done.3, bf16[416,768]{1,0:T(8,128)(2,1)S(1)} %get-tuple-element.197.refs_2_, ...), custom_call_target="tpu_custom_call" | custom-call | flops 1150000000 | bytes 768 | tf_op jit(solution)/shard_map/heads/pallas_call | solution.py:576
  118.9 0.9 halve.18
  120.2 6.2 %heads.3 = (bf16[416,1152]{1,0:T(8,128)(2,1)S(1)}, bf16[16,24,1152]{2,1,0:T(8,128)(2,1)S(1)}, bf16[16,24,1152]{2,1,0:T(8,128)(2,1)S(1)}, f32[8,128]{1,0:T(8,128)}) custom-call(s32[5]{0:T(128)S(1)} %stack.39.place.refs_0_, bf16[416,2304]{1,0:T(8,128)(2,1)S(1)} %copy-done.3, bf16[416,768]{1,0:T(8,128)(2,1)S(1)} %get-tuple-element.197.refs_2_, ...), custom_call_target="tpu_custom_call" | custom-call | flops 2300000000 | bytes 768 | tf_op jit(solution)/shard_map/heads/pallas_call | solution.py:576
  126.4 0.9 halve.19
  127.4 1.9 %collective-permute-start.26 = (bf16[8,24,1920]{2,1,0:T(8,128)(2,1)S(1)}, bf16[8,24,1920]{2,1,0:T(8,128)(2,1)S(1)}, u32[]{:S(2)}, u32[]{:S(2)}) collective-permute-start(bf16[8,24,1920]{2,1,0:T(8,128)(2,1)S(1)} %get-tuple-element.226), channel_id=1, source_target_pairs={{0,2},{1,5},{2,0},{3,7},{4,6},{5,1},{6,4},{7,3},{8,10},{9,13},{10,... | collective-permute-start | bytes 2211848 | tf_op jit(solution)/shard_map/ppermute | solution.py:127
  130.7 1.2 collective-permute-start.31
  131.9 4.6 %inward.1 = (bf16[16,24,1280]{2,1,0:T(8,128)(2,1)S(1)}, bf16[16,24,1280]{2,1,0:T(8,128)(2,1)S(1)}, f32[394,768]{1,0:T(8,128)}, f32[8,128]{1,0:T(8,128)}) custom-call(s32[5]{0:T(128)S(1)} %stack.39.place.refs_0_, bf16[416,768]{1,0:T(8,128)(2,1)S(1)} %get-tuple-element.155.refs_1_, f32[416,768]{1,0:T(8,128)S(1)} %get-tuple-element.195.refs_2_, ...), custom_call_target="tpu_custom_call" | custom-call | flops 2300000000 | bytes 768 | tf_op jit(solution)/shard_map/inward/pallas_call | solution.py:576
  137.2 1.7 collective-permute-done.26.other_up.other_low
  141.2 1.6 collective-permute-start.28
  142.9 3.4 %collective-permute-start.33 = (bf16[2,96,768]{2,1,0:T(8,128)(2,1)S(1)}, bf16[2,96,768]{2,1,0:T(8,128)(2,1)S(1)}, u32[]{:S(2)}, u32[]{:S(2)}) collective-permute-start(bf16[2,96,768]{2,1,0:T(8,128)(2,1)S(1)} %get-tuple-element.250), channel_id=1, source_target_pairs={{0,16},{1,17},{2,18},{3,19},{4,20},{5,21},{6,22},{7,23},{8,24},{9,... | collective-permute-start | bytes 884744 | tf_op jit(solution)/shard_map/ppermute | solution.py:127
  146.3 6.7 %down.1 = (bf16[394,768]{1,0:T(8,128)(2,1)}, f32[8,128]{1,0:T(8,128)}) custom-call(s32[5]{0:T(128)S(1)} %stack.39.place.refs_0_, s32[394]{0:T(512)S(1)} %copy-done.10, bf16[416,3072]{1,0:T(8,128)(2,1)} %get-tuple-element.184.refs_2_, f32[416,768]{1,0:T(8,128)S(1)} %get-tuple-element.185.refs_2_.refs_3_, bf16[2,2,2,2,96,768]{5,4,3,2,1,0:T(8,128)(2,1)} %bitcast.22.refs_4_, ...), custom_call_target="tpu_custom_call" | custom-call | flops 575000000 | bytes 768 | tf_op jit(solution)/shard_map/down/pallas_call | solution.py:576
  153.6 1.0 collective-permute-start.34
  156.8 1.3 collective-permute-start.35
  158.2 3.4 %collective-permute-done.30.other_up.other_low = bf16[4,24,1280]{2,1,0:T(8,128)(2,1)S(1)} collective-permute-done((bf16[4,24,1280]{2,1,0:T(8,128)(2,1)S(1)}, bf16[4,24,1280]{2,1,0:T(8,128)(2,1)S(1)}, u32[]{:S(2)}, u32[]{:S(2)}) %collective-permute-start.30) | collective-permute-done | bytes 245792 | tf_op jit(solution)/shard_map/ppermute | solution.py:127
  162.9 1.9 %collective-permute-done.35.other_up.other_low = bf16[2,24,3072]{2,1,0:T(8,128)(2,1)S(1)} collective-permute-done((bf16[2,24,3072]{2,1,0:T(8,128)(2,1)S(1)}, bf16[2,24,3072]{2,1,0:T(8,128)(2,1)S(1)}, u32[]{:S(2)}, u32[]{:S(2)}) %collective-permute-start.35) | collective-permute-done | bytes 294944 | tf_op jit(solution)/shard_map/ppermute | solution.py:127
  165.4 1.3 collective-permute-done.34.other_up.other_low
  167.9 1.7 collective-permute-start.39
  169.6 2.9 %collective-permute-start.38 = (bf16[1,24,3072]{2,1,0:T(8,128)(2,1)S(1)}, bf16[1,24,3072]{2,1,0:T(8,128)(2,1)S(1)}, u32[]{:S(2)}, u32[]{:S(2)}) collective-permute-start(bf16[1,24,3072]{2,1,0:T(8,128)(2,1)S(1)} %get-tuple-element.264), channel_id=1, source_target_pairs={{0,16},{1,17},{2,18},{3,19},{4,20},{5,21},{6,22},{7,23},{8,24},{9,... | collective-permute-start | bytes 442376 | tf_op jit(solution)/shard_map/ppermute | solution.py:127
  173.9 5.7 %collective-permute-done.36 = bf16[1,24,1280]{2,1,0:T(8,128)(2,1)S(1)} collective-permute-done((bf16[1,24,1280]{2,1,0:T(8,128)(2,1)S(1)}, bf16[1,24,1280]{2,1,0:T(8,128)(2,1)S(1)}, u32[]{:S(2)}, u32[]{:S(2)}) %collective-permute-start.36) | collective-permute-done | bytes 61472 | tf_op jit(solution)/shard_map/ppermute | solution.py:127
  (133 shorter events, 29.0 us)
Async XLA Ops:
  0.6 5.9 %copy-start.13 = (bf16[24,3072]{1,0:T(8,128)(2,1)S(1)}, bf16[24,3072]{1,0:T(8,128)(2,1)}, u32[]{:S(2)}) copy-start(bf16[24,3072]{1,0:T(8,128)(2,1)} %refs_1_.5) | copy-start | bytes 442372
  2.5 10.1 %collective-permute-start.2 = (bf16[1,24,2432]{2,1,0:T(8,128)(2,1)}, bf16[1,24,2432]{2,1,0:T(8,128)(2,1)S(1)}, u32[]{:S(2)}, u32[]{:S(2)}) collective-permute-start(bf16[1,24,2432]{2,1,0:T(8,128)(2,1)} %get-tuple-element.144.held), channel_id=1, source_target_pairs={{0,16},{1,17},{2,18},{3,19},{4,20},{5,21},{6,22},{7,23},{8,24},{9,... | collective-permute-start | bytes 350216 | tf_op jit(solution)/shard_map/ppermute | solution.py:127
  6.5 14.5 %collective-permute-start.5 = (bf16[1,24,1536]{2,1,0:T(8,128)(2,1)S(1)}, bf16[1,24,1536]{2,1,0:T(8,128)(2,1)S(1)}, u32[]{:S(2)}, u32[]{:S(2)}) collective-permute-start(bf16[1,24,1536]{2,1,0:T(8,128)(2,1)S(1)} %get-tuple-element.150.held), channel_id=1, source_target_pairs={{0,2},{1,5},{2,0},{3,7},{4,6},{5,1},{6,4},{7,3},{8,10},{9,13},{10,... | collective-permute-start | bytes 221192 | tf_op jit(solution)/shard_map/ppermute | solution.py:127
  8.1 9.7 %collective-permute-start.1 = (bf16[1,96,768]{2,1,0:T(8,128)(2,1)S(1)}, bf16[1,96,768]{2,1,0:T(8,128)(2,1)S(1)}, u32[]{:S(2)}, u32[]{:S(2)}) collective-permute-start(bf16[1,96,768]{2,1,0:T(8,128)(2,1)S(1)} %bitcast.64), channel_id=1, source_target_pairs={{0,8},{1,9},{2,10},{3,11},{4,12},{5,13},{6,14},{7,15},{8,0},{9,1},... | collective-permute-start | bytes 442376 | tf_op jit(solution)/shard_map/ppermute | solution.py:127
  9.7 8.7 %collective-permute-start = (bf16[1,24,2304]{2,1,0:T(8,128)(2,1)S(1)}, bf16[1,24,2304]{2,1,0:T(8,128)(2,1)S(1)}, u32[]{:S(2)}, u32[]{:S(2)}) collective-permute-start(bf16[1,24,2304]{2,1,0:T(8,128)(2,1)S(1)} %get-tuple-element.143.held), channel_id=1, source_target_pairs={{0,16},{1,17},{2,18},{3,19},{4,20},{5,21},{6,22},{7,23},{8,24},{9,... | collective-permute-start | bytes 331784 | tf_op jit(solution)/shard_map/ppermute | solution.py:127
  13.2 8.7 %collective-permute-start.4 = (bf16[2,24,2432]{2,1,0:T(8,128)(2,1)S(1)}, bf16[2,24,2432]{2,1,0:T(8,128)(2,1)S(1)}, u32[]{:S(2)}, u32[]{:S(2)}) collective-permute-start(bf16[2,24,2432]{2,1,0:T(8,128)(2,1)S(1)} %bitcast.60), channel_id=1, source_target_pairs={{0,8},{1,9},{2,10},{3,11},{4,12},{5,13},{6,14},{7,15},{8,0},{9,1},... | collective-permute-start | bytes 700424 | tf_op jit(solution)/shard_map/ppermute | solution.py:127
  18.9 6.9 %collective-permute-start.3 = (bf16[2,24,2304]{2,1,0:T(8,128)(2,1)S(1)}, bf16[2,24,2304]{2,1,0:T(8,128)(2,1)S(1)}, u32[]{:S(2)}, u32[]{:S(2)}) collective-permute-start(bf16[2,24,2304]{2,1,0:T(8,128)(2,1)S(1)} %bitcast.62), channel_id=1, source_target_pairs={{0,2},{1,5},{2,0},{3,7},{4,6},{5,1},{6,4},{7,3},{8,10},{9,13},{10,... | collective-permute-start | bytes 663560 | tf_op jit(solution)/shard_map/ppermute | solution.py:127
  20.1 9.7 %collective-permute-start.7 = (bf16[2,96,768]{2,1,0:T(8,128)(2,1)S(1)}, bf16[2,96,768]{2,1,0:T(8,128)(2,1)S(1)}, u32[]{:S(2)}, u32[]{:S(2)}) collective-permute-start(bf16[2,96,768]{2,1,0:T(8,128)(2,1)S(1)} %bitcast.56), channel_id=1, source_target_pairs={{0,2},{1,5},{2,0},{3,7},{4,6},{5,1},{6,4},{7,3},{8,10},{9,13},{10,... | collective-permute-start | bytes 884744 | tf_op jit(solution)/shard_map/ppermute | solution.py:127
  21.8 7.1 %copy-start.9 = (s32[394]{0:T(512)S(1)}, s32[394]{0:T(512)}, u32[]{:S(2)}) copy-start(s32[394]{0:T(512)} %refs_1_.7) | copy-start | bytes 4732
  21.8 7.1 %copy-start.11 = (bf16[394,768]{1,0:T(8,128)(2,1)S(1)}, bf16[394,768]{1,0:T(8,128)(2,1)}, u32[]{:S(2)}) copy-start(bf16[394,768]{1,0:T(8,128)(2,1)} %refs_1_.6) | copy-start | bytes 1815556
  21.8 7.1 %copy-start.12 = (bf16[394,768]{1,0:T(8,128)(2,1)S(1)}, bf16[394,768]{1,0:T(8,128)(2,1)}, u32[]{:S(2)}) copy-start(bf16[394,768]{1,0:T(8,128)(2,1)} %refs_2_.3) | copy-start | bytes 1815556
  22.4 10.6 %collective-permute-start.6 = (bf16[4,24,2432]{2,1,0:T(8,128)(2,1)S(1)}, bf16[4,24,2432]{2,1,0:T(8,128)(2,1)S(1)}, u32[]{:S(2)}, u32[]{:S(2)}) collective-permute-start(bf16[4,24,2432]{2,1,0:T(8,128)(2,1)S(1)} %bitcast.52), channel_id=1, source_target_pairs={{0,2},{1,5},{2,0},{3,7},{4,6},{5,1},{6,4},{7,3},{8,10},{9,13},{10,... | collective-permute-start | bytes 1400840 | tf_op jit(solution)/shard_map/ppermute | solution.py:127
  24.0 10.2 %collective-permute-start.10 = (bf16[2,24,1536]{2,1,0:T(8,128)(2,1)S(1)}, bf16[2,24,1536]{2,1,0:T(8,128)(2,1)S(1)}, u32[]{:S(2)}, u32[]{:S(2)}) collective-permute-start(bf16[2,24,1536]{2,1,0:T(8,128)(2,1)S(1)} %bitcast.66), channel_id=1, source_target_pairs={{0,16},{1,17},{2,18},{3,19},{4,20},{5,21},{6,22},{7,23},{8,24},{9,... | collective-permute-start | bytes 442376 | tf_op jit(solution)/shard_map/ppermute | solution.py:127
  26.4 21.5 %collective-permute-start.9 = (bf16[4,24,2304]{2,1,0:T(8,128)(2,1)S(1)}, bf16[4,24,2304]{2,1,0:T(8,128)(2,1)S(1)}, u32[]{:S(2)}, u32[]{:S(2)}) collective-permute-start(bf16[4,24,2304]{2,1,0:T(8,128)(2,1)S(1)} %bitcast.54), channel_id=1, source_target_pairs={{0,8},{1,9},{2,10},{3,11},{4,12},{5,13},{6,14},{7,15},{8,0},{9,1},... | collective-permute-start | bytes 1327112 | tf_op jit(solution)/shard_map/ppermute | solution.py:127
  30.4 27.8 %collective-permute-start.12 = (bf16[4,96,768]{2,1,0:T(8,128)(2,1)S(1)}, bf16[4,96,768]{2,1,0:T(8,128)(2,1)S(1)}, u32[]{:S(2)}, u32[]{:S(2)}) collective-permute-start(bf16[4,96,768]{2,1,0:T(8,128)(2,1)S(1)} %bitcast.48), channel_id=1, source_target_pairs={{0,16},{1,17},{2,18},{3,19},{4,20},{5,21},{6,22},{7,23},{8,24},{9,... | collective-permute-start | bytes 1769480 | tf_op jit(solution)/shard_map/ppermute | solution.py:127
  33.7 15.0 %collective-permute-start.8 = (bf16[8,24,2432]{2,1,0:T(8,128)(2,1)S(1)}, bf16[8,24,2432]{2,1,0:T(8,128)(2,1)S(1)}, u32[]{:S(2)}, u32[]{:S(2)}) collective-permute-start(bf16[8,24,2432]{2,1,0:T(8,128)(2,1)S(1)} %bitcast.46), channel_id=1, source_target_pairs={{0,4},{1,3},{2,6},{3,1},{4,0},{5,7},{6,2},{7,5},{8,12},{9,11},{10,... | collective-permute-start | bytes 2801672 | tf_op jit(solution)/shard_map/ppermute | solution.py:127
  34.8 15.7 %collective-permute-start.13 = (bf16[4,24,1536]{2,1,0:T(8,128)(2,1)S(1)}, bf16[4,24,1536]{2,1,0:T(8,128)(2,1)S(1)}, u32[]{:S(2)}, u32[]{:S(2)}) collective-permute-start(bf16[4,24,1536]{2,1,0:T(8,128)(2,1)S(1)} %bitcast.58), channel_id=1, source_target_pairs={{0,4},{1,3},{2,6},{3,1},{4,0},{5,7},{6,2},{7,5},{8,12},{9,11},{10,... | collective-permute-start | bytes 884744 | tf_op jit(solution)/shard_map/ppermute | solution.py:127
  48.5 18.1 %collective-permute-start.14 = (bf16[8,24,2304]{2,1,0:T(8,128)(2,1)S(1)}, bf16[8,24,2304]{2,1,0:T(8,128)(2,1)S(1)}, u32[]{:S(2)}, u32[]{:S(2)}) collective-permute-start(bf16[8,24,2304]{2,1,0:T(8,128)(2,1)S(1)} %bitcast.40), channel_id=1, source_target_pairs={{0,4},{1,3},{2,6},{3,1},{4,0},{5,7},{6,2},{7,5},{8,12},{9,11},{10,... | collective-permute-start | bytes 2654216 | tf_op jit(solution)/shard_map/ppermute | solution.py:127
  49.4 10.4 %collective-permute-start.11 = (bf16[16,24,2432]{2,1,0:T(8,128)(2,1)S(1)}, bf16[16,24,2432]{2,1,0:T(8,128)(2,1)S(1)}, u32[]{:S(2)}, u32[]{:S(2)}) collective-permute-start(bf16[16,24,2432]{2,1,0:T(8,128)(2,1)S(1)} %bitcast.37), channel_id=1, source_target_pairs={{0,1},{1,0},{2,3},{3,2},{4,5},{5,4},{6,7},{7,6},{8,9},{9,8},{10,11... | collective-permute-start | bytes 5603336 | tf_op jit(solution)/shard_map/ppermute | solution.py:127
  51.1 19.6 %collective-permute-start.16 = (bf16[8,24,1536]{2,1,0:T(8,128)(2,1)S(1)}, bf16[8,24,1536]{2,1,0:T(8,128)(2,1)S(1)}, u32[]{:S(2)}, u32[]{:S(2)}) collective-permute-start(bf16[8,24,1536]{2,1,0:T(8,128)(2,1)S(1)} %bitcast.50), channel_id=1, source_target_pairs={{0,8},{1,9},{2,10},{3,11},{4,12},{5,13},{6,14},{7,15},{8,0},{9,1},... | collective-permute-start | bytes 1769480 | tf_op jit(solution)/shard_map/ppermute | solution.py:127
  58.8 16.3 %collective-permute-start.18 = (bf16[8,96,768]{2,1,0:T(8,128)(2,1)S(1)}, bf16[8,96,768]{2,1,0:T(8,128)(2,1)S(1)}, u32[]{:S(2)}, u32[]{:S(2)}) collective-permute-start(bf16[8,96,768]{2,1,0:T(8,128)(2,1)S(1)} %bitcast.44), channel_id=1, source_target_pairs={{0,4},{1,3},{2,6},{3,1},{4,0},{5,7},{6,2},{7,5},{8,12},{9,11},{10,... | collective-permute-start | bytes 3538952 | tf_op jit(solution)/shard_map/ppermute | solution.py:127
  59.8 6.7 %copy-start = (bf16[16,24,2432]{2,1,0:T(8,128)(2,1)}, bf16[16,24,2432]{2,1,0:T(8,128)(2,1)S(1)}, u32[]{:S(2)}) copy-start(bf16[16,24,2432]{2,1,0:T(8,128)(2,1)S(1)} %collective-permute-done.11.refs_3_.refs_8_) | copy-start | bytes 5603332
  66.6 5.8 %copy-start.2 = (bf16[416,2304]{1,0:T(8,128)(2,1)}, bf16[416,2304]{1,0:T(8,128)(2,1)S(1)}, u32[]{:S(2)}) copy-start(bf16[416,2304]{1,0:T(8,128)(2,1)S(1)} %get-tuple-element.196.refs_1_) | copy-start | bytes 5750788
  66.6 5.8 %copy-start.4 = (bf16[416,768]{1,0:T(8,128)(2,1)}, bf16[416,768]{1,0:T(8,128)(2,1)S(1)}, u32[]{:S(2)}) copy-start(bf16[416,768]{1,0:T(8,128)(2,1)S(1)} %get-tuple-element.199.refs_4_) | copy-start | bytes 1916932
  68.9 8.8 %collective-permute-start.15 = (bf16[16,24,2304]{2,1,0:T(8,128)(2,1)}, bf16[16,24,2304]{2,1,0:T(8,128)(2,1)}, u32[]{:S(2)}, u32[]{:S(2)}) collective-permute-start(bf16[16,24,2304]{2,1,0:T(8,128)(2,1)} %bitcast.17.refs_4_.refs_5_), channel_id=1, source_target_pairs={{0,1},{1,0},{2,3},{3,2},{4,5},{5,4},{6,7},{7,6},{8,9},{9,8},{10,11... | collective-permute-start | bytes 5308424 | tf_op jit(solution)/shard_map/ppermute | solution.py:127
  72.4 5.3 %collective-permute-start.17 = (bf16[16,24,1536]{2,1,0:T(8,128)(2,1)}, bf16[16,24,1536]{2,1,0:T(8,128)(2,1)}, u32[]{:S(2)}, u32[]{:S(2)}) collective-permute-start(bf16[16,24,1536]{2,1,0:T(8,128)(2,1)} %bitcast.19.refs_6_.refs_7_), channel_id=1, source_target_pairs={{0,1},{1,0},{2,3},{3,2},{4,5},{5,4},{6,7},{7,6},{8,9},{9,8},{10,11... | collective-permute-start | bytes 3538952 | tf_op jit(solution)/shard_map/ppermute | solution.py:127
  77.3 14.0 %collective-permute-start.19 = (bf16[16,96,768]{2,1,0:T(8,128)(2,1)}, bf16[16,96,768]{2,1,0:T(8,128)(2,1)}, u32[]{:S(2)}, u32[]{:S(2)}) collective-permute-start(bf16[16,96,768]{2,1,0:T(8,128)(2,1)} %bitcast.23), channel_id=1, source_target_pairs={{0,1},{1,0},{2,3},{3,2},{4,5},{5,4},{6,7},{7,6},{8,9},{9,8},{10,11... | collective-permute-start | bytes 7077896 | tf_op jit(solution)/shard_map/ppermute | solution.py:127
  90.8 8.9 %collective-permute-start.20 = (bf16[2,2,2,2,96,768]{5,4,3,2,1,0:T(8,128)(2,1)S(1)}, bf16[2,2,2,2,96,768]{5,4,3,2,1,0:T(8,128)(2,1)S(1)}, u32[]{:S(2)}, u32[]{:S(2)}) collective-permute-start(bf16[2,2,2,2,96,768]{5,4,3,2,1,0:T(8,128)(2,1)S(1)} %get-tuple-element.192), channel_id=1, source_target_pairs={{0,1},{1,0},{2,3},{3,2},{4,5},{5,4},{6,7},{7,6},{8,9},{9,8},{10,11... | collective-permute-start | bytes 7077896 | tf_op jit(solution)/shard_map/ppermute | solution.py:127
  99.6 11.3 %collective-permute-start.21 = (bf16[16,24,3072]{2,1,0:T(8,128)(2,1)S(1)}, bf16[16,24,3072]{2,1,0:T(8,128)(2,1)S(1)}, u32[]{:S(2)}, u32[]{:S(2)}) collective-permute-start(bf16[16,24,3072]{2,1,0:T(8,128)(2,1)S(1)} %get-tuple-element.203), channel_id=1, source_target_pairs={{0,1},{1,0},{2,3},{3,2},{4,5},{5,4},{6,7},{7,6},{8,9},{9,8},{10,11... | collective-permute-start | bytes 7077896 | tf_op jit(solution)/shard_map/ppermute | solution.py:127
  100.9 18.0 %collective-permute-start.22 = (bf16[8,96,768]{2,1,0:T(8,128)(2,1)S(1)}, bf16[8,96,768]{2,1,0:T(8,128)(2,1)S(1)}, u32[]{:S(2)}, u32[]{:S(2)}) collective-permute-start(bf16[8,96,768]{2,1,0:T(8,128)(2,1)S(1)} %get-tuple-element.208), channel_id=1, source_target_pairs={{0,2},{1,5},{2,0},{3,7},{4,6},{5,1},{6,4},{7,3},{8,10},{9,13},{10,... | collective-permute-start | bytes 3538952 | tf_op jit(solution)/shard_map/ppermute | solution.py:127
  112.3 17.5 %collective-permute-start.23 = (bf16[8,24,3072]{2,1,0:T(8,128)(2,1)S(1)}, bf16[8,24,3072]{2,1,0:T(8,128)(2,1)S(1)}, u32[]{:S(2)}, u32[]{:S(2)}) collective-permute-start(bf16[8,24,3072]{2,1,0:T(8,128)(2,1)S(1)} %get-tuple-element.217), channel_id=1, source_target_pairs={{0,2},{1,5},{2,0},{3,7},{4,6},{5,1},{6,4},{7,3},{8,10},{9,13},{10,... | collective-permute-start | bytes 3538952 | tf_op jit(solution)/shard_map/ppermute | solution.py:127
  118.8 7.6 %collective-permute-start.24 = (bf16[16,24,1920]{2,1,0:T(8,128)(2,1)S(1)}, bf16[16,24,1920]{2,1,0:T(8,128)(2,1)S(1)}, u32[]{:S(2)}, u32[]{:S(2)}) collective-permute-start(bf16[16,24,1920]{2,1,0:T(8,128)(2,1)S(1)} %get-tuple-element.219), channel_id=1, source_target_pairs={{0,1},{1,0},{2,3},{3,2},{4,5},{5,4},{6,7},{7,6},{8,9},{9,8},{10,11... | collective-permute-start | bytes 4423688 | tf_op jit(solution)/shard_map/ppermute | solution.py:127
  119.8 16.7 %collective-permute-start.27 = (bf16[4,96,768]{2,1,0:T(8,128)(2,1)S(1)}, bf16[4,96,768]{2,1,0:T(8,128)(2,1)S(1)}, u32[]{:S(2)}, u32[]{:S(2)}) collective-permute-start(bf16[4,96,768]{2,1,0:T(8,128)(2,1)S(1)} %get-tuple-element.228), channel_id=1, source_target_pairs={{0,8},{1,9},{2,10},{3,11},{4,12},{5,13},{6,14},{7,15},{8,0},{9,1},... | collective-permute-start | bytes 1769480 | tf_op jit(solution)/shard_map/ppermute | solution.py:127
  127.4 11.5 %collective-permute-start.26 = (bf16[8,24,1920]{2,1,0:T(8,128)(2,1)S(1)}, bf16[8,24,1920]{2,1,0:T(8,128)(2,1)S(1)}, u32[]{:S(2)}, u32[]{:S(2)}) collective-permute-start(bf16[8,24,1920]{2,1,0:T(8,128)(2,1)S(1)} %get-tuple-element.226), channel_id=1, source_target_pairs={{0,2},{1,5},{2,0},{3,7},{4,6},{5,1},{6,4},{7,3},{8,10},{9,13},{10,... | collective-permute-start | bytes 2211848 | tf_op jit(solution)/shard_map/ppermute | solution.py:127
  130.7 25.4 %collective-permute-start.31 = (bf16[4,24,3072]{2,1,0:T(8,128)(2,1)S(1)}, bf16[4,24,3072]{2,1,0:T(8,128)(2,1)S(1)}, u32[]{:S(2)}, u32[]{:S(2)}) collective-permute-start(bf16[4,24,3072]{2,1,0:T(8,128)(2,1)S(1)} %get-tuple-element.244), channel_id=1, source_target_pairs={{0,8},{1,9},{2,10},{3,11},{4,12},{5,13},{6,14},{7,15},{8,0},{9,1},... | collective-permute-start | bytes 1769480 | tf_op jit(solution)/shard_map/ppermute | solution.py:127
  136.5 3.9 %collective-permute-start.25 = (bf16[16,24,1280]{2,1,0:T(8,128)(2,1)S(1)}, bf16[16,24,1280]{2,1,0:T(8,128)(2,1)S(1)}, u32[]{:S(2)}, u32[]{:S(2)}) collective-permute-start(bf16[16,24,1280]{2,1,0:T(8,128)(2,1)S(1)} %get-tuple-element.224), channel_id=1, source_target_pairs={{0,1},{1,0},{2,3},{3,2},{4,5},{5,4},{6,7},{7,6},{8,9},{9,8},{10,11... | collective-permute-start | bytes 2949128 | tf_op jit(solution)/shard_map/ppermute | solution.py:127
  139.7 13.3 %collective-permute-start.29 = (bf16[4,24,1920]{2,1,0:T(8,128)(2,1)S(1)}, bf16[4,24,1920]{2,1,0:T(8,128)(2,1)S(1)}, u32[]{:S(2)}, u32[]{:S(2)}) collective-permute-start(bf16[4,24,1920]{2,1,0:T(8,128)(2,1)S(1)} %get-tuple-element.238), channel_id=1, source_target_pairs={{0,4},{1,3},{2,6},{3,1},{4,0},{5,7},{6,2},{7,5},{8,12},{9,11},{10,... | collective-permute-start | bytes 1105928 | tf_op jit(solution)/shard_map/ppermute | solution.py:127
  140.4 5.9 %copy-start.10 = (s32[394]{0:T(512)S(1)}, s32[394]{0:T(512)}, u32[]{:S(2)}) copy-start(s32[394]{0:T(512)} %refs_1_.7) | copy-start | bytes 4732
  141.2 13.4 %collective-permute-start.28 = (bf16[8,24,1280]{2,1,0:T(8,128)(2,1)S(1)}, bf16[8,24,1280]{2,1,0:T(8,128)(2,1)S(1)}, u32[]{:S(2)}, u32[]{:S(2)}) collective-permute-start(bf16[8,24,1280]{2,1,0:T(8,128)(2,1)S(1)} %get-tuple-element.236), channel_id=1, source_target_pairs={{0,2},{1,5},{2,0},{3,7},{4,6},{5,1},{6,4},{7,3},{8,10},{9,13},{10,... | collective-permute-start | bytes 1474568 | tf_op jit(solution)/shard_map/ppermute | solution.py:127
  142.9 24.4 %collective-permute-start.33 = (bf16[2,96,768]{2,1,0:T(8,128)(2,1)S(1)}, bf16[2,96,768]{2,1,0:T(8,128)(2,1)S(1)}, u32[]{:S(2)}, u32[]{:S(2)}) collective-permute-start(bf16[2,96,768]{2,1,0:T(8,128)(2,1)S(1)} %get-tuple-element.250), channel_id=1, source_target_pairs={{0,16},{1,17},{2,18},{3,19},{4,20},{5,21},{6,22},{7,23},{8,24},{9,... | collective-permute-start | bytes 884744 | tf_op jit(solution)/shard_map/ppermute | solution.py:127
  153.6 13.0 %collective-permute-start.34 = (bf16[2,24,1920]{2,1,0:T(8,128)(2,1)S(1)}, bf16[2,24,1920]{2,1,0:T(8,128)(2,1)S(1)}, u32[]{:S(2)}, u32[]{:S(2)}) collective-permute-start(bf16[2,24,1920]{2,1,0:T(8,128)(2,1)S(1)} %get-tuple-element.252), channel_id=1, source_target_pairs={{0,16},{1,17},{2,18},{3,19},{4,20},{5,21},{6,22},{7,23},{8,24},{9,... | collective-permute-start | bytes 552968 | tf_op jit(solution)/shard_map/ppermute | solution.py:127
  155.3 6.3 %collective-permute-start.30 = (bf16[4,24,1280]{2,1,0:T(8,128)(2,1)S(1)}, bf16[4,24,1280]{2,1,0:T(8,128)(2,1)S(1)}, u32[]{:S(2)}, u32[]{:S(2)}) collective-permute-start(bf16[4,24,1280]{2,1,0:T(8,128)(2,1)S(1)} %get-tuple-element.242), channel_id=1, source_target_pairs={{0,4},{1,3},{2,6},{3,1},{4,0},{5,7},{6,2},{7,5},{8,12},{9,11},{10,... | collective-permute-start | bytes 737288 | tf_op jit(solution)/shard_map/ppermute | solution.py:127
  156.8 7.9 %collective-permute-start.35 = (bf16[2,24,3072]{2,1,0:T(8,128)(2,1)S(1)}, bf16[2,24,3072]{2,1,0:T(8,128)(2,1)S(1)}, u32[]{:S(2)}, u32[]{:S(2)}) collective-permute-start(bf16[2,24,3072]{2,1,0:T(8,128)(2,1)S(1)} %get-tuple-element.254), channel_id=1, source_target_pairs={{0,4},{1,3},{2,6},{3,1},{4,0},{5,7},{6,2},{7,5},{8,12},{9,11},{10,... | collective-permute-start | bytes 884744 | tf_op jit(solution)/shard_map/ppermute | solution.py:127
  162.2 10.3 %collective-permute-start.32 = (bf16[2,24,1280]{2,1,0:T(8,128)(2,1)S(1)}, bf16[2,24,1280]{2,1,0:T(8,128)(2,1)S(1)}, u32[]{:S(2)}, u32[]{:S(2)}) collective-permute-start(bf16[2,24,1280]{2,1,0:T(8,128)(2,1)S(1)} %get-tuple-element.248), channel_id=1, source_target_pairs={{0,8},{1,9},{2,10},{3,11},{4,12},{5,13},{6,14},{7,15},{8,0},{9,1},... | collective-permute-start | bytes 368648 | tf_op jit(solution)/shard_map/ppermute | solution.py:127
  167.2 6.0 %collective-permute-start.37 = (bf16[1,24,1920]{2,1,0:T(8,128)(2,1)S(1)}, bf16[1,24,1920]{2,1,0:T(8,128)(2,1)S(1)}, u32[]{:S(2)}, u32[]{:S(2)}) collective-permute-start(bf16[1,24,1920]{2,1,0:T(8,128)(2,1)S(1)} %get-tuple-element.262), channel_id=1, source_target_pairs={{0,8},{1,9},{2,10},{3,11},{4,12},{5,13},{6,14},{7,15},{8,0},{9,1},... | collective-permute-start | bytes 276488 | tf_op jit(solution)/shard_map/ppermute | solution.py:127
  167.9 13.3 %collective-permute-start.39 = (bf16[1,96,768]{2,1,0:T(8,128)(2,1)S(1)}, bf16[1,96,768]{2,1,0:T(8,128)(2,1)S(1)}, u32[]{:S(2)}, u32[]{:S(2)}) collective-permute-start(bf16[1,96,768]{2,1,0:T(8,128)(2,1)S(1)} %get-tuple-element.266), channel_id=1, source_target_pairs={{0,4},{1,3},{2,6},{3,1},{4,0},{5,7},{6,2},{7,5},{8,12},{9,11},{10,... | collective-permute-start | bytes 442376 | tf_op jit(solution)/shard_map/ppermute | solution.py:127
  169.6 12.4 %collective-permute-start.38 = (bf16[1,24,3072]{2,1,0:T(8,128)(2,1)S(1)}, bf16[1,24,3072]{2,1,0:T(8,128)(2,1)S(1)}, u32[]{:S(2)}, u32[]{:S(2)}) collective-permute-start(bf16[1,24,3072]{2,1,0:T(8,128)(2,1)S(1)} %get-tuple-element.264), channel_id=1, source_target_pairs={{0,16},{1,17},{2,18},{3,19},{4,20},{5,21},{6,22},{7,23},{8,24},{9,... | collective-permute-start | bytes 442376 | tf_op jit(solution)/shard_map/ppermute | solution.py:127
  173.1 6.5 %collective-permute-start.36 = (bf16[1,24,1280]{2,1,0:T(8,128)(2,1)S(1)}, bf16[1,24,1280]{2,1,0:T(8,128)(2,1)S(1)}, u32[]{:S(2)}, u32[]{:S(2)}) collective-permute-start(bf16[1,24,1280]{2,1,0:T(8,128)(2,1)S(1)} %get-tuple-element.260), channel_id=1, source_target_pairs={{0,16},{1,17},{2,18},{3,19},{4,20},{5,21},{6,22},{7,23},{8,24},{9,... | collective-permute-start | bytes 184328 | tf_op jit(solution)/shard_map/ppermute | solution.py:127
  (10 other events, 26.1 us)
